TPU v7x, 32 devices: a whole 2x2x4 slice. The times are simulated.
32 devices in a mesh: dp: 2 (over y), fsdp: 16 (over z, x, core).
Axes of the slice: x: 2, y: 2, z: 4, core: 2. Of those that a mesh axis runs over, the one named last changes fastest.
Arguments:
- tokens: bfloat16 [32768, 1024], P(('dp', 'fsdp')), may hold values from -12 to 12
- ln_gain: bfloat16 [1024], P(('dp', 'fsdp')), may hold values from 0.099609375 to 1.8984375
- ln_bias: bfloat16 [1024], P(('dp', 'fsdp')), may hold values from -1.75 to 1.75
- qkv_weight: bfloat16 [1024, 3072], P(('dp', 'fsdp')), may hold values from -0.1875 to 0.1875
- qkv_bias: bfloat16 [3072], P(('dp', 'fsdp')), may hold values from -1.75 to 1.75
- out_weight: bfloat16 [1024, 1024], P(('dp', 'fsdp')), may hold values from -0.75 to 0.75
- out_bias: bfloat16 [1024], P(('dp', 'fsdp')), may hold values from -1.75 to 1.75
- fc1_weight: bfloat16 [1024, 4096], P(('dp', 'fsdp')), may hold values from -0.1875 to 0.1875
- fc1_bias: bfloat16 [4096], P(('dp', 'fsdp')), may hold values from -3 to 3
- fc2_weight: bfloat16 [4096, 1024], P(('dp', 'fsdp')), may hold values from -0.09375 to 0.09375
- fc2_bias: bfloat16 [1024], P(('dp', 'fsdp')), may hold values from -1.75 to 1.75
- cotangent: float32 [32768, 1024], P(('dp', 'fsdp')), may hold values from -6 to 6
- doc_lengths: int32 [32, 4], P(('dp', 'fsdp')), may hold values from 1 to 512, 1024 in all within a row
- node_seeds: int32 [64, 64], replicated, may hold values from 0 to 1023
- node_weights: int32 [64], replicated, may hold values from 1 to 16
Outputs:
- output: float32 [32768, 1024], P(('dp', 'fsdp'))
- input_grad: float32 [32768, 1024], P(('dp', 'fsdp'))
- g_ln_gain: float32 [1024], P(('dp', 'fsdp'))
- g_ln_bias: float32 [1024], P(('dp', 'fsdp'))
- g_qkv_weight: float32 [1024, 3072], P(('dp', 'fsdp'))
- g_qkv_bias: float32 [3072], P(('dp', 'fsdp'))
- g_out_weight: float32 [1024, 1024], P(('dp', 'fsdp'))
- g_out_bias: float32 [1024], P(('dp', 'fsdp'))
- g_fc1_weight: float32 [1024, 4096], P(('dp', 'fsdp'))
- g_fc1_bias: float32 [4096], P(('dp', 'fsdp'))
- g_fc2_weight: float32 [4096, 1024], P(('dp', 'fsdp'))
- g_fc2_bias: float32 [1024], P(('dp', 'fsdp'))
Inputs may be any that keep to these rules, and one draw needn't show every extreme that they name: `doc_lengths`: each row holds the lengths of 4 documents that fill one sequence of 1024 tokens; its longest document has exactly 512 tokens.
All inputs are finite; a program needn't handle non-finite values.
Results may differ from a plain program's by a relative error of at most 0.0093.
Values may be sent and summed in bfloat16 or wider, within the bound.
No kernel may reach another device: no remote copies, remote signals or barrier semaphores. Data moves between devices by JAX's collectives and lax.ppermute only.
A program may use at most 256 MiB of HBM per device.

v0:
```python
import math

import jax
import jax.numpy as jnp
from jax import lax
from jax.sharding import PartitionSpec as P

D = 1024
HEADS = 16
HD = 64
ROT = 16
LEN = 1024
DOCS = 4


feature_scale = 0.2
epsilon = 1e-05
precise = lax.Precision.HIGHEST


def tables(node_seeds, node_weights):
    width = node_seeds.shape[1]
    uniform_pts = (node_seeds.astype(jnp.float32) + 0.5) / 1024.0
    nodes = math.sqrt(2.0) * lax.erf_inv(2.0 * uniform_pts - 1.0)
    order = jnp.arange(width).astype(jnp.float32)
    scales = jnp.where(order[:, None] == 0.0, math.sqrt(1.0 / width), math.sqrt(2.0 / width))
    basis = scales * jnp.cos(
        math.pi * (2.0 * order[None, :] + 1.0) * order[:, None] / (2.0 * width)
    )
    projection = jnp.dot(nodes, basis, precision=precise)
    weights_float = node_weights.astype(jnp.float32)
    return (projection, weights_float / jnp.sum(weights_float))


def layout(lengths):
    ends = jnp.cumsum(lengths)
    starts = ends - lengths
    places = jnp.arange(LEN, dtype=jnp.int32)
    doc_ids = jnp.sum((places[:, None] >= ends[None, :]).astype(jnp.int32), axis=1)
    owners = doc_ids[:, None] == jnp.arange(DOCS, dtype=jnp.int32)[None, :]
    begins = jnp.sum(jnp.where(owners, starts[None, :], 0), axis=1)
    return (doc_ids, (places - begins).astype(jnp.float32))


def rotary(positions):
    half_rot = ROT // 2
    freqs = 10000.0 ** (-2.0 * jnp.arange(half_rot).astype(jnp.float32) / ROT)
    angles = positions[:, None] * freqs[None, :]
    return (jnp.cos(angles), jnp.sin(angles))


def rotate(heads, cos_table, sin_table):
    half_rot = cos_table.shape[1]
    first = heads[..., :half_rot]
    second = heads[..., half_rot : 2 * half_rot]
    rest = heads[..., 2 * half_rot :]
    cos_wide = cos_table[:, None, :]
    sin_wide = sin_table[:, None, :]
    return jnp.concatenate(
        [first * cos_wide - second * sin_wide, second * cos_wide + first * sin_wide, rest], axis=-1
    )


def features(heads, cos_table, sin_table, projection):
    turned = feature_scale * rotate(heads, cos_table, sin_table)
    exponent = jnp.einsum("lhd,md->lhm", turned, projection, precision=precise)
    exponent = exponent - 0.5 * jnp.sum(turned * turned, axis=-1, keepdims=True)
    return jnp.exp(exponent)


def plain_dot(left, right):
    return jnp.dot(left, right, preferred_element_type=jnp.float32)


def outer_sum(left, right):
    return lax.dot_general(
        left, right, (((0,), (0,)), ((), ())), preferred_element_type=jnp.float32
    )


def back_proj(left, right):
    return lax.dot_general(
        left, right, (((1,), (1,)), ((), ())), preferred_element_type=jnp.float32
    )


def gelu_slope(upper):
    return 0.5 * (1.0 + lax.erf(upper / math.sqrt(2.0))) + upper * jnp.exp(
        -0.5 * upper * upper
    ) / math.sqrt(2.0 * math.pi)


def block_mask(doc_ids, first, block):
    places = jnp.arange(doc_ids.shape[0], dtype=jnp.int32)
    rows_here = places[first : first + block]
    same_doc = doc_ids[first : first + block, None] == doc_ids[None, :]
    return same_doc & (rows_here[:, None] >= places[None, :])


def attend(fq_low, fk_low, values_low, doc_ids):
    seq_len = doc_ids.shape[0]
    block = min(512, seq_len)
    outputs = []
    denoms = []
    for first in range(0, seq_len, block):
        mask = block_mask(doc_ids, first, block)
        raw = jnp.einsum(
            "qhm,khm->hqk",
            fq_low[first : first + block],
            fk_low,
            preferred_element_type=jnp.float32,
        )
        scores = jnp.where(mask[None], raw, 0.0)
        denom = jnp.sum(scores, axis=-1)
        numer = jnp.einsum(
            "hqk,khd->qhd",
            scores.astype(jnp.bfloat16),
            values_low,
            preferred_element_type=jnp.float32,
        )
        outputs.append(numer / denom.T[:, :, None])
        denoms.append(denom)
    return (jnp.concatenate(outputs, axis=0), jnp.concatenate(denoms, axis=1))


def attend_back(fq_low, fk_low, values_low, doc_ids, grad_out, attn_out, denom):
    seq_len = doc_ids.shape[0]
    block = min(512, seq_len)
    d_values = jnp.zeros(values_low.shape, jnp.float32)
    d_fk = jnp.zeros(fk_low.shape, jnp.float32)
    d_fq_parts = []
    for first in range(0, seq_len, block):
        mask = block_mask(doc_ids, first, block)
        fq_block = fq_low[first : first + block]
        raw = jnp.einsum("qhm,khm->hqk", fq_block, fk_low, preferred_element_type=jnp.float32)
        scores_low = jnp.where(mask[None], raw, 0.0).astype(jnp.bfloat16)
        den_block = denom[:, first : first + block].T
        grad_block = grad_out[first : first + block]
        d_num_low = (grad_block / den_block[:, :, None]).astype(jnp.bfloat16)
        d_denom = -jnp.sum(grad_block * attn_out[first : first + block], axis=-1) / den_block
        d_prod = jnp.einsum(
            "qhd,khd->hqk", d_num_low, values_low, preferred_element_type=jnp.float32
        )
        d_scores_low = jnp.where(
            mask[None],
            (d_prod + d_denom.T[:, :, None]).astype(jnp.bfloat16),
            jnp.zeros((), jnp.bfloat16),
        )
        d_values = d_values + jnp.einsum(
            "hqk,qhd->khd", scores_low, d_num_low, preferred_element_type=jnp.float32
        )
        d_fq_parts.append(
            jnp.einsum("hqk,khm->qhm", d_scores_low, fk_low, preferred_element_type=jnp.float32)
        )
        d_fk = d_fk + jnp.einsum(
            "hqk,qhm->khm", d_scores_low, fq_block, preferred_element_type=jnp.float32
        )
    return (jnp.concatenate(d_fq_parts, axis=0), d_fk, d_values)


def shards(
    tokens,
    ln_gain,
    ln_bias,
    qkv_weight,
    qkv_bias,
    out_weight,
    out_bias,
    fc1_weight,
    fc1_bias,
    fc2_weight,
    fc2_bias,
    cotangent,
    doc_lengths,
    node_seeds,
    node_weights,
):
    whole = (
        lax.all_gather(ln_gain, ("dp", "fsdp"), axis=0, tiled=True),
        lax.all_gather(ln_bias, ("dp", "fsdp"), axis=0, tiled=True),
        lax.all_gather(qkv_weight, ("dp", "fsdp"), axis=0, tiled=True),
        lax.all_gather(qkv_bias, ("dp", "fsdp"), axis=0, tiled=True),
        lax.all_gather(out_weight, ("dp", "fsdp"), axis=0, tiled=True),
        lax.all_gather(out_bias, ("dp", "fsdp"), axis=0, tiled=True),
        lax.all_gather(fc1_weight, ("dp", "fsdp"), axis=0, tiled=True),
        lax.all_gather(fc1_bias, ("dp", "fsdp"), axis=0, tiled=True),
        lax.all_gather(fc2_weight, ("dp", "fsdp"), axis=0, tiled=True),
        lax.all_gather(fc2_bias, ("dp", "fsdp"), axis=0, tiled=True),
    )
    (
        norm_gain,
        norm_shift,
        joint_weight,
        joint_bias,
        attn_weight,
        attn_bias,
        up_weight,
        up_bias,
        down_weight,
        down_bias,
    ) = whole
    rows_x = tokens.astype(jnp.float32)
    center = rows_x - jnp.mean(rows_x, axis=-1, keepdims=True)
    inv_std = lax.rsqrt(jnp.mean(center * center, axis=-1, keepdims=True) + epsilon)
    normed = center * inv_std
    hidden = normed * norm_gain.astype(jnp.float32) + norm_shift.astype(jnp.float32)
    hidden_low = hidden.astype(jnp.bfloat16)
    mixed = plain_dot(hidden_low, joint_weight) + joint_bias.astype(jnp.float32)
    upper = plain_dot(hidden_low, up_weight) + up_bias.astype(jnp.float32)
    act_low = jax.nn.gelu(upper, approximate=False).astype(jnp.bfloat16)
    branch_mlp = plain_dot(act_low, down_weight) + down_bias.astype(jnp.float32)
    projection, quad = tables(node_seeds, node_weights)
    seq = 0
    doc_ids, positions = layout(doc_lengths[seq])
    cos_table, sin_table = rotary(positions)
    query_heads = mixed[:, :D].reshape(LEN, HEADS, HD)
    key_heads = mixed[:, D : 2 * D].reshape(LEN, HEADS, HD)
    values_low = mixed[:, 2 * D :].reshape(LEN, HEADS, HD).astype(jnp.bfloat16)
    fq_low = (features(query_heads, cos_table, sin_table, projection) * quad).astype(jnp.bfloat16)
    fk_low = features(key_heads, cos_table, sin_table, projection).astype(jnp.bfloat16)
    attn_seq, denom = attend(fq_low, fk_low, values_low, doc_ids)
    kept = [
        (
            doc_ids,
            cos_table,
            sin_table,
            query_heads,
            key_heads,
            values_low,
            fq_low,
            fk_low,
            attn_seq,
            denom,
        )
    ]
    attn_parts = attn_seq.reshape(LEN, D)
    attn_low = attn_parts.astype(jnp.bfloat16)
    branch_attn = plain_dot(attn_low, attn_weight) + attn_bias.astype(jnp.float32)
    output = rows_x + branch_attn + branch_mlp
    again = (
        lax.all_gather(ln_gain, ("dp", "fsdp"), axis=0, tiled=True),
        lax.all_gather(ln_bias, ("dp", "fsdp"), axis=0, tiled=True),
        lax.all_gather(qkv_weight, ("dp", "fsdp"), axis=0, tiled=True),
        lax.all_gather(qkv_bias, ("dp", "fsdp"), axis=0, tiled=True),
        lax.all_gather(out_weight, ("dp", "fsdp"), axis=0, tiled=True),
        lax.all_gather(out_bias, ("dp", "fsdp"), axis=0, tiled=True),
        lax.all_gather(fc1_weight, ("dp", "fsdp"), axis=0, tiled=True),
        lax.all_gather(fc1_bias, ("dp", "fsdp"), axis=0, tiled=True),
        lax.all_gather(fc2_weight, ("dp", "fsdp"), axis=0, tiled=True),
        lax.all_gather(fc2_bias, ("dp", "fsdp"), axis=0, tiled=True),
    )
    (
        norm_gain,
        norm_shift,
        joint_weight,
        joint_bias,
        attn_weight,
        attn_bias,
        up_weight,
        up_bias,
        down_weight,
        down_bias,
    ) = again
    dy_low = cotangent.astype(jnp.bfloat16)
    dy_sums = jnp.sum(dy_low.astype(jnp.float32), axis=0)
    g_down_weight = outer_sum(act_low, dy_low)
    g_attn_weight = outer_sum(attn_low, dy_low)
    d_up_low = (back_proj(dy_low, down_weight) * gelu_slope(upper)).astype(jnp.bfloat16)
    g_up_weight = outer_sum(hidden_low, d_up_low)
    g_up_bias = jnp.sum(d_up_low.astype(jnp.float32), axis=0)
    d_attn = back_proj(dy_low, attn_weight)
    seq = 0
    (
        doc_ids,
        cos_table,
        sin_table,
        query_heads,
        key_heads,
        values_low,
        fq_low,
        fk_low,
        attn_seq,
        denom,
    ) = kept[seq]
    grad_out = d_attn.reshape(LEN, HEADS, HD)
    d_fq, d_fk, d_values = attend_back(
        fq_low, fk_low, values_low, doc_ids, grad_out, attn_seq, denom
    )

    def feature_pair(query_part, key_part):
        return (
            features(query_part, cos_table, sin_table, projection) * quad,
            features(key_part, cos_table, sin_table, projection),
        )

    unused, pull = jax.vjp(feature_pair, query_heads, key_heads)
    d_queries, d_keys = pull((d_fq, d_fk))
    d_mixed_parts = jnp.concatenate(
        [d_queries.reshape(LEN, D), d_keys.reshape(LEN, D), d_values.reshape(LEN, D)], axis=1
    )
    d_mixed_low = d_mixed_parts.astype(jnp.bfloat16)
    g_joint_weight = outer_sum(hidden_low, d_mixed_low)
    g_joint_bias = jnp.sum(d_mixed_low.astype(jnp.float32), axis=0)
    d_hidden = back_proj(d_mixed_low, joint_weight) + back_proj(d_up_low, up_weight)
    g_norm_gain = jnp.sum(d_hidden * normed, axis=0)
    g_norm_shift = jnp.sum(d_hidden, axis=0)
    d_normed = d_hidden * norm_gain.astype(jnp.float32)
    mean_grad = jnp.mean(d_normed, axis=-1, keepdims=True)
    mean_cross = jnp.mean(d_normed * normed, axis=-1, keepdims=True)
    input_grad = cotangent + inv_std * (d_normed - mean_grad - normed * mean_cross)
    reduced = (
        lax.psum_scatter(g_norm_gain, ("dp", "fsdp"), scatter_dimension=0, tiled=True),
        lax.psum_scatter(g_norm_shift, ("dp", "fsdp"), scatter_dimension=0, tiled=True),
        lax.psum_scatter(g_joint_weight, ("dp", "fsdp"), scatter_dimension=0, tiled=True),
        lax.psum_scatter(g_joint_bias, ("dp", "fsdp"), scatter_dimension=0, tiled=True),
        lax.psum_scatter(g_attn_weight, ("dp", "fsdp"), scatter_dimension=0, tiled=True),
        lax.psum_scatter(dy_sums, ("dp", "fsdp"), scatter_dimension=0, tiled=True),
        lax.psum_scatter(g_up_weight, ("dp", "fsdp"), scatter_dimension=0, tiled=True),
        lax.psum_scatter(g_up_bias, ("dp", "fsdp"), scatter_dimension=0, tiled=True),
        lax.psum_scatter(g_down_weight, ("dp", "fsdp"), scatter_dimension=0, tiled=True),
        lax.psum_scatter(dy_sums, ("dp", "fsdp"), scatter_dimension=0, tiled=True),
    )
    return (
        output,
        input_grad,
        reduced[0],
        reduced[1],
        reduced[2],
        reduced[3],
        reduced[4],
        reduced[5],
        reduced[6],
        reduced[7],
        reduced[8],
        reduced[9],
    )


def solution(mesh):
    in_specs = (
        P(("dp", "fsdp"), None),
        P(("dp", "fsdp")),
        P(("dp", "fsdp")),
        P(("dp", "fsdp"), None),
        P(("dp", "fsdp")),
        P(("dp", "fsdp"), None),
        P(("dp", "fsdp")),
        P(("dp", "fsdp"), None),
        P(("dp", "fsdp")),
        P(("dp", "fsdp"), None),
        P(("dp", "fsdp")),
        P(("dp", "fsdp"), None),
        P(("dp", "fsdp"), None),
        P(),
        P(),
    )
    out_specs = (
        P(("dp", "fsdp"), None),
        P(("dp", "fsdp"), None),
        P(("dp", "fsdp")),
        P(("dp", "fsdp")),
        P(("dp", "fsdp"), None),
        P(("dp", "fsdp")),
        P(("dp", "fsdp"), None),
        P(("dp", "fsdp")),
        P(("dp", "fsdp"), None),
        P(("dp", "fsdp")),
        P(("dp", "fsdp"), None),
        P(("dp", "fsdp")),
    )
    return jax.shard_map(shards, mesh=mesh, in_specs=in_specs, out_specs=out_specs, check_vma=False)
```

profile of v0, /device:TPU:0, one launch (start us, length us, event | category | flops | bytes accessed | tf_op | source)
XLA Modules:
  0.0 979.2 jit_solution(15464834726994419618)
XLA Ops:
  18.3 43.3 %all-reduce.17 = (bf16[3072]{0:T(1024)(128)(2,1)S(1)}, bf16[1024]{0:T(1024)(128)(2,1)S(1)}, bf16[1024]{0:T(1024)(128)(2,1)S(1)}, bf16[1024]{0:T(1024)(128)(2,1)}, bf16[1024]{0:T(1024)(128)(2,1)}) all-reduce(bf16[3072]{0:T(1024)(128)(2,1)S(1)} %dynamic-update-slice.2, ...), channel_id=1, replica_groups=mesh['dp'=2,'fsdp'=16] {'dp','fsdp'}, use_global_device_ids=true, to_apply=%add.8 | all-reduce | flops 7168 | bytes 28672
  79.7 62.0 %all-gather.6.cloned.1.call-done = bf16[1024,3072]{1,0:T(8,128)(2,1)} async-done(((bf16[32,3072]{1,0:T(8,128)(2,1)}), bf16[1024,3072]{1,0:T(8,128)(2,1)}) %all-gather.6.cloned.1.call-update) | async-done | bytes 6291472 | tf_op jit(solution)/shard_map/all_gather | solution.py:181
  141.8 9.0 broadcast_add_fusion
  207.6 13.2 %bitcast_divide_fusion.1 = f32[512,16,64]{0,2,1:T(8,128)} fusion(bf16[1024,16,64]{0,2,1:T(8,128)(2,1)} %bitcast.93, bf16[16,512,1024]{2,1,0:T(8,128)(2,1)} %get-tuple-element.61, pred[512,1024]{1,0:T(8,128)(4,1)} %get-tuple-element.50, f32[512,16]{0,1:T(8,128)S(1)} %bitcast.104), kind=kOutput, calls=%fused_computation.87 | convolution fusion | flops 1082654720 | bytes 21528576 | tf_op jit(solution)/shard_map/hqk,khd->qhd/dot_general | solution.py:115
  220.8 11.8 %multiply_reduce_fusion.3 = (f32[512,16]{0,1:T(8,128)S(1)}, f32[512,16]{0,1:T(8,128)S(1)}, bf16[512,16,64]{0,2,1:T(8,128)(2,1)S(1)}, bf16[512,16,64]{0,2,1:T(8,128)(2,1)S(1)}) fusion(f32[1024,1024]{0,1:T(8,128)} %copy-done.21, f32[512,16,64]{0,2,1:T(8,128)} %bitcast_divide_fusion.1, f32[512,16]{0,1:T(8,128)S(1)} %bitcast.101, ...), kind=kOutput, calls=%fused_computation.88 | convolution fusion | flops 1085784064 | bytes 27885568 | tf_op jit(solution)/shard_map/hqk,khd->qhd/dot_general | solution.py:115
  239.2 11.7 %fusion.9 = bf16[16,512,1024]{2,1,0:T(8,128)(2,1)} fusion(f32[16,512]{1,0:T(8,128)S(1)} %bitcast_divide_fusion.3, pred[512,1024]{1,0:T(8,128)(4,1)} %get-tuple-element.50, bf16[1024,16,64]{0,2,1:T(8,128)(2,1)} %bitcast.95, f32[512,16,64]{0,2,1:T(8,128)} %bitcast.99, f32[512,16]{0,1:T(8,128)S(1)} %bitcast.105), kind=kOutput, calls=%fused_computation.17 | convolution fusion | flops 1099956224 | bytes 21561344 | tf_op jit(solution)/shard_map/qhd,khd->hqk/dot_general | solution.py:141
  250.9 10.8 %fusion.52 = f32[16,64,1024]{2,1,0:T(8,128)} fusion(bf16[16,512,1024]{2,1,0:T(8,128)(2,1)} %fusion.9, bf16[1024,16,64]{0,2,1:T(8,128)(2,1)S(1)} %copy-done.14), kind=kOutput, calls=%fused_computation.105 | convolution fusion | flops 1073741824 | bytes 22020096 | tf_op jit(solution)/shard_map/hqk,qhm->khm/dot_general | solution.py:155
  261.8 12.9 %convolution_bitcast_fusion.1 = f32[512,16,64]{0,2,1:T(8,128)} fusion(bf16[1024,16,64]{0,2,1:T(8,128)(2,1)} %copy-done.5, bf16[16,512,1024]{2,1,0:T(8,128)(2,1)} %fusion.9), kind=kOutput, calls=%fused_computation.100 | convolution fusion | flops 1073741824 | bytes 20971520 | tf_op jit(solution)/shard_map/hqk,khm->qhm/dot_general | solution.py:153
  274.8 11.3 %fusion.10 = bf16[16,512,1024]{2,1,0:T(8,128)(2,1)} fusion(f32[16,512]{1,0:T(8,128)S(1)} %bitcast_divide_fusion.2, pred[512,1024]{1,0:T(8,128)(4,1)} %get-tuple-element.51, bf16[1024,16,64]{0,2,1:T(8,128)(2,1)} %bitcast.96, f32[512,16,64]{0,2,1:T(8,128)} %bitcast.97, f32[512,16]{0,1:T(8,128)S(1)} %bitcast.102), kind=kOutput, calls=%fused_computation.18 | convolution fusion | flops 1099956224 | bytes 21561344 | tf_op jit(solution)/shard_map/qhd,khd->hqk/dot_general | solution.py:141
  303.5 13.0 %convolution_bitcast_fusion = f32[512,16,64]{0,2,1:T(8,128)} fusion(bf16[1024,16,64]{0,2,1:T(8,128)(2,1)} %copy-done.5, bf16[16,512,1024]{2,1,0:T(8,128)(2,1)} %fusion.10), kind=kOutput, calls=%fused_computation.99 | convolution fusion | flops 1073741824 | bytes 20971520 | tf_op jit(solution)/shard_map/hqk,khm->qhm/dot_general | solution.py:153
  338.5 11.3 %fusion.18 = f32[16,64,1024]{2,1,0:T(8,128)} fusion(bf16[16,512,1024]{2,1,0:T(8,128)(2,1)} %get-tuple-element.61, pred[512,1024]{1,0:T(8,128)(4,1)S(1)} %copy-done.31, f32[512,16,64]{0,2,1:T(8,128)S(1)} %bitcast.100, f32[512,16]{0,1:T(8,128)S(1)} %bitcast.106), kind=kOutput, calls=%fused_computation.41 | convolution fusion | flops 1083179008 | bytes 23625728 | tf_op jit(solution)/shard_map/hqk,qhd->khd/dot_general | solution.py:149
  349.8 12.4 %add_convert_fusion.2 = bf16[16,64,1024]{2,1,0:T(8,128)(2,1)} fusion(f32[16,64,1024]{2,1,0:T(8,128)} %fusion.18, bf16[16,512,1024]{2,1,0:T(8,128)(2,1)} %get-tuple-element.59, pred[512,1024]{1,0:T(8,128)(4,1)S(1)} %copy-done.29, f32[512,16,64]{0,2,1:T(8,128)} %bitcast.98, f32[512,16]{0,1:T(8,128)S(1)} %bitcast.103), kind=kOutput, calls=%fused_computation.71 | convolution fusion | flops 1085276160 | bytes 25722880 | tf_op jit(solution)/shard_map/hqk,qhd->khd/dot_general | solution.py:149
  362.2 14.8 %fusion.172 = f32[1024,3072]{1,0:T(8,128)} fusion(bf16[1024,1024]{0,1:T(8,128)(2,1)} %bitcast.90, bf16[1024,1024]{0,1:T(8,128)(2,1)} %bitcast.82, bf16[1024,1024]{0,1:T(8,128)(2,1)} %bitcast.85, bf16[1024,1024]{1,0:T(8,128)(2,1)S(1)} %copy-done.7, f32[1024]{0:T(1024)S(1)} %copy-done.44, f32[1024]{0:T(1024)S(1)} %copy-done.41, f32[1024]{0:T(1024)S(1)} %copy-done.39, ...), kind=kOutput, calls=%fused_computation.256 | convolution fusion | flops 6467616768 | bytes 20987904 | tf_op jit(solution)/shard_map/dot_general | solution.py:76
  377.7 39.4 %all-gather = bf16[32,1,128]{2,1,0:T(2,128)(2,1)S(1)} all-gather(bf16[1,1,128]{2,1,0:T(2,128)(2,1)S(1)} %bitcast.109), channel_id=1, replica_groups=mesh['dp'=2,'fsdp'=16] {'dp','fsdp'}, dimensions={0}, use_global_device_ids=true | all-gather | bytes 8448 | tf_op jit(solution)/shard_map/all_gather | solution.py:186
  417.1 49.2 %fusion.2 = (bf16[1024,4096]{1,0:T(8,128)(2,1)S(1)}, f32[1024,4096]{1,0:T(8,128)}) fusion(f32[4096]{0:T(1024)S(1)} %bitcast.107, bf16[1024,4096]{1,0:T(8,128)(2,1)} %all-gather.10.cloned.1.call-done, bf16[1024,1024]{1,0:T(8,128)(2,1)S(1)} %copy-done.7, f32[1024]{0:T(1024)S(1)} %copy-done.44, f32[1024]{0:T(1024)S(1)} %copy-done.41, f32[1024]{0:T(1024)S(1)} %copy-done.39, ...), kind=kOutput, calls=%fused_computation.10 | convolution fusion | flops 8873050112 | bytes 35684352 | tf_op jit(solution)/shard_map/dot_general | solution.py:72
  469.6 11.7 %fusion.187 = f32[4096,1024]{1,0:T(8,128)} fusion(bf16[1024,4096]{1,0:T(8,128)(2,1)S(1)} %get-tuple-element.63, bf16[1024,1024]{1,0:T(8,128)(2,1)S(1)} %copy-done.26), kind=kOutput, calls=%fused_computation.267 | convolution fusion | flops 8589934592 | bytes 27262976 | tf_op jit(solution)/shard_map/dot_general | solution.py:76
  481.5 18.5 %convert_reduce_fusion = (f32[4096]{0:T(1024)S(1)}, bf16[1024,4096]{1,0:T(8,128)(2,1)S(1)}) fusion(f32[1024,4096]{1,0:T(8,128)} %get-tuple-element.64, f32[4096]{0:T(1024)S(1)} %bitcast.108, bf16[1024,1024]{1,0:T(8,128)(2,1)} %get-tuple-element.29, bf16[4096,1024]{1,0:T(8,128)(2,1)} %all-gather.12.cloned.1.call-done), kind=kOutput, calls=%fused_computation.19 | convolution fusion | flops 8644456448 | bytes 35684352 | tf_op jit(solution)/shard_map/dot_general | solution.py:82
  503.3 12.2 %fusion.174 = f32[1024,4096]{1,0:T(8,128)} fusion(bf16[1024,4096]{1,0:T(8,128)(2,1)S(1)} %get-tuple-element.69, bf16[1024,1024]{1,0:T(8,128)(2,1)S(1)} %copy-done.7, f32[1024]{0:T(1024)S(1)} %copy-done.44, f32[1024]{0:T(1024)S(1)} %copy-done.41, f32[1024]{0:T(1024)S(1)} %copy-done.39, f32[1024]{0:T(1024)S(1)} %copy-done.37), kind=kOutput, calls=%fused_computation.258 | convolution fusion | flops 8596226048 | bytes 27279360 | tf_op jit(solution)/shard_map/dot_general | solution.py:76
  526.0 9.6 fusion.173
  535.6 16.8 %fusion.34 = (f32[1024]{0:T(1024)S(1)}, f32[1024]{0:T(1024)S(1)}, f32[1024]{0:T(1024)S(1)}, f32[1024]{0:T(1024)S(1)}, f32[1024,1024]{1,0:T(8,128)}) fusion(bf16[1024,1024]{1,0:T(8,128)(2,1)S(1)} %copy-done.7, f32[1024]{0:T(1024)S(1)} %copy-done.39, f32[1024]{0:T(1024)S(1)} %copy-done.37, f32[1024]{0:T(1024)S(1)} %copy-done.41, ...), kind=kOutput, calls=%fused_computation.57 | convolution fusion | flops 8601464832 | bytes 27291648 | tf_op jit(solution)/shard_map/dot_general | solution.py:82
  552.4 39.0 %all-reduce.16 = (f32[1024]{0:T(1024)S(1)}, f32[1024]{0:T(1024)S(1)}, f32[3072]{0:T(1024)S(1)}, f32[1024]{0:T(1024)S(1)}, f32[4096]{0:T(1024)S(1)}) all-reduce(f32[1024]{0:T(1024)S(1)} %get-tuple-element.12, f32[1024]{0:T(1024)S(1)} %get-tuple-element.15, ...), channel_id=2, replica_groups=mesh['dp'=2,'fsdp'=16] {'dp','fsdp'}, use_global_device_ids=true, to_apply=%region_17.18.clone | all-reduce | flops 10240 | bytes 81920
  599.8 15.1 %fusion.36 = f32[1024,1024]{1,0:T(8,128)} fusion(bf16[1024,1024]{1,0:T(8,128)(2,1)S(1)} %copy-done.7, f32[1024,1024]{1,0:T(8,128)S(1)} %copy-done.57, f32[1024]{0:T(1024)S(1)} %convert_element_type.135, f32[1024]{0:T(1024)S(1)} %convert_element_type.132, bf16[1024,4096]{1,0:T(8,128)(2,1)} %copy-done.58, bf16[4096,1024]{1,0:T(8,128)(2,1)} %all-gather.12.cloned.1.call-done), kind=kOutput, calls=%fused_computation.59 | convolution fusion | flops 8595177472 | bytes 27271168 | tf_op jit(solution)/shard_map/dot_general | solution.py:72
  614.9 169.6 %reduce-scatter.11.cloned.1.call-done = f32[128,1024]{1,0:T(8,128)} async-done(((f32[4096,1024]{1,0:T(8,128)}), f32[128,1024]{1,0:T(8,128)}) %reduce-scatter.11.cloned.1.call-update) | async-done | bytes 524304 | tf_op jit(solution)/shard_map/reduce_scatter | solution.py:320
  784.5 187.2 %reduce-scatter.9.cloned.1.call-done = f32[32,4096]{1,0:T(8,128)} async-done(((f32[1024,4096]{1,0:T(8,128)}), f32[32,4096]{1,0:T(8,128)}) %reduce-scatter.9.cloned.1.call-update) | async-done | bytes 524304 | tf_op jit(solution)/shard_map/reduce_scatter | solution.py:318
  (223 shorter events, 158.1 us)
Async XLA Ops:
  7.2 54.6 %copy-start.49 = (s32[64,64]{1,0:T(8,128)S(1)}, s32[64,64]{1,0:T(8,128)}, u32[]{:S(2)}) copy-start(s32[64,64]{1,0:T(8,128)} %param.28) | copy-start | bytes 49156
  7.3 63.2 %all-gather.8.cloned.1.call-start = ((), (), s32[]{:S(2)}) async-start(), calls=%async_computation.5 | async-start | bytes 2162688 | tf_op jit(solution)/shard_map/all_gather | solution.py:183
  8.0 133.8 %all-gather.6.cloned.1.call-start = ((), (), s32[]{:S(2)}) async-start(), calls=%async_computation.4 | async-start | bytes 6488064 | tf_op jit(solution)/shard_map/all_gather | solution.py:181
  8.7 408.4 %all-gather.10.cloned.1.call-start = ((), (), s32[]{:S(2)}) async-start(), calls=%async_computation.6 | async-start | bytes 8650752 | tf_op jit(solution)/shard_map/all_gather | solution.py:185
  9.5 472.0 %all-gather.12.cloned.1.call-start = ((), (), s32[]{:S(2)}) async-start(), calls=%async_computation.7 | async-start | bytes 8650752 | tf_op jit(solution)/shard_map/all_gather | solution.py:187
  10.0 604.8 %reduce-scatter.7.cloned.1.call-start = ((), (), s32[]{:S(2)}) async-start(), calls=%async_computation.9 | async-start | bytes 4325376 | tf_op jit(solution)/shard_map/reduce_scatter | solution.py:316
  16.3 125.4 %copy-start.36 = (f32[1024]{0:T(1024)}, f32[1024]{0:T(1024)S(1)}, u32[]{:S(2)}) copy-start(f32[1024]{0:T(1024)S(1)} %broadcast_multiply_fusion.4) | copy-start | bytes 12292
  17.1 124.7 %copy-start.38 = (f32[1024]{0:T(1024)}, f32[1024]{0:T(1024)S(1)}, u32[]{:S(2)}) copy-start(f32[1024]{0:T(1024)S(1)} %add_rsqrt_fusion) | copy-start | bytes 12292
  61.6 80.2 %copy-start.40 = (f32[1024]{0:T(1024)}, f32[1024]{0:T(1024)S(1)}, u32[]{:S(2)}) copy-start(f32[1024]{0:T(1024)S(1)} %convert_element_type.116) | copy-start | bytes 12292
  61.6 80.2 %copy-start.43 = (f32[1024]{0:T(1024)}, f32[1024]{0:T(1024)S(1)}, u32[]{:S(2)}) copy-start(f32[1024]{0:T(1024)S(1)} %convert_element_type.117) | copy-start | bytes 12292
  61.8 111.0 %copy-start.32 = (f32[1024,8]{0,1:T(8,128)}, f32[1024,8]{0,1:T(8,128)S(1)}, u32[]{:S(2)}) copy-start(f32[1024,8]{0,1:T(8,128)S(1)} %get-tuple-element.48) | copy-start | bytes 98308
  61.8 111.0 %copy-start.34 = (f32[1024,8]{0,1:T(8,128)}, f32[1024,8]{0,1:T(8,128)S(1)}, u32[]{:S(2)}) copy-start(f32[1024,8]{0,1:T(8,128)S(1)} %get-tuple-element.49) | copy-start | bytes 98308
  183.7 15.1 %copy-start.5 = (bf16[1024,16,64]{0,2,1:T(8,128)(2,1)}, bf16[1024,16,64]{0,2,1:T(8,128)(2,1)S(1)}, u32[]{:S(2)}) copy-start(bf16[1024,16,64]{0,2,1:T(8,128)(2,1)S(1)} %get-tuple-element.54) | copy-start | bytes 6291460
  274.7 340.2 %reduce-scatter.5.cloned.1.call-start = ((), (), s32[]{:S(2)}) async-start(), calls=%async_computation.8 | async-start | bytes 12976128 | tf_op jit(solution)/shard_map/reduce_scatter | solution.py:314
  349.8 12.4 %copy-start.7 = (bf16[1024,1024]{1,0:T(8,128)(2,1)S(1)}, bf16[1024,1024]{1,0:T(8,128)(2,1)}, u32[]{:S(2)}) copy-start(bf16[1024,1024]{1,0:T(8,128)(2,1)} %param.15) | copy-start | bytes 6291460
  349.8 12.4 %copy-start.37 = (f32[1024]{0:T(1024)S(1)}, f32[1024]{0:T(1024)}, u32[]{:S(2)}) copy-start(f32[1024]{0:T(1024)} %copy-done.36) | copy-start | bytes 12292
  349.8 12.4 %copy-start.39 = (f32[1024]{0:T(1024)S(1)}, f32[1024]{0:T(1024)}, u32[]{:S(2)}) copy-start(f32[1024]{0:T(1024)} %copy-done.38) | copy-start | bytes 12292
  349.8 12.4 %copy-start.41 = (f32[1024]{0:T(1024)S(1)}, f32[1024]{0:T(1024)}, u32[]{:S(2)}) copy-start(f32[1024]{0:T(1024)} %copy-done.40) | copy-start | bytes 12292
  349.8 12.4 %copy-start.44 = (f32[1024]{0:T(1024)S(1)}, f32[1024]{0:T(1024)}, u32[]{:S(2)}) copy-start(f32[1024]{0:T(1024)} %copy-done.43) | copy-start | bytes 12292
  377.0 407.4 %reduce-scatter.11.cloned.1.call-start = ((), (), s32[]{:S(2)}) async-start(), calls=%async_computation.11 | async-start | bytes 17301504 | tf_op jit(solution)/shard_map/reduce_scatter | solution.py:320
  417.1 52.5 %copy-start.26 = (bf16[1024,1024]{1,0:T(8,128)(2,1)S(1)}, bf16[1024,1024]{1,0:T(8,128)(2,1)}, u32[]{:S(2)}) copy-start(bf16[1024,1024]{1,0:T(8,128)(2,1)} %get-tuple-element.29) | copy-start | bytes 6291460
  481.4 490.3 %reduce-scatter.9.cloned.1.call-start = ((), (), s32[]{:S(2)}) async-start(), calls=%async_computation.10 | async-start | bytes 17301504 | tf_op jit(solution)/shard_map/reduce_scatter | solution.py:318
  535.6 16.8 %copy-start.42 = (f32[1024]{0:T(1024)S(1)}, f32[1024]{0:T(1024)}, u32[]{:S(2)}) copy-start(f32[1024]{0:T(1024)} %get-tuple-element.28) | copy-start | bytes 12292
  592.1 379.6 %copy-start.55 = (f32[32]{0:T(128)}, f32[32]{0:T(128)S(1)}, u32[]{:S(2)}) copy-start(f32[32]{0:T(128)S(1)} %dynamic-slice.3) | copy-start | bytes 388
  (45 other events, 259.2 us)
Sparse Core Ops, SparseCore 0:
  10.9 59.4 all-gather.7
  73.3 68.4 all-gather.5
  144.6 75.9 all-gather.9
  223.3 75.9 all-gather.11
  302.0 139.8 reduce-scatter.6
  448.3 153.0 reduce-scatter.4
  604.3 180.0 reduce-scatter.10
  787.4 184.1 reduce-scatter.8
where the time goes:
time: 986 us; the launch traced here: 979 us
  waiting for transfers between devices  423 us (43%)
  matrix products  332 us (34%)
  blocking collectives  122 us (12%)
  local copies, waits for them, and re-layouts  49.4 us (5%)
  other arithmetic  37.6 us (4%)
  between operations  15.2 us (2%)
    reduce_scatter x1, waiting for transfers between devices, shards(): lax.psum_scatter(g_up_weight, ('dp', 'fsdp'), scatter_dimension=0, tiled=...  187 us
    reduce_scatter x1, waiting for transfers between devices, shards(): lax.psum_scatter(g_down_weight, ('dp', 'fsdp'), scatter_dimension=0, tile...  170 us
    unnamed x2, blocking collectives  82.3 us
    dot_general x4, matrix products, plain_dot(): return jnp.dot(left, right, preferred_element_type=jnp.float32)  77.8 us
    all_gather x1, waiting for transfers between devices, shards(): lax.all_gather(qkv_weight, ('dp', 'fsdp'), axis=0, tiled=True)  62 us
    dot_general x4, matrix products, back_proj(): lax.dot_general(left, right, (((1,), (1,)), ((), ())), preferred_element_...  49.5 us
    dot_general x4, matrix products, outer_sum(): lax.dot_general(left, right, (((0,), (0,)), ((), ())), preferred_element_...  43.1 us
    all_gather x1, blocking collectives, shards(): lax.all_gather(fc1_bias, ('dp', 'fsdp'), axis=0, tiled=True)  39.4 us
  transfers between devices with their start and end apart: 8, of which 4 were waited for; matrix products, arithmetic and copies ran while one was open for 41% of the time, Pallas kernels for 0%

commit v1 on v0

v1 whole, which is shorter than its diff:
```python
import functools
import math

import jax
import jax.numpy as jnp
from jax import lax
from jax.experimental import pallas as pl
from jax.experimental.pallas import tpu as pltpu
from jax.sharding import PartitionSpec as P

D = 1024
HEADS = 16
HD = 64
ROT = 16
LEN = 1024
DOCS = 4
FF = 4096
AXES = ("dp", "fsdp")

feature_scale = 0.2
epsilon = 1e-05
precise = lax.Precision.HIGHEST
bf16 = jnp.bfloat16
f32 = jnp.float32


class Grid:
    def __init__(self, dp, fsdp):
        self.dp, self.fsdp = dp, fsdp
        rest = fsdp // 2
        self.nx = 4 if rest % 16 == 0 else 2
        self.nz = rest // self.nx
        self.ny = dp
        self.n = dp * fsdp
        self.sizes = {"y": self.ny, "z": self.nz, "x": self.nx, "c": 2}
        self.stride = {"y": fsdp, "z": self.nx * 2, "x": 2, "c": 1}

    def digits(self):
        y = lax.axis_index("dp")
        f = lax.axis_index("fsdp")
        return {"y": y, "z": f // (self.nx * 2), "x": (f // 2) % self.nx, "c": f % 2}

    def swap(self, value, digit, k):
        stride = self.stride[digit]
        size = self.sizes[digit]
        pairs = []
        for i in range(self.n):
            d = (i // stride) % size
            pairs.append((i, i + ((d ^ k) - d) * stride))
        return lax.ppermute(value, AXES, pairs)


def place(pieces, outs, moves):
    n_in = len(pieces)
    n_out = len(outs)

    def body(*refs):
        ins, res, sem = refs[:n_in], refs[n_in : n_in + n_out], refs[-1]
        copies = []
        for i, (src, src_at, dst, dst_at) in enumerate(moves):
            copies.append(
                pltpu.make_async_copy(ins[src].at[src_at()], res[dst].at[dst_at()], sem.at[i])
            )
        for copy in copies:
            copy.start()
        for copy in copies:
            copy.wait()

    total = sum(math.prod(o.shape) * o.dtype.itemsize for o in outs)
    return pl.pallas_call(
        body,
        out_shape=tuple(outs),
        in_specs=[pl.BlockSpec(memory_space=pl.ANY)] * n_in,
        out_specs=tuple([pl.BlockSpec(memory_space=pl.ANY)] * n_out),
        scratch_shapes=[pltpu.SemaphoreType.DMA((len(moves),))],
        cost_estimate=pl.CostEstimate(flops=0, transcendentals=0, bytes_accessed=2 * total),
        name="place",
    )(*pieces)


def gather(grid, shard, cut, fields):
    rows, cols = shard.shape
    ny, nz, nx = grid.ny, grid.nz, grid.nx
    dt = shard.dtype
    spans = ((0, cut), (cut, cols))

    pieces = [shard] + [grid.swap(shard, "z", k) for k in range(1, nz)]
    outs = [jax.ShapeDtypeStruct((nz, rows, hi - lo), dt) for lo, hi in spans]
    moves = []
    for k in range(nz):
        for half, (lo, hi) in enumerate(spans):
            moves.append(
                (
                    k,
                    lambda lo=lo, hi=hi: (slice(None), pl.ds(lo, hi - lo)),
                    half,
                    lambda k=k: (grid.digits()["z"] ^ k,),
                )
            )
    part_a, part_b = place(pieces, outs, moves)

    pieces_a = [part_a] + [grid.swap(part_a, "x", k) for k in range(1, nx)]
    pieces_b = [part_b] + [grid.swap(part_b, "y", k) for k in range(1, ny)]
    (part_a,) = place(
        pieces_a,
        [jax.ShapeDtypeStruct((nz, nx) + part_a.shape[1:], dt)],
        [
            (k, lambda: (slice(None),), 0, lambda k=k: (slice(None), grid.digits()["x"] ^ k))
            for k in range(nx)
        ],
    )
    (part_b,) = place(
        pieces_b,
        [jax.ShapeDtypeStruct((ny, nz) + part_b.shape[1:], dt)],
        [(k, lambda: (slice(None),), 0, lambda k=k: (grid.digits()["y"] ^ k,)) for k in range(ny)],
    )
    pieces_a = [part_a] + [grid.swap(part_a, "y", k) for k in range(1, ny)]
    pieces_b = [part_b] + [grid.swap(part_b, "x", k) for k in range(1, nx)]
    every = []
    for half, group in ((0, pieces_a), (1, pieces_b)):
        for k, piece in enumerate(group):
            every.append((half, k, 0, piece))
            every.append((half, k, 1, grid.swap(piece, "c", 1)))
    outs = [
        jax.ShapeDtypeStruct((ny, nz, nx, 2, blocks, rows, width // blocks), dt)
        for _, width, blocks in fields
    ]
    moves = []
    for p, (half, k, core, _) in enumerate(every):
        lo, hi = spans[half]
        for o, (first, width, blocks) in enumerate(fields):
            step = width // blocks
            for b in range(blocks):
                start, end = max(lo, first + b * step), min(hi, first + (b + 1) * step)
                if start >= end:
                    continue

                def src_at(start=start, end=end, lo=lo):
                    return (slice(None), slice(None), slice(None), pl.ds(start - lo, end - start))

                def dst_at(half=half, k=k, core=core, b=b, start=start, end=end, at=first + b * step):
                    d = grid.digits()
                    tail = (d["c"] ^ core, b, slice(None), pl.ds(start - at, end - start))
                    if half == 0:
                        return (d["y"] ^ k, slice(None), slice(None)) + tail
                    return (slice(None), slice(None), d["x"] ^ k) + tail

                moves.append((p, src_at, o, dst_at))
    full = place([e[3] for e in every], outs, moves)
    return [
        w.reshape(grid.n * blocks * rows, width // blocks)
        for w, (_, width, blocks) in zip(full, fields)
    ]


def pick(value, axis, index):
    return lax.dynamic_index_in_dim(value, index, axis, keepdims=False)


def reduce_to_owner(grid, grad):
    n = grid.n
    rows = grad.shape[0] // n
    cols = grad.shape[1]
    d = grid.digits()
    ny, nz, nx = grid.ny, grid.nz, grid.nx
    whole = grad.reshape(ny, nz, nx, 2, rows, cols)
    got = grid.swap(pick(whole, 3, 1 - d["c"]), "c", 1)
    terms = [pick(whole, 3, d["c"]), got]

    def total(parts):
        out = parts[0].astype(f32)
        for part in parts[1:]:
            out = out + part.astype(f32)
        return out

    halves = []
    for half in range(2):
        lo = half * (cols // 2)
        now = [t[..., lo : lo + cols // 2] for t in terms]
        order = (("x", 2), ("y", 0)) if half == 0 else (("y", 0), ("x", 1))
        for digit, axis in order:
            size = grid.sizes[digit]
            arrived = [
                grid.swap(total([pick(t, axis, d[digit] ^ k) for t in now]).astype(bf16), digit, k)
                for k in range(1, size)
            ]
            now = [pick(t, axis, d[digit]) for t in now] + arrived
        halves.append(total(now).astype(bf16))
    joint = jnp.concatenate(halves, axis=-1)
    arrived = [grid.swap(pick(joint, 0, d["z"] ^ k), "z", k) for k in range(1, nz)]
    return total([pick(joint, 0, d["z"])] + arrived)


def reduce_small(grid, grad):
    d = grid.digits()
    now = grad.reshape(grid.ny, grid.nz, grid.nx, 2, grad.shape[1])
    for digit, axis in (("c", 3), ("x", 2), ("y", 0), ("z", 0)):
        mine = pick(now, axis, d[digit])
        for k in range(1, grid.sizes[digit]):
            mine = mine + grid.swap(pick(now, axis, d[digit] ^ k), digit, k)
        now = mine
    return now


def tables(node_seeds, node_weights):
    width = node_seeds.shape[1]
    uniform_pts = (node_seeds.astype(jnp.float32) + 0.5) / 1024.0
    nodes = math.sqrt(2.0) * lax.erf_inv(2.0 * uniform_pts - 1.0)
    order = jnp.arange(width).astype(jnp.float32)
    scales = jnp.where(order[:, None] == 0.0, math.sqrt(1.0 / width), math.sqrt(2.0 / width))
    basis = scales * jnp.cos(
        math.pi * (2.0 * order[None, :] + 1.0) * order[:, None] / (2.0 * width)
    )
    projection = jnp.dot(nodes, basis, precision=precise)
    weights_float = node_weights.astype(jnp.float32)
    return (projection, weights_float / jnp.sum(weights_float))


def layout(lengths):
    ends = jnp.cumsum(lengths)
    starts = ends - lengths
    places = jnp.arange(LEN, dtype=jnp.int32)
    doc_ids = jnp.sum((places[:, None] >= ends[None, :]).astype(jnp.int32), axis=1)
    owners = doc_ids[:, None] == jnp.arange(DOCS, dtype=jnp.int32)[None, :]
    begins = jnp.sum(jnp.where(owners, starts[None, :], 0), axis=1)
    return (doc_ids, (places - begins).astype(jnp.float32))


def rotary(positions):
    half_rot = ROT // 2
    freqs = 10000.0 ** (-2.0 * jnp.arange(half_rot).astype(jnp.float32) / ROT)
    angles = positions[:, None] * freqs[None, :]
    return (jnp.cos(angles), jnp.sin(angles))


def rotate(heads, cos_table, sin_table):
    half_rot = cos_table.shape[1]
    first = heads[..., :half_rot]
    second = heads[..., half_rot : 2 * half_rot]
    rest = heads[..., 2 * half_rot :]
    cos_wide = cos_table[:, None, :]
    sin_wide = sin_table[:, None, :]
    return jnp.concatenate(
        [first * cos_wide - second * sin_wide, second * cos_wide + first * sin_wide, rest], axis=-1
    )


def features(heads, cos_table, sin_table, projection):
    turned = feature_scale * rotate(heads, cos_table, sin_table)
    exponent = jnp.einsum("lhd,md->lhm", turned, projection, precision=precise)
    exponent = exponent - 0.5 * jnp.sum(turned * turned, axis=-1, keepdims=True)
    return jnp.exp(exponent)


def plain_dot(left, right):
    return jnp.dot(left, right, preferred_element_type=jnp.float32)


def outer_sum(left, right, out=jnp.float32):
    return lax.dot_general(left, right, (((0,), (0,)), ((), ())), preferred_element_type=out)


def back_proj(left, right):
    return lax.dot_general(
        left, right, (((1,), (1,)), ((), ())), preferred_element_type=jnp.float32
    )


def gelu_slope(upper):
    return 0.5 * (1.0 + lax.erf(upper / math.sqrt(2.0))) + upper * jnp.exp(
        -0.5 * upper * upper
    ) / math.sqrt(2.0 * math.pi)


def block_mask(doc_ids, first, block):
    places = jnp.arange(doc_ids.shape[0], dtype=jnp.int32)
    rows_here = places[first : first + block]
    same_doc = doc_ids[first : first + block, None] == doc_ids[None, :]
    return same_doc & (rows_here[:, None] >= places[None, :])


def attend(fq_low, fk_low, values_low, doc_ids):
    seq_len = doc_ids.shape[0]
    block = min(512, seq_len)
    outputs = []
    denoms = []
    for first in range(0, seq_len, block):
        mask = block_mask(doc_ids, first, block)
        raw = jnp.einsum(
            "qhm,khm->hqk",
            fq_low[first : first + block],
            fk_low,
            preferred_element_type=jnp.float32,
        )
        scores = jnp.where(mask[None], raw, 0.0)
        denom = jnp.sum(scores, axis=-1)
        numer = jnp.einsum(
            "hqk,khd->qhd",
            scores.astype(jnp.bfloat16),
            values_low,
            preferred_element_type=jnp.float32,
        )
        outputs.append(numer / denom.T[:, :, None])
        denoms.append(denom)
    return (jnp.concatenate(outputs, axis=0), jnp.concatenate(denoms, axis=1))


def attend_back(fq_low, fk_low, values_low, doc_ids, grad_out, attn_out, denom):
    seq_len = doc_ids.shape[0]
    block = min(512, seq_len)
    d_values = jnp.zeros(values_low.shape, jnp.float32)
    d_fk = jnp.zeros(fk_low.shape, jnp.float32)
    d_fq_parts = []
    for first in range(0, seq_len, block):
        mask = block_mask(doc_ids, first, block)
        fq_block = fq_low[first : first + block]
        raw = jnp.einsum("qhm,khm->hqk", fq_block, fk_low, preferred_element_type=jnp.float32)
        scores_low = jnp.where(mask[None], raw, 0.0).astype(jnp.bfloat16)
        den_block = denom[:, first : first + block].T
        grad_block = grad_out[first : first + block]
        d_num_low = (grad_block / den_block[:, :, None]).astype(jnp.bfloat16)
        d_denom = -jnp.sum(grad_block * attn_out[first : first + block], axis=-1) / den_block
        d_prod = jnp.einsum(
            "qhd,khd->hqk", d_num_low, values_low, preferred_element_type=jnp.float32
        )
        d_scores_low = jnp.where(
            mask[None],
            (d_prod + d_denom.T[:, :, None]).astype(jnp.bfloat16),
            jnp.zeros((), jnp.bfloat16),
        )
        d_values = d_values + jnp.einsum(
            "hqk,qhd->khd", scores_low, d_num_low, preferred_element_type=jnp.float32
        )
        d_fq_parts.append(
            jnp.einsum("hqk,khm->qhm", d_scores_low, fk_low, preferred_element_type=jnp.float32)
        )
        d_fk = d_fk + jnp.einsum(
            "hqk,qhm->khm", d_scores_low, fq_block, preferred_element_type=jnp.float32
        )
    return (jnp.concatenate(d_fq_parts, axis=0), d_fk, d_values)


def shards(
    grid,
    tokens,
    ln_gain,
    ln_bias,
    qkv_weight,
    qkv_bias,
    out_weight,
    out_bias,
    fc1_weight,
    fc1_bias,
    fc2_weight,
    fc2_bias,
    cotangent,
    doc_lengths,
    node_seeds,
    node_weights,
):
    n = grid.n
    rows = qkv_weight.shape[0]
    staged = rows % 16 == 0
    vectors = (ln_gain, ln_bias, qkv_bias, out_bias, fc1_bias, fc2_bias)
    small = jnp.concatenate(vectors)
    per_row = small.shape[0] // rows
    small = jnp.pad(small.reshape(rows, per_row), ((0, 0), (0, 128 - per_row)))
    if staged:
        first = jnp.concatenate([qkv_weight, small], axis=1)
        joint_weight, small_all = gather(grid, first, 13 * 128, ((0, 3072, 1), (3072, 128, 1)))
        blocks = fc2_weight.shape[0] // rows
        folded = fc2_weight.reshape(blocks, rows, D).transpose(1, 0, 2).reshape(rows, blocks * D)
        second = jnp.concatenate([out_weight, fc1_weight, folded], axis=1)
        attn_weight, up_weight, down_weight = gather(
            grid, second, 9 * 512, ((0, D, 1), (D, FF, 1), (D + FF, FF, blocks))
        )
    else:
        joint_weight, small_all, attn_weight, up_weight, down_weight = [
            lax.all_gather(w, AXES, axis=0, tiled=True)
            for w in (qkv_weight, small, out_weight, fc1_weight, fc2_weight)
        ]
    small_all = small_all[:, :per_row].reshape(n, rows * per_row)
    wide = []
    at = 0
    for v in vectors:
        wide.append(small_all[:, at : at + v.shape[0]].reshape(n * v.shape[0]).astype(f32))
        at += v.shape[0]
    norm_gain, norm_shift, joint_bias, attn_bias, up_bias, down_bias = wide

    rows_x = tokens.astype(jnp.float32)
    center = rows_x - jnp.mean(rows_x, axis=-1, keepdims=True)
    inv_std = lax.rsqrt(jnp.mean(center * center, axis=-1, keepdims=True) + epsilon)
    normed = center * inv_std
    hidden = normed * norm_gain + norm_shift
    hidden_low = hidden.astype(jnp.bfloat16)
    dy_low = cotangent.astype(jnp.bfloat16)
    dy_sums = jnp.sum(dy_low.astype(jnp.float32), axis=0)

    mixed = plain_dot(hidden_low, joint_weight) + joint_bias
    projection, quad = tables(node_seeds, node_weights)
    doc_ids, positions = layout(doc_lengths[0])
    cos_table, sin_table = rotary(positions)
    query_heads = mixed[:, :D].reshape(LEN, HEADS, HD)
    key_heads = mixed[:, D : 2 * D].reshape(LEN, HEADS, HD)
    values_low = mixed[:, 2 * D :].reshape(LEN, HEADS, HD).astype(jnp.bfloat16)
    fq_low = (features(query_heads, cos_table, sin_table, projection) * quad).astype(jnp.bfloat16)
    fk_low = features(key_heads, cos_table, sin_table, projection).astype(jnp.bfloat16)
    attn_seq, denom = attend(fq_low, fk_low, values_low, doc_ids)
    attn_low = attn_seq.reshape(LEN, D).astype(jnp.bfloat16)

    branch_attn = plain_dot(attn_low, attn_weight) + attn_bias
    g_attn_weight = outer_sum(attn_low, dy_low, bf16)
    grad_out = back_proj(dy_low, attn_weight).reshape(LEN, HEADS, HD)
    d_fq, d_fk, d_values = attend_back(
        fq_low, fk_low, values_low, doc_ids, grad_out, attn_seq, denom
    )

    def feature_pair(query_part, key_part):
        return (
            features(query_part, cos_table, sin_table, projection) * quad,
            features(key_part, cos_table, sin_table, projection),
        )

    unused, pull = jax.vjp(feature_pair, query_heads, key_heads)
    d_queries, d_keys = pull((d_fq, d_fk))
    d_mixed_low = jnp.concatenate(
        [d_queries.reshape(LEN, D), d_keys.reshape(LEN, D), d_values.reshape(LEN, D)], axis=1
    ).astype(jnp.bfloat16)
    g_joint_weight = outer_sum(hidden_low, d_mixed_low, bf16)
    g_joint_bias = jnp.sum(d_mixed_low.astype(jnp.float32), axis=0)

    upper = plain_dot(hidden_low, up_weight) + up_bias
    act_low = jax.nn.gelu(upper, approximate=False).astype(jnp.bfloat16)
    g_down_weight = outer_sum(act_low, dy_low, bf16)
    d_up_low = (back_proj(dy_low, down_weight) * gelu_slope(upper)).astype(jnp.bfloat16)
    g_up_weight = outer_sum(hidden_low, d_up_low, bf16)
    g_up_bias = jnp.sum(d_up_low.astype(jnp.float32), axis=0)
    branch_mlp = plain_dot(act_low, down_weight) + down_bias
    output = rows_x + branch_attn + branch_mlp

    d_hidden = back_proj(d_mixed_low, joint_weight) + back_proj(d_up_low, up_weight)
    g_norm_gain = jnp.sum(d_hidden * normed, axis=0)
    g_norm_shift = jnp.sum(d_hidden, axis=0)
    d_normed = d_hidden * norm_gain
    mean_grad = jnp.mean(d_normed, axis=-1, keepdims=True)
    mean_cross = jnp.mean(d_normed * normed, axis=-1, keepdims=True)
    input_grad = cotangent + inv_std * (d_normed - mean_grad - normed * mean_cross)

    grads = (g_norm_gain, g_norm_shift, g_joint_bias, dy_sums, g_up_bias)
    packed = jnp.concatenate([g.reshape(n, -1) for g in grads], axis=1)
    if staged:
        attn_part = reduce_to_owner(grid, jnp.concatenate([g_attn_weight, g_joint_weight], axis=1))
        s_attn, s_joint = attn_part[:, :D], attn_part[:, D:]
        s_down = reduce_to_owner(grid, g_down_weight)
        s_up = reduce_to_owner(grid, g_up_weight)
        s_small = reduce_small(grid, packed)
    else:
        s_attn, s_joint, s_down, s_up = [
            lax.psum_scatter(g.astype(f32), AXES, scatter_dimension=0, tiled=True)
            for g in (g_attn_weight, g_joint_weight, g_down_weight, g_up_weight)
        ]
        s_small = lax.psum_scatter(packed, AXES, scatter_dimension=0, tiled=True)[0]
    small_outs = []
    at = 0
    for g in grads:
        small_outs.append(s_small[at : at + g.shape[0] // n])
        at += g.shape[0] // n
    s_gain, s_shift, s_joint_bias, s_dy, s_up_bias = small_outs
    return (
        output,
        input_grad,
        s_gain,
        s_shift,
        s_joint,
        s_joint_bias,
        s_attn,
        s_dy,
        s_up,
        s_up_bias,
        s_down,
        s_dy,
    )


def solution(mesh):
    grid = Grid(mesh.shape["dp"], mesh.shape["fsdp"])
    rows2, rows1 = P(AXES, None), P(AXES)
    in_specs = (
        rows2,
        rows1,
        rows1,
        rows2,
        rows1,
        rows2,
        rows1,
        rows2,
        rows1,
        rows2,
        rows1,
        rows2,
        rows2,
        P(),
        P(),
    )
    out_specs = (
        rows2,
        rows2,
        rows1,
        rows1,
        rows2,
        rows1,
        rows2,
        rows1,
        rows2,
        rows1,
        rows2,
        rows1,
    )
    return jax.shard_map(
        functools.partial(shards, grid),
        mesh=mesh,
        in_specs=in_specs,
        out_specs=out_specs,
        check_vma=False,
    )
```

time: 986 us -> 1780 us (1.81)
  Pallas kernels: 0 us -> 1070 us
  waiting for transfers between devices: 423 us -> 129 us
  blocking collectives: 122 us -> 0 us
  starting transfers between devices: 0.32 us -> 99 us
  local copies, waits for them, and re-layouts: 49.4 us -> 97.9 us
    pallas_call x0 -> x8, Pallas kernels: none -> 1070 us  [place(): pl.pallas_call(body, out_shape=tuple(outs), in_specs=[pl.BlockSpec(memory...]
    reduce_scatter x4 -> x0, waiting for transfers between devices: 357 us -> none  [the longest x1 187 us: shards(): lax.psum_scatter(g_up_weight, ('dp', 'fsdp'), scatter_dimension=0, tiled=...]
    ppermute x0 -> x52, waiting for transfers between devices: none -> 129 us  [swap(): return lax.ppermute(value, AXES, pairs)]
    ppermute x0 -> x52, starting transfers between devices: none -> 99 us  [swap(): return lax.ppermute(value, AXES, pairs)]
    unnamed x2 -> x0, blocking collectives: 82.3 us -> none
    all_gather x4 -> x0, waiting for transfers between devices: 63.7 us -> none  [the longest x1 62 us: shards(): lax.all_gather(qkv_weight, ('dp', 'fsdp'), axis=0, tiled=True)]
    all_gather x1 -> x0, blocking collectives: 39.4 us -> none  [shards(): lax.all_gather(fc1_bias, ('dp', 'fsdp'), axis=0, tiled=True)]
    dynamic_slice x0 -> x12, local copies, waits for them, and re-layouts: none -> 34.8 us  [pick(): return lax.dynamic_index_in_dim(value, index, axis, keepdims=False)]
  transfers between devices with their start and end apart: 8 -> 52, of which waited for: 4 -> 17; matrix products, arithmetic and copies ran while one was open for 41% -> 11% of each run, Pallas kernels for 0% -> 28%
where the time goes in v1:
time: 1780 us
  Pallas kernels  1070 us (60%)
  matrix products  333 us (19%)
  waiting for transfers between devices  129 us (7%)
  starting transfers between devices  99 us (6%)
  local copies, waits for them, and re-layouts  97.9 us (6%)
  other arithmetic  45.7 us (3%)
    pallas_call x8, Pallas kernels, place(): pl.pallas_call(body, out_shape=tuple(outs), in_specs=[pl.BlockSpec(memory...  1070 us
    ppermute x52, waiting for transfers between devices, swap(): return lax.ppermute(value, AXES, pairs)  129 us
    ppermute x52, starting transfers between devices, swap(): return lax.ppermute(value, AXES, pairs)  99 us
    dot_general x4, matrix products, plain_dot(): return jnp.dot(left, right, preferred_element_type=jnp.float32)  76.6 us
    dot_general x4, matrix products, back_proj(): lax.dot_general(left, right, (((1,), (1,)), ((), ())), preferred_element_...  49.9 us
    dot_general x4, matrix products, outer_sum(): lax.dot_general(left, right, (((0,), (0,)), ((), ())), preferred_element_...  46.2 us
  transfers between devices with their start and end apart: 52, of which 17 were waited for; matrix products, arithmetic and copies ran while one was open for 11% of the time, Pallas kernels for 28%

profile of v1, /device:TPU:0, one launch (start us, length us, event | category | flops | bytes accessed | tf_op | source)
XLA Modules:
  0.0 1776.6 jit_solution(17283650595783539582)
XLA Ops:
  22.3 28.7 %collective-permute-start = (bf16[32,3200]{1,0:T(8,128)(2,1)S(1)}, bf16[32,3200]{1,0:T(8,128)(2,1)}, u32[]{:S(2)}, u32[]{:S(2)}) collective-permute-start(bf16[32,3200]{1,0:T(8,128)(2,1)S(1)} %fusion.118.refs_0_), channel_id=1, source_target_pairs={{0,4},{1,5},{2,6},{3,7},{4,0},{5,1},{6,2},{7,3},{8,12},{9,13},{10,... | collective-permute-start | bytes 614408 | tf_op jit(solution)/shard_map/ppermute | solution.py:50
  62.2 26.0 %place.8 = (bf16[4,32,1664]{2,1,0:T(8,128)(2,1)}, bf16[4,32,1536]{2,1,0:T(8,128)(2,1)}) custom-call(bf16[32,3200]{1,0:T(8,128)(2,1)} %copy-done.50, bf16[32,3200]{1,0:T(8,128)(2,1)} %collective-permute-done.refs_1_, bf16[32,3200]{1,0:T(8,128)(2,1)} %collective-permute-done.1.refs_2_, bf16[32,3200]{1,0:T(8,128)(2,1)} %collective-permute-done.2.refs_3_), custom_call_target="tpu_custom_call" | custom-call | bytes 1638400 | tf_op jit(solution)/shard_map/place/pallas_call | solution.py:70
  92.3 72.6 %place.12 = (bf16[4,32,4608]{2,1,0:T(8,128)(2,1)}, bf16[4,32,4608]{2,1,0:T(8,128)(2,1)}) custom-call(bf16[32,9216]{1,0:T(8,128)(2,1)} %copy-done.51, bf16[32,9216]{1,0:T(8,128)(2,1)} %collective-permute-done.11.refs_1_, bf16[32,9216]{1,0:T(8,128)(2,1)} %collective-permute-done.12.refs_2_, bf16[32,9216]{1,0:T(8,128)(2,1)} %copy-done.52), custom_call_target="tpu_custom_call" | custom-call | bytes 4718592 | tf_op jit(solution)/shard_map/place/pallas_call | solution.py:70
  165.5 26.9 %place.9.refs_0_ = bf16[4,2,32,1664]{3,2,1,0:T(8,128)(2,1)} custom-call(bf16[4,32,1664]{2,1,0:T(8,128)(2,1)} %get-tuple-element.21.refs_0_, bf16[4,32,1664]{2,1,0:T(8,128)(2,1)} %collective-permute-done.3.refs_1_), custom_call_target="tpu_custom_call" | custom-call | bytes 1703936 | tf_op jit(solution)/shard_map/place/pallas_call | solution.py:70
  194.5 25.0 %place.10.refs_4_ = bf16[2,4,32,1536]{3,2,1,0:T(8,128)(2,1)} custom-call(bf16[4,32,1536]{2,1,0:T(8,128)(2,1)} %get-tuple-element.22.refs_0_, bf16[4,32,1536]{2,1,0:T(8,128)(2,1)} %collective-permute-done.7.refs_1_), custom_call_target="tpu_custom_call" | custom-call | bytes 1572864 | tf_op jit(solution)/shard_map/place/pallas_call | solution.py:70
  227.4 12.9 collective-permute-done.9.refs_6_
  243.9 72.6 %place.14.refs_4_ = bf16[2,4,32,4608]{3,2,1,0:T(8,128)(2,1)} custom-call(bf16[4,32,4608]{2,1,0:T(8,128)(2,1)} %get-tuple-element.26.refs_0_, bf16[4,32,4608]{2,1,0:T(8,128)(2,1)} %collective-permute-done.18.refs_1_), custom_call_target="tpu_custom_call" | custom-call | bytes 4718592 | tf_op jit(solution)/shard_map/place/pallas_call | solution.py:70
  317.1 72.6 %place.13.refs_0_ = bf16[4,2,32,4608]{3,2,1,0:T(8,128)(2,1)} custom-call(bf16[4,32,4608]{2,1,0:T(8,128)(2,1)} %get-tuple-element.25.refs_0_, bf16[4,32,4608]{2,1,0:T(8,128)(2,1)} %collective-permute-done.14.refs_1_), custom_call_target="tpu_custom_call" | custom-call | bytes 4718592 | tf_op jit(solution)/shard_map/place/pallas_call | solution.py:70
  390.6 199.7 %place.11 = (bf16[2,4,2,2,1,32,3072]{6,5,4,3,2,1,0:T(8,128)(2,1)}, bf16[2,4,2,2,1,32,128]{6,5,4,3,2,1,0:T(8,128)(2,1)}) custom-call(bf16[4,2,32,1664]{3,2,1,0:T(8,128)(2,1)} %place.9.refs_0_, bf16[4,2,32,1664]{3,2,1,0:T(8,128)(2,1)} %collective-permute-done.4.refs_1_, bf16[4,2,32,1664]{3,2,1,0:T(8,128)(2,1)} %collective-permute-done.5.refs_2_, ...), custom_call_target="tpu_custom_call" | custom-call | bytes 13107200 | tf_op jit(solution)/shard_map/place/pallas_call | solution.py:70
  661.6 12.9 bitcast_divide_fusion.1
  676.0 573.1 %place.15 = (bf16[2,4,2,2,1,32,1024]{6,5,4,3,2,1,0:T(8,128)(2,1)}, bf16[2,4,2,2,1,32,4096]{6,5,4,3,2,1,0:T(8,128)(2,1)}, bf16[2,4,2,2,4,32,1024]{6,5,4,3,2,1,0:T(8,128)(2,1)}) custom-call(bf16[4,2,32,4608]{3,2,1,0:T(8,128)(2,1)} %place.13.refs_0_, bf16[4,2,32,4608]{3,2,1,0:T(8,128)(2,1)} %collective-permute-done.15.refs_1_, ...), custom_call_target="tpu_custom_call" | custom-call | bytes 37748736 | tf_op jit(solution)/shard_map/place/pallas_call | solution.py:70
  1322.8 12.3 convolution_bitcast_fusion.1
  1368.1 49.8 %fusion.2 = (bf16[1024,4096]{1,0:T(8,128)(2,1)}, f32[1024,4096]{1,0:T(8,128)}) fusion(f32[4096]{0:T(1024)S(1)} %copy-done.73, bf16[1024,4096]{1,0:T(8,128)(2,1)S(1)} %bitcast.334, bf16[1024,1024]{1,0:T(8,128)(2,1)S(1)} %copy-done.8, f32[1024]{0:T(1024)S(1)} %copy-done.80, f32[1024]{0:T(1024)S(1)} %copy-done.70, f32[1024]{0:T(1024)S(1)} %copy-done.72, ...), kind=kOutput, calls=%fused_computation.10 | convolution fusion | flops 8873050112 | bytes 35684352 | tf_op jit(solution)/shard_map/dot_general | solution.py:256
  1417.9 19.1 %convert_reduce_fusion = (f32[4096]{0:T(1024)}, bf16[1024,4096]{1,0:T(8,128)(2,1)}) fusion(f32[1024,4096]{1,0:T(8,128)} %get-tuple-element.114, f32[4096]{0:T(1024)S(1)} %copy-done.73, bf16[4096,1024]{1,0:T(8,128)(2,1)S(1)} %bitcast.328, bf16[1024,1024]{1,0:T(8,128)(2,1)S(1)} %copy-done.36), kind=kOutput, calls=%fused_computation.19 | convolution fusion | flops 8644456448 | bytes 35684352 | tf_op jit(solution)/shard_map/dot_general | solution.py:264
  1436.9 12.6 fusion.262
  1449.5 15.4 fusion.245
  1465.0 12.4 add_convert_fusion.2
  1516.2 14.8 fusion.264
  1531.1 13.7 fusion.34
  1568.1 13.4 fusion.36
  1633.3 13.2 collective-permute-done.29
  1650.9 18.1 %collective-permute-done.45 = bf16[2,4,128,512]{3,2,1,0:T(8,128)(2,1)S(1)} collective-permute-done((bf16[2,4,128,512]{3,2,1,0:T(8,128)(2,1)S(1)}, bf16[2,4,128,512]{3,2,1,0:T(8,128)(2,1)S(1)}, u32[]{:S(2)}, u32[]{:S(2)}) %collective-permute-start.45) | collective-permute-done | bytes 1048608 | tf_op jit(solution)/shard_map/ppermute | solution.py:50
  1672.8 18.7 %collective-permute-done.37 = bf16[2,4,32,2048]{3,2,1,0:T(8,128)(2,1)S(1)} collective-permute-done((bf16[2,4,32,2048]{3,2,1,0:T(8,128)(2,1)S(1)}, bf16[2,4,32,2048]{3,2,1,0:T(8,128)(2,1)S(1)}, u32[]{:S(2)}, u32[]{:S(2)}) %collective-permute-start.37) | collective-permute-done | bytes 1048608 | tf_op jit(solution)/shard_map/ppermute | solution.py:50
  1738.0 17.1 collective-permute-start.42
  (430 shorter events, 420.5 us)
Async XLA Ops:
  11.1 43.8 %collective-permute-start.1 = (bf16[32,3200]{1,0:T(8,128)(2,1)S(1)}, bf16[32,3200]{1,0:T(8,128)(2,1)}, u32[]{:S(2)}, u32[]{:S(2)}) collective-permute-start(bf16[32,3200]{1,0:T(8,128)(2,1)S(1)} %fusion.118.refs_0_), channel_id=1, source_target_pairs={{0,8},{1,9},{2,10},{3,11},{4,12},{5,13},{6,14},{7,15},{8,0},{9,1},... | collective-permute-start | bytes 614408 | tf_op jit(solution)/shard_map/ppermute | solution.py:50
  14.2 77.3 %collective-permute-start.13 = (bf16[32,9216]{1,0:T(8,128)(2,1)S(1)}, bf16[32,9216]{1,0:T(8,128)(2,1)S(1)}, u32[]{:S(2)}, u32[]{:S(2)}) collective-permute-start(bf16[32,9216]{1,0:T(8,128)(2,1)S(1)} %constant_dynamic-update-slice_fusion.refs_0_), channel_id=1, source_target_pairs={{0,12},{1,13},{2,14},{3,15},{4,8},{5,9},{6,10},{7,11},{8,4},{9,5},... | collective-permute-start | bytes 1769480 | tf_op jit(solution)/shard_map/ppermute | solution.py:50
  16.2 75.3 %collective-permute-start.12 = (bf16[32,9216]{1,0:T(8,128)(2,1)S(1)}, bf16[32,9216]{1,0:T(8,128)(2,1)}, u32[]{:S(2)}, u32[]{:S(2)}) collective-permute-start(bf16[32,9216]{1,0:T(8,128)(2,1)S(1)} %constant_dynamic-update-slice_fusion.refs_0_), channel_id=1, source_target_pairs={{0,8},{1,9},{2,10},{3,11},{4,12},{5,13},{6,14},{7,15},{8,0},{9,1},... | collective-permute-start | bytes 1769480 | tf_op jit(solution)/shard_map/ppermute | solution.py:50
  17.3 74.2 %collective-permute-start.11 = (bf16[32,9216]{1,0:T(8,128)(2,1)S(1)}, bf16[32,9216]{1,0:T(8,128)(2,1)}, u32[]{:S(2)}, u32[]{:S(2)}) collective-permute-start(bf16[32,9216]{1,0:T(8,128)(2,1)S(1)} %constant_dynamic-update-slice_fusion.refs_0_), channel_id=1, source_target_pairs={{0,4},{1,5},{2,6},{3,7},{4,0},{5,1},{6,2},{7,3},{8,12},{9,13},{10,... | collective-permute-start | bytes 1769480 | tf_op jit(solution)/shard_map/ppermute | solution.py:50
  88.2 77.3 %collective-permute-start.3 = (bf16[4,32,1664]{2,1,0:T(8,128)(2,1)}, bf16[4,32,1664]{2,1,0:T(8,128)(2,1)}, u32[]{:S(2)}, u32[]{:S(2)}) collective-permute-start(bf16[4,32,1664]{2,1,0:T(8,128)(2,1)} %get-tuple-element.21.refs_0_), channel_id=1, source_target_pairs={{0,2},{1,3},{2,0},{3,1},{4,6},{5,7},{6,4},{7,5},{8,10},{9,11},{10,... | collective-permute-start | bytes 1277960 | tf_op jit(solution)/shard_map/ppermute | solution.py:50
  89.9 104.6 %collective-permute-start.7 = (bf16[4,32,1536]{2,1,0:T(8,128)(2,1)}, bf16[4,32,1536]{2,1,0:T(8,128)(2,1)}, u32[]{:S(2)}, u32[]{:S(2)}) collective-permute-start(bf16[4,32,1536]{2,1,0:T(8,128)(2,1)} %get-tuple-element.22.refs_0_), channel_id=1, source_target_pairs={{0,16},{1,17},{2,18},{3,19},{4,20},{5,21},{6,22},{7,23},{8,24},{9,... | collective-permute-start | bytes 1179656 | tf_op jit(solution)/shard_map/ppermute | solution.py:50
  164.9 75.4 %collective-permute-start.18 = (bf16[4,32,4608]{2,1,0:T(8,128)(2,1)}, bf16[4,32,4608]{2,1,0:T(8,128)(2,1)}, u32[]{:S(2)}, u32[]{:S(2)}) collective-permute-start(bf16[4,32,4608]{2,1,0:T(8,128)(2,1)} %get-tuple-element.26.refs_0_), channel_id=1, source_target_pairs={{0,16},{1,17},{2,18},{3,19},{4,20},{5,21},{6,22},{7,23},{8,24},{9,... | collective-permute-start | bytes 3538952 | tf_op jit(solution)/shard_map/ppermute | solution.py:50
  224.0 92.5 %collective-permute-start.14 = (bf16[4,32,4608]{2,1,0:T(8,128)(2,1)}, bf16[4,32,4608]{2,1,0:T(8,128)(2,1)}, u32[]{:S(2)}, u32[]{:S(2)}) collective-permute-start(bf16[4,32,4608]{2,1,0:T(8,128)(2,1)} %get-tuple-element.25.refs_0_), channel_id=1, source_target_pairs={{0,2},{1,3},{2,0},{3,1},{4,6},{5,7},{6,4},{7,5},{8,10},{9,11},{10,... | collective-permute-start | bytes 3538952 | tf_op jit(solution)/shard_map/ppermute | solution.py:50
  226.8 163.0 %collective-permute-start.4 = (bf16[4,2,32,1664]{3,2,1,0:T(8,128)(2,1)S(1)}, bf16[4,2,32,1664]{3,2,1,0:T(8,128)(2,1)}, u32[]{:S(2)}, u32[]{:S(2)}) collective-permute-start(bf16[4,2,32,1664]{3,2,1,0:T(8,128)(2,1)S(1)} %copy-done.31), channel_id=1, source_target_pairs={{0,1},{1,0},{2,3},{3,2},{4,5},{5,4},{6,7},{7,6},{8,9},{9,8},{10,11... | collective-permute-start | bytes 2555912 | tf_op jit(solution)/shard_map/ppermute | solution.py:50
  226.9 163.6 %collective-permute-start.6 = (bf16[4,2,32,1664]{3,2,1,0:T(8,128)(2,1)}, bf16[4,2,32,1664]{3,2,1,0:T(8,128)(2,1)}, u32[]{:S(2)}, u32[]{:S(2)}) collective-permute-start(bf16[4,2,32,1664]{3,2,1,0:T(8,128)(2,1)} %collective-permute-done.5.refs_2_), channel_id=1, source_target_pairs={{0,1},{1,0},{2,3},{3,2},{4,5},{5,4},{6,7},{7,6},{8,9},{9,8},{10,11... | collective-permute-start | bytes 2555912 | tf_op jit(solution)/shard_map/ppermute | solution.py:50
  240.3 149.4 %collective-permute-start.8 = (bf16[2,4,32,1536]{3,2,1,0:T(8,128)(2,1)}, bf16[2,4,32,1536]{3,2,1,0:T(8,128)(2,1)}, u32[]{:S(2)}, u32[]{:S(2)}) collective-permute-start(bf16[2,4,32,1536]{3,2,1,0:T(8,128)(2,1)} %place.10.refs_4_), channel_id=1, source_target_pairs={{0,1},{1,0},{2,3},{3,2},{4,5},{5,4},{6,7},{7,6},{8,9},{9,8},{10,11... | collective-permute-start | bytes 2359304 | tf_op jit(solution)/shard_map/ppermute | solution.py:50
  240.3 150.1 %collective-permute-start.10 = (bf16[2,4,32,1536]{3,2,1,0:T(8,128)(2,1)}, bf16[2,4,32,1536]{3,2,1,0:T(8,128)(2,1)}, u32[]{:S(2)}, u32[]{:S(2)}) collective-permute-start(bf16[2,4,32,1536]{3,2,1,0:T(8,128)(2,1)} %collective-permute-done.9.refs_6_), channel_id=1, source_target_pairs={{0,1},{1,0},{2,3},{3,2},{4,5},{5,4},{6,7},{7,6},{8,9},{9,8},{10,11... | collective-permute-start | bytes 2359304 | tf_op jit(solution)/shard_map/ppermute | solution.py:50
  316.5 335.7 %collective-permute-start.20 = (bf16[2,4,32,4608]{3,2,1,0:T(8,128)(2,1)}, bf16[2,4,32,4608]{3,2,1,0:T(8,128)(2,1)}, u32[]{:S(2)}, u32[]{:S(2)}) collective-permute-start(bf16[2,4,32,4608]{3,2,1,0:T(8,128)(2,1)} %place.14.refs_4_), channel_id=1, source_target_pairs={{0,2},{1,3},{2,0},{3,1},{4,6},{5,7},{6,4},{7,5},{8,10},{9,11},{10,... | collective-permute-start | bytes 7077896 | tf_op jit(solution)/shard_map/ppermute | solution.py:50
  389.7 284.8 %collective-permute-start.19 = (bf16[2,4,32,4608]{3,2,1,0:T(8,128)(2,1)}, bf16[2,4,32,4608]{3,2,1,0:T(8,128)(2,1)}, u32[]{:S(2)}, u32[]{:S(2)}) collective-permute-start(bf16[2,4,32,4608]{3,2,1,0:T(8,128)(2,1)} %place.14.refs_4_), channel_id=1, source_target_pairs={{0,1},{1,0},{2,3},{3,2},{4,5},{5,4},{6,7},{7,6},{8,9},{9,8},{10,11... | collective-permute-start | bytes 7077896 | tf_op jit(solution)/shard_map/ppermute | solution.py:50
  389.8 262.8 %collective-permute-start.16 = (bf16[4,2,32,4608]{3,2,1,0:T(8,128)(2,1)}, bf16[4,2,32,4608]{3,2,1,0:T(8,128)(2,1)}, u32[]{:S(2)}, u32[]{:S(2)}) collective-permute-start(bf16[4,2,32,4608]{3,2,1,0:T(8,128)(2,1)} %place.13.refs_0_), channel_id=1, source_target_pairs={{0,16},{1,17},{2,18},{3,19},{4,20},{5,21},{6,22},{7,23},{8,24},{9,... | collective-permute-start | bytes 7077896 | tf_op jit(solution)/shard_map/ppermute | solution.py:50
  390.4 284.2 %collective-permute-start.15 = (bf16[4,2,32,4608]{3,2,1,0:T(8,128)(2,1)}, bf16[4,2,32,4608]{3,2,1,0:T(8,128)(2,1)}, u32[]{:S(2)}, u32[]{:S(2)}) collective-permute-start(bf16[4,2,32,4608]{3,2,1,0:T(8,128)(2,1)} %place.13.refs_0_), channel_id=1, source_target_pairs={{0,1},{1,0},{2,3},{3,2},{4,5},{5,4},{6,7},{7,6},{8,9},{9,8},{10,11... | collective-permute-start | bytes 7077896 | tf_op jit(solution)/shard_map/ppermute | solution.py:50
  1515.8 101.6 %collective-permute-start.28 = (bf16[2,4,2,32,4096]{4,3,1,0,2:T(8,128)(2,1)}, bf16[2,4,2,32,4096]{4,3,1,0,2:T(8,128)(2,1)}, u32[]{:S(2)}, u32[]{:S(2)}) collective-permute-start(bf16[2,4,2,32,4096]{4,3,1,0,2:T(8,128)(2,1)} %bitcast.279), channel_id=1, source_target_pairs={{0,1},{1,0},{2,3},{3,2},{4,5},{5,4},{6,7},{7,6},{8,9},{9,8},{10,11... | collective-permute-start | bytes 12582920 | tf_op jit(solution)/shard_map/ppermute | solution.py:50
  1563.1 60.9 %collective-permute-start.44 = (bf16[2,4,2,128,1024]{4,3,1,0,2:T(8,128)(2,1)}, bf16[2,4,2,128,1024]{4,3,1,0,2:T(8,128)(2,1)}, u32[]{:S(2)}, u32[]{:S(2)}) collective-permute-start(bf16[2,4,2,128,1024]{4,3,1,0,2:T(8,128)(2,1)} %bitcast.275), channel_id=1, source_target_pairs={{0,1},{1,0},{2,3},{3,2},{4,5},{5,4},{6,7},{7,6},{8,9},{9,8},{10,11... | collective-permute-start | bytes 12582920 | tf_op jit(solution)/shard_map/ppermute | solution.py:50
  1563.3 65.0 %collective-permute-start.36 = (bf16[2,4,2,32,4096]{4,3,1,0,2:T(8,128)(2,1)}, bf16[2,4,2,32,4096]{4,3,1,0,2:T(8,128)(2,1)}, u32[]{:S(2)}, u32[]{:S(2)}) collective-permute-start(bf16[2,4,2,32,4096]{4,3,1,0,2:T(8,128)(2,1)} %bitcast.277), channel_id=1, source_target_pairs={{0,1},{1,0},{2,3},{3,2},{4,5},{5,4},{6,7},{7,6},{8,9},{9,8},{10,11... | collective-permute-start | bytes 12582920 | tf_op jit(solution)/shard_map/ppermute | solution.py:50
  1627.8 43.2 %collective-permute-start.47 = (bf16[4,2,128,512]{3,2,0,1:T(8,128)(2,1)S(1)}, bf16[4,2,128,512]{3,2,0,1:T(8,128)(2,1)S(1)}, u32[]{:S(2)}, u32[]{:S(2)}) collective-permute-start(bf16[4,2,128,512]{3,2,0,1:T(8,128)(2,1)S(1)} %fusion.58), channel_id=1, source_target_pairs={{0,16},{1,17},{2,18},{3,19},{4,20},{5,21},{6,22},{7,23},{8,24},{9,... | collective-permute-start | bytes 3145736 | tf_op jit(solution)/shard_map/ppermute | solution.py:50
  1631.4 60.1 %collective-permute-start.37 = (bf16[2,4,32,2048]{3,2,1,0:T(8,128)(2,1)S(1)}, bf16[2,4,32,2048]{3,2,1,0:T(8,128)(2,1)S(1)}, u32[]{:S(2)}, u32[]{:S(2)}) collective-permute-start(bf16[2,4,32,2048]{3,2,1,0:T(8,128)(2,1)S(1)} %fusion.55), channel_id=1, source_target_pairs={{0,2},{1,3},{2,0},{3,1},{4,6},{5,7},{6,4},{7,5},{8,10},{9,11},{10,... | collective-permute-start | bytes 3145736 | tf_op jit(solution)/shard_map/ppermute | solution.py:50
  1646.5 47.0 %collective-permute-start.39 = (bf16[4,2,32,2048]{3,2,0,1:T(8,128)(2,1)S(1)}, bf16[4,2,32,2048]{3,2,0,1:T(8,128)(2,1)S(1)}, u32[]{:S(2)}, u32[]{:S(2)}) collective-permute-start(bf16[4,2,32,2048]{3,2,0,1:T(8,128)(2,1)S(1)} %fusion.56), channel_id=1, source_target_pairs={{0,16},{1,17},{2,18},{3,19},{4,20},{5,21},{6,22},{7,23},{8,24},{9,... | collective-permute-start | bytes 3145736 | tf_op jit(solution)/shard_map/ppermute | solution.py:50
  1650.1 54.7 %collective-permute-start.30 = (bf16[4,32,2048]{2,1,0:T(8,128)(2,1)S(1)}, bf16[4,32,2048]{2,1,0:T(8,128)(2,1)S(1)}, u32[]{:S(2)}, u32[]{:S(2)}) collective-permute-start(bf16[4,32,2048]{2,1,0:T(8,128)(2,1)S(1)} %fusion.76), channel_id=1, source_target_pairs={{0,16},{1,17},{2,18},{3,19},{4,20},{5,21},{6,22},{7,23},{8,24},{9,... | collective-permute-start | bytes 1572872 | tf_op jit(solution)/shard_map/ppermute | solution.py:50
  1671.0 44.9 %collective-permute-start.46 = (bf16[4,128,512]{2,1,0:T(8,128)(2,1)S(1)}, bf16[4,128,512]{2,1,0:T(8,128)(2,1)S(1)}, u32[]{:S(2)}, u32[]{:S(2)}) collective-permute-start(bf16[4,128,512]{2,1,0:T(8,128)(2,1)S(1)} %fusion.62), channel_id=1, source_target_pairs={{0,16},{1,17},{2,18},{3,19},{4,20},{5,21},{6,22},{7,23},{8,24},{9,... | collective-permute-start | bytes 1572872 | tf_op jit(solution)/shard_map/ppermute | solution.py:50
  (121 other events, 5046.5 us)

commit v2 on v1

v2 whole, which is shorter than its diff:
```python
import functools
import math

import jax
import jax.numpy as jnp
from jax import lax
from jax.experimental import pallas as pl
from jax.experimental.pallas import tpu as pltpu
from jax.sharding import PartitionSpec as P

D = 1024
HEADS = 16
HD = 64
ROT = 16
LEN = 1024
DOCS = 4
FF = 4096
AXES = ("dp", "fsdp")
PARTS = 2
BLOCK = 512

feature_scale = 0.2
epsilon = 1e-05
precise = lax.Precision.HIGHEST
bf16 = jnp.bfloat16
f32 = jnp.float32


class Grid:
    def __init__(self, dp, fsdp):
        self.dp, self.fsdp = dp, fsdp
        rest = fsdp // 2
        self.nx = 4 if rest % 16 == 0 else 2
        self.nz = rest // self.nx
        self.ny = dp
        self.n = dp * fsdp
        self.sizes = {"y": self.ny, "z": self.nz, "x": self.nx, "c": 2}
        self.stride = {"y": fsdp, "z": self.nx * 2, "x": 2, "c": 1}

    def digits(self):
        y = lax.axis_index("dp")
        f = lax.axis_index("fsdp")
        return {"y": y, "z": f // (self.nx * 2), "x": (f // 2) % self.nx, "c": f % 2}

    def swap(self, value, digit, k):
        stride = self.stride[digit]
        size = self.sizes[digit]
        pairs = []
        for i in range(self.n):
            d = (i // stride) % size
            pairs.append((i, i + ((d ^ k) - d) * stride))
        return lax.ppermute(value, AXES, pairs)


def place(pieces, outs, moves):
    n_in = len(pieces)
    n_out = len(outs)

    def body(*refs):
        ins, res = refs[:n_in], refs[n_in : n_in + n_out]
        held, sem, done = refs[n_in + n_out : n_in + 2 * n_out], refs[-2], refs[-1]
        copies = []
        for i, (src, src_at, dst, dst_at) in enumerate(moves):
            copies.append(
                pltpu.make_async_copy(ins[src].at[src_at()], held[dst].at[dst_at()], sem.at[i])
            )
        for copy in copies:
            copy.start()
        back = []
        for o in range(n_out):
            for copy, move in zip(copies, moves):
                if move[2] == o:
                    copy.wait()
            back.append(pltpu.make_async_copy(held[o], res[o], done.at[o]))
            back[-1].start()
        for copy in back:
            copy.wait()

    total = sum(math.prod(o.shape) * o.dtype.itemsize for o in outs)
    return pl.pallas_call(
        body,
        out_shape=tuple(outs),
        in_specs=[pl.BlockSpec(memory_space=pl.ANY)] * n_in,
        out_specs=tuple([pl.BlockSpec(memory_space=pl.ANY)] * n_out),
        scratch_shapes=[pltpu.VMEM(o.shape, o.dtype) for o in outs]
        + [pltpu.SemaphoreType.DMA((len(moves),)), pltpu.SemaphoreType.DMA((n_out,))],
        compiler_params=pltpu.CompilerParams(vmem_limit_bytes=total + (2 << 20)),
        cost_estimate=pl.CostEstimate(flops=0, transcendentals=0, bytes_accessed=2 * total),
        name="place",
    )(*pieces)


def gather(grid, shard, cut, fields):
    rows, cols = shard.shape
    ny, nz, nx = grid.ny, grid.nz, grid.nx
    dt = shard.dtype
    spans = ((0, cut), (cut, cols))

    pieces = [shard] + [grid.swap(shard, "z", k) for k in range(1, nz)]
    outs = [jax.ShapeDtypeStruct((nz, rows, hi - lo), dt) for lo, hi in spans]
    moves = []
    for k in range(nz):
        for half, (lo, hi) in enumerate(spans):
            moves.append(
                (
                    k,
                    lambda lo=lo, hi=hi: (slice(None), pl.ds(lo, hi - lo)),
                    half,
                    lambda k=k: (grid.digits()["z"] ^ k,),
                )
            )
    part_a, part_b = place(pieces, outs, moves)

    pieces_a = [part_a] + [grid.swap(part_a, "x", k) for k in range(1, nx)]
    pieces_b = [part_b] + [grid.swap(part_b, "y", k) for k in range(1, ny)]
    (part_a,) = place(
        pieces_a,
        [jax.ShapeDtypeStruct((nz, nx) + part_a.shape[1:], dt)],
        [
            (k, lambda: (slice(None),), 0, lambda k=k: (slice(None), grid.digits()["x"] ^ k))
            for k in range(nx)
        ],
    )
    (part_b,) = place(
        pieces_b,
        [jax.ShapeDtypeStruct((ny, nz) + part_b.shape[1:], dt)],
        [(k, lambda: (slice(None),), 0, lambda k=k: (grid.digits()["y"] ^ k,)) for k in range(ny)],
    )
    pieces_a = [part_a] + [grid.swap(part_a, "y", k) for k in range(1, ny)]
    pieces_b = [part_b] + [grid.swap(part_b, "x", k) for k in range(1, nx)]
    every = []
    for half, group in ((0, pieces_a), (1, pieces_b)):
        for k, piece in enumerate(group):
            every.append((half, k, 0, piece))
            every.append((half, k, 1, grid.swap(piece, "c", 1)))
    outs = [
        jax.ShapeDtypeStruct((ny, nz, nx, 2, blocks, rows, width // blocks), dt)
        for _, width, blocks in fields
    ]
    moves = []
    for p, (half, k, core, _) in enumerate(every):
        lo, hi = spans[half]
        for o, (first, width, blocks) in enumerate(fields):
            step = width // blocks
            for b in range(blocks):
                start, end = max(lo, first + b * step), min(hi, first + (b + 1) * step)
                if start >= end:
                    continue

                def src_at(start=start, end=end, lo=lo):
                    return (slice(None), slice(None), slice(None), pl.ds(start - lo, end - start))

                def dst_at(half=half, k=k, core=core, b=b, start=start, end=end, at=first + b * step):
                    d = grid.digits()
                    tail = (d["c"] ^ core, b, slice(None), pl.ds(start - at, end - start))
                    if half == 0:
                        return (d["y"] ^ k, slice(None), slice(None)) + tail
                    return (slice(None), slice(None), d["x"] ^ k) + tail

                moves.append((p, src_at, o, dst_at))
    full = place([e[3] for e in every], outs, moves)
    return [
        w.reshape(grid.n * blocks * rows, width // blocks)
        for w, (_, width, blocks) in zip(full, fields)
    ]


def fold(groups):
    k, _, _, _, rows, cols = groups[0][0][0].shape
    digits = jnp.stack([value for _, value, _ in groups]).astype(jnp.int32)
    args, in_specs, out_specs, shapes = [], [], [], []
    step = cols // 2
    moved = 0
    for i, (terms, _, n) in enumerate(groups):
        _, a, _, b, _, _ = terms[0].shape
        for j in range(n):
            for term in terms:
                args.append(term)
                in_specs.append(
                    pl.BlockSpec(
                        (1, a, 1, b, rows, step),
                        lambda s, t, ref, i=i, j=j: (s, 0, ref[i] ^ j, 0, 0, t),
                    )
                )
            out_specs.append(pl.BlockSpec((1, a, b, rows, step), lambda s, t, ref: (s, 0, 0, 0, t)))
            shapes.append(jax.ShapeDtypeStruct((k, a, b, rows, cols), bf16))
            moved += (len(terms) + 1) * 2 * k * a * b * rows * cols

    def body(ref, *refs):
        at = 0
        out = len(args)
        for terms, _, n in groups:
            for _ in range(n):
                total = refs[at][:, :, 0].astype(f32)
                for more in refs[at + 1 : at + len(terms)]:
                    total = total + more[:, :, 0].astype(f32)
                refs[out][...] = total.astype(bf16)
                at += len(terms)
                out += 1

    outs = pl.pallas_call(
        body,
        grid_spec=pltpu.PrefetchScalarGridSpec(
            num_scalar_prefetch=1, grid=(k, 2), in_specs=in_specs, out_specs=out_specs
        ),
        out_shape=tuple(shapes),
        compiler_params=pltpu.CompilerParams(vmem_limit_bytes=40 << 20),
        cost_estimate=pl.CostEstimate(flops=moved, transcendentals=0, bytes_accessed=moved),
        name="fold",
    )(digits, *args)
    result = []
    at = 0
    for _, _, n in groups:
        result.append(list(outs[at : at + n]))
        at += n
    return result


def reduce_to_owner(grid, keep_a, send_a, keep_b, send_b):
    k, half, cols = keep_a.shape
    ny, nz, nx = grid.ny, grid.nz, grid.nx
    rows = half // (ny * nz * nx)
    d = grid.digits()
    got_a, got_b = grid.swap(send_a, "c", 1), grid.swap(send_b, "c", 1)
    view = lambda a, n, b: lambda v: v.reshape(k, a, n, b, rows, cols)
    by_x, by_y = view(ny * nz, nx, 1), view(1, ny, nz * nx)
    part_a, part_b = fold(
        [
            ([by_x(keep_a), by_x(got_a)], d["x"], nx),
            ([by_y(keep_b), by_y(got_b)], d["y"], ny),
        ]
    )
    terms_a = [part_a[0]] + [grid.swap(part_a[j], "x", j) for j in range(1, nx)]
    terms_b = [part_b[0]] + [grid.swap(part_b[j], "y", j) for j in range(1, ny)]
    by_y, by_x = view(1, ny, nz), view(nz, nx, 1)
    part_a, part_b = fold(
        [
            ([by_y(v) for v in terms_a], d["y"], ny),
            ([by_x(v) for v in terms_b], d["x"], nx),
        ]
    )
    terms_a = [part_a[0]] + [grid.swap(part_a[j], "y", j) for j in range(1, ny)]
    terms_b = [part_b[0]] + [grid.swap(part_b[j], "x", j) for j in range(1, nx)]
    by_z = view(1, nz, 1)
    part_a, part_b = fold(
        [([by_z(v) for v in terms_a], d["z"], nz), ([by_z(v) for v in terms_b], d["z"], nz)]
    )
    result = []
    for part in (part_a, part_b):
        total = part[0].astype(f32)
        for j in range(1, nz):
            total = total + grid.swap(part[j], "z", j).astype(f32)
        result.append(total.reshape(k, rows, cols))
    return result


def reduce_small(grid, grad):
    d = grid.digits()
    now = grad.reshape(grid.ny, grid.nz, grid.nx, 2, grad.shape[1])
    for digit, axis in (("c", 3), ("x", 2), ("y", 0), ("z", 0)):
        mine = pick(now, axis, d[digit])
        for k in range(1, grid.sizes[digit]):
            mine = mine + grid.swap(pick(now, axis, d[digit] ^ k), digit, k)
        now = mine
    return now


def tables(node_seeds, node_weights):
    width = node_seeds.shape[1]
    uniform_pts = (node_seeds.astype(jnp.float32) + 0.5) / 1024.0
    nodes = math.sqrt(2.0) * lax.erf_inv(2.0 * uniform_pts - 1.0)
    order = jnp.arange(width).astype(jnp.float32)
    scales = jnp.where(order[:, None] == 0.0, math.sqrt(1.0 / width), math.sqrt(2.0 / width))
    basis = scales * jnp.cos(
        math.pi * (2.0 * order[None, :] + 1.0) * order[:, None] / (2.0 * width)
    )
    projection = jnp.dot(nodes, basis, precision=precise)
    weights_float = node_weights.astype(jnp.float32)
    return (projection, weights_float / jnp.sum(weights_float))


def layout(lengths):
    ends = jnp.cumsum(lengths)
    starts = ends - lengths
    places = jnp.arange(LEN, dtype=jnp.int32)
    doc_ids = jnp.sum((places[:, None] >= ends[None, :]).astype(jnp.int32), axis=1)
    owners = doc_ids[:, None] == jnp.arange(DOCS, dtype=jnp.int32)[None, :]
    begins = jnp.sum(jnp.where(owners, starts[None, :], 0), axis=1)
    return (doc_ids, (places - begins).astype(jnp.float32))


def rotary(positions):
    half_rot = ROT // 2
    freqs = 10000.0 ** (-2.0 * jnp.arange(half_rot).astype(jnp.float32) / ROT)
    angles = positions[:, None] * freqs[None, :]
    return (jnp.cos(angles), jnp.sin(angles))


TILE = 256
WIDE = 256
PER = WIDE // HD
STEPS = LEN // TILE
PAIRS = [(q, k) for q in range(STEPS) for k in range(max(0, q - 2), q + 1)]


def nn(a, b):
    return lax.dot_general(a, b, (((1,), (0,)), ((), ())), preferred_element_type=f32)


def nt(a, b):
    return lax.dot_general(a, b, (((1,), (1,)), ((), ())), preferred_element_type=f32)


def halves(v):
    high = v.astype(bf16)
    return high, (v - high.astype(f32)).astype(bf16)


def attention_body(
    rows,
    core_ref,
    hid_ref,
    hid_t_ref,
    dy_ref,
    wq_ref,
    wk_ref,
    wv_ref,
    bq_ref,
    bk_ref,
    bv_ref,
    wo_ref,
    cos_ref,
    left_ref,
    right_ref,
    proj_ref,
    proj_low_ref,
    ones_ref,
    quad_ref,
    doc_col_ref,
    doc_row_ref,
    branch_ref,
    dh_ref,
    keep_qk_ref,
    send_qk_ref,
    keep_vo_ref,
    send_vo_ref,
    sums_ref,
    mask,
    scores,
    yq,
    yk,
    fq,
    fk,
    val,
    val_h,
    fq_t,
    dnum,
    dnum_t,
    cross,
    cross_low,
    att_t,
    num,
    den,
    dfq,
    dfk_t,
    dv_t,
    dmq,
    dmk,
    dmv,
    eq,
    ek,
):
    step = pl.program_id(0)
    span = [pl.ds(r * TILE, TILE) for r in range(STEPS)]
    lane = lax.broadcasted_iota(jnp.int32, (TILE, WIDE), 1) // HD
    ones = ones_ref[...]
    proj, proj_low = proj_ref[...], proj_low_ref[...]

    @pl.when(step == 0)
    def _():
        for i, (q, k) in enumerate(PAIRS):
            here = doc_col_ref[span[q], :] == doc_row_ref[:, span[k]]
            if q == k:
                row = lax.broadcasted_iota(jnp.int32, (TILE, TILE), 0)
                col = lax.broadcasted_iota(jnp.int32, (TILE, TILE), 1)
                here = here & (row >= col)
            mask[i] = jnp.where(here, 1.0, 0.0).astype(bf16)

    for r in range(STEPS):
        hid = hid_ref[span[r], :]
        val[span[r], :] = (nn(hid, wv_ref[...]) + bv_ref[...]).astype(bf16)
        for w_ref, b_ref, y_out, f_out, scale in (
            (wq_ref, bq_ref, yq, fq, True),
            (wk_ref, bk_ref, yk, fk, False),
        ):
            raw = nn(hid, w_ref[...]) + b_ref[...]
            y = (
                raw * cos_ref[span[r], :]
                + pltpu.roll(raw, WIDE - 8, 1) * left_ref[span[r], :]
                + pltpu.roll(raw, 8, 1) * right_ref[span[r], :]
            )
            y_high, y_low = halves(y)
            s_high, s_low = halves(y * y)
            power = nt(y_high, proj) + nt(y_low, proj) + nt(y_high, proj_low)
            power = power - 0.5 * (nn(s_high, ones) + nn(s_low, ones))
            feat = jnp.exp(power)
            if scale:
                feat = feat * quad_ref[...]
            y_out[span[r], :] = y
            f_out[span[r], :] = feat.astype(bf16)
            (eq if scale else ek)[span[r], :] = feat
            if scale:
                fq_t[:, span[r]] = feat.T.astype(bf16)

    def forward(h, carry):
        own = lane == h
        for r in range(STEPS):
            val_h[h, span[r], :] = jnp.where(own, val[span[r], :], jnp.ones((), bf16))
        total = None
        for i, (q, k) in enumerate(PAIRS):
            query = jnp.where(own, fq[span[q], :], jnp.zeros((), bf16))
            tile = nt(query, fk[span[k], :]).astype(bf16) * mask[i]
            scores[h * len(PAIRS) + i] = tile
            part = nn(tile, val_h[h, span[k], :])
            total = part if total is None else total + part
            if k == q:
                num[span[q], :] = jnp.where(own, total, num[span[q], :])
                den[span[q], :] = jnp.where(own, pltpu.roll(total, HD, 1), den[span[q], :])
                total = None
        return carry

    lax.fori_loop(0, PER, forward, 0)

    for r in range(STEPS):
        grad = nt(dy_ref[span[r], :], wo_ref[...])
        inv = 1.0 / den[span[r], :]
        att = num[span[r], :] * inv
        att_low = att.astype(bf16)
        more = nn(att_low, wo_ref[...])

        @pl.when(step == 0)
        def _():
            branch_ref[span[r], :] = more

        @pl.when(step > 0)
        def _():
            branch_ref[span[r], :] = branch_ref[span[r], :] + more

        d_num = grad * inv
        dnum[span[r], :] = d_num.astype(bf16)
        dnum_t[:, span[r]] = d_num.T.astype(bf16)
        att_t[:, span[r]] = att.T.astype(bf16)
        high, low = halves(pltpu.roll(-d_num * att, HD, 1))
        cross[span[r], :] = high
        cross_low[span[r], :] = pltpu.roll(low.astype(f32), HD, 1).astype(bf16)

    def backward(h, carry):
        own = lane == h
        after = lane == lax.rem(h + 1, PER)
        later = lane == lax.rem(h + 2, PER)
        mine = pl.ds(pl.multiple_of(h * HD, HD), HD)
        dfk_t[mine, :] = jnp.zeros((HD, LEN), f32)
        dv_t[mine, :] = jnp.zeros((HD, LEN), f32)
        total = None
        for i, (q, k) in enumerate(PAIRS):
            left = jnp.where(
                own,
                dnum[span[q], :],
                jnp.where(
                    after,
                    cross[span[q], :],
                    jnp.where(later, cross_low[span[q], :], jnp.zeros((), bf16)),
                ),
            )
            tile = nt(left, val_h[h, span[k], :]).astype(bf16) * mask[i]
            part = nn(tile, fk[span[k], :])
            total = part if total is None else total + part
            dfk_t[mine, span[k]] += nn(fq_t[mine, span[q]], tile)
            dv_t[mine, span[k]] += nn(dnum_t[mine, span[q]], scores[h * len(PAIRS) + i])
            if k == q:
                dfq[span[q], :] = jnp.where(own, total, dfq[span[q], :])
                total = None
        return carry

    lax.fori_loop(0, PER, backward, 0)

    sums = [jnp.zeros((1, WIDE), f32)] * 3
    for r in range(STEPS):
        grads = []
        for d_feat, feat, y in (
            (dfq[span[r], :], eq, yq),
            (dfk_t[:, span[r]].T, ek, yk),
        ):
            e_high, e_low = halves(d_feat * feat[span[r], :])
            d_y = nn(e_high, proj) + nn(e_low, proj) + nn(e_high, proj_low)
            d_y = d_y - (nn(e_high, ones) + nn(e_low, ones)) * y[span[r], :]
            grads.append(
                d_y * cos_ref[span[r], :]
                - pltpu.roll(d_y, WIDE - 8, 1) * left_ref[span[r], :]
                - pltpu.roll(d_y, 8, 1) * right_ref[span[r], :]
            )
        grads.append(dv_t[:, span[r]].T)
        lows = [g.astype(bf16) for g in grads]
        for i, out in enumerate((dmq, dmk, dmv)):
            out[span[r], :] = lows[i]
            sums[i] = sums[i] + jnp.sum(lows[i].astype(f32), axis=0, keepdims=True)
        more = nt(lows[0], wq_ref[...]) + nt(lows[1], wk_ref[...]) + nt(lows[2], wv_ref[...])

        @pl.when(step == 0)
        def _():
            dh_ref[span[r], :] = more

        @pl.when(step > 0)
        def _():
            dh_ref[span[r], :] = dh_ref[span[r], :] + more

    for i in range(3):
        sums_ref[pl.ds(i, 1), :] = sums[i]

    for r in range(STEPS):
        rows_of = hid_t_ref[span[r], :]
        keep = r < STEPS // 2
        at = pl.ds((r % (STEPS // 2)) * TILE, TILE)
        qk, vo = (keep_qk_ref, keep_vo_ref) if keep else (send_qk_ref, send_vo_ref)
        qk[0, at, :] = nn(rows_of, dmq[...]).astype(bf16)
        qk[1, at, :] = nn(rows_of, dmk[...]).astype(bf16)
        vo[0, at, pl.ds(pl.multiple_of(step * WIDE, WIDE), WIDE)] = nn(rows_of, dmv[...]).astype(bf16)
    first = core_ref[0] == 0
    for p in range(WIDE // (2 * rows)):
        pair = nn(att_t[pl.ds(p * 2 * rows, 2 * rows), :], dy_ref[...]).astype(bf16)
        even, odd = pair[:rows], pair[rows:]
        at = pl.ds(pl.multiple_of(step * (WIDE // 2), WIDE // 2) + p * rows, rows)
        keep_vo_ref[1, at, :] = jnp.where(first, even, odd)
        send_vo_ref[1, at, :] = jnp.where(first, odd, even)


def attention(core, rows, hid, hid_t, dy, wqk, wv, bqkv, wo, cos_t, left_t, right_t, proj, proj_low, ones, quad, doc_col, doc_row):
    groups = wo.shape[0] // WIDE
    whole = lambda shape: pl.BlockSpec(shape, lambda g: (0, 0), pipeline_mode=pl.Buffered(1))
    col = lambda shift: pl.BlockSpec((D, WIDE), lambda g: (0, g + shift * groups))
    bias = lambda shift: pl.BlockSpec((1, WIDE), lambda g: (0, g + shift * groups))
    half = D // 2
    all_three = pl.BlockSpec((2, half, D), lambda g: (0, 0, 0), pipeline_mode=pl.Buffered(1))
    in_specs = [
        pl.BlockSpec(memory_space=pltpu.SMEM),
        whole((LEN, D)),
        whole((D, LEN)),
        whole((LEN, D)),
        col(0),
        col(1),
        col(0),
        bias(0),
        bias(1),
        bias(2),
        pl.BlockSpec((WIDE, D), lambda g: (g, 0)),
        whole((LEN, WIDE)),
        whole((LEN, WIDE)),
        whole((LEN, WIDE)),
        whole((WIDE, WIDE)),
        whole((WIDE, WIDE)),
        whole((WIDE, WIDE)),
        whole((1, WIDE)),
        whole((LEN, 1)),
        whole((1, LEN)),
    ]
    span = groups * WIDE
    shapes = [
        ((LEN, D), f32, whole((LEN, D))),
        ((LEN, D), f32, whole((LEN, D))),
        ((2, half, span), bf16, pl.BlockSpec((2, half, WIDE), lambda g: (0, 0, g))),
        ((2, half, span), bf16, pl.BlockSpec((2, half, WIDE), lambda g: (0, 0, g))),
        ((2, half, D), bf16, all_three),
        ((2, half, D), bf16, all_three),
        ((8, span), f32, pl.BlockSpec((8, WIDE), lambda g: (0, g))),
    ]
    vm = lambda shape, dt: pltpu.VMEM(shape, dt)
    scratch = [
        vm((len(PAIRS), TILE, TILE), bf16),
        vm((PER * len(PAIRS), TILE, TILE), bf16),
        vm((LEN, WIDE), f32),
        vm((LEN, WIDE), f32),
        vm((LEN, WIDE), bf16),
        vm((LEN, WIDE), bf16),
        vm((LEN, WIDE), bf16),
        vm((PER, LEN, WIDE), bf16),
        vm((WIDE, LEN), bf16),
        vm((LEN, WIDE), bf16),
        vm((WIDE, LEN), bf16),
        vm((LEN, WIDE), bf16),
        vm((LEN, WIDE), bf16),
        vm((WIDE, LEN), bf16),
        vm((LEN, WIDE), f32),
        vm((LEN, WIDE), f32),
        vm((LEN, WIDE), f32),
        vm((WIDE, LEN), f32),
        vm((WIDE, LEN), f32),
        vm((LEN, WIDE), bf16),
        vm((LEN, WIDE), bf16),
        vm((LEN, WIDE), bf16),
        vm((LEN, WIDE), f32),
        vm((LEN, WIDE), f32),
    ]
    return pl.pallas_call(
        functools.partial(attention_body, rows),
        grid=(groups,),
        out_shape=tuple(jax.ShapeDtypeStruct(s, t) for s, t, _ in shapes),
        in_specs=in_specs,
        out_specs=tuple(spec for _, _, spec in shapes),
        scratch_shapes=scratch,
        compiler_params=pltpu.CompilerParams(vmem_limit_bytes=56 << 20),
        cost_estimate=pl.CostEstimate(
            flops=groups * 20 * (1 << 30), transcendentals=0, bytes_accessed=30 << 20
        ),
        name="attention",
    )(core, hid, hid_t, dy, wqk, wqk, wv, bqkv, bqkv, bqkv, wo, cos_t, left_t, right_t, proj, proj_low, ones, quad, doc_col, doc_row)


def mlp_body(
    rows,
    wide,
    core_ref,
    hid_ref,
    hid_t_ref,
    dy_ref,
    w1_ref,
    b1_ref,
    w2_ref,
    out_ref,
    dh_ref,
    keep_1_ref,
    send_1_ref,
    keep_2_ref,
    send_2_ref,
    sums_ref,
    act_t,
    dup,
):
    step = pl.program_id(0)
    block = w2_ref.shape[0]
    tile = 256
    total = jnp.zeros((1, block), f32)
    for r in range(LEN // tile):
        at = pl.ds(r * tile, tile)
        upper = nn(hid_ref[at, :], w1_ref[...]) + b1_ref[...]
        bell = jnp.exp(-0.5 * upper * upper)
        phi = 0.5 + 0.5 * lax.erf(upper * (1.0 / math.sqrt(2.0)))
        act = upper * phi
        act_low = act.astype(bf16)
        act_t[:, at] = act.T.astype(bf16)
        slope = phi + upper * bell * (1.0 / math.sqrt(2.0 * math.pi))
        d_up = (nt(dy_ref[at, :], w2_ref[...]) * slope).astype(bf16)
        dup[at, :] = d_up
        total = total + jnp.sum(d_up.astype(f32), axis=0, keepdims=True)
        more = nn(act_low, w2_ref[...])
        back = nt(d_up, w1_ref[...])

        @pl.when(step == 0)
        def _():
            out_ref[at, :] = more
            dh_ref[at, :] = back

        @pl.when(step > 0)
        def _():
            out_ref[at, :] = out_ref[at, :] + more
            dh_ref[at, :] = dh_ref[at, :] + back

    sums_ref[...] = total
    for r in range(D // tile):
        res = nn(hid_t_ref[pl.ds(r * tile, tile), :], dup[...]).astype(bf16)
        half = D // tile // 2
        out = keep_1_ref if r < half else send_1_ref
        out[0, pl.ds((r % half) * tile, tile), :] = res
    first = core_ref[0] == 0
    for p in range(block // (2 * wide)):
        pair = nn(act_t[pl.ds(p * 2 * wide, 2 * wide), :], dy_ref[...]).astype(bf16)
        for b in range(wide // rows):
            even = pair[b * rows : (b + 1) * rows]
            odd = pair[wide + b * rows : wide + (b + 1) * rows]
            keep_2_ref[b, pl.ds(p * rows, rows), :] = jnp.where(first, even, odd)
            send_2_ref[b, pl.ds(p * rows, rows), :] = jnp.where(first, odd, even)


def mlp(core, rows, wide, block, hid, hid_t, dy, w1, b1, w2):
    units = w2.shape[0]
    grid = units // block
    whole = lambda shape: pl.BlockSpec(shape, lambda g: (0, 0), pipeline_mode=pl.Buffered(1))
    half = D // 2
    pairs = block // (2 * wide)
    folds = wide // rows
    per = D // block
    fold_1 = pl.BlockSpec((1, half, block), lambda g: (g // per, 0, g % per))
    shapes = [
        ((LEN, D), f32, whole((LEN, D))),
        ((LEN, D), f32, whole((LEN, D))),
        ((units // D, half, D), bf16, fold_1),
        ((units // D, half, D), bf16, fold_1),
        ((folds, grid * pairs * rows, D), bf16, pl.BlockSpec((folds, pairs * rows, D), lambda g: (0, g, 0))),
        ((folds, grid * pairs * rows, D), bf16, pl.BlockSpec((folds, pairs * rows, D), lambda g: (0, g, 0))),
        ((1, units), f32, pl.BlockSpec((1, block), lambda g: (0, g))),
    ]
    return pl.pallas_call(
        functools.partial(mlp_body, rows, wide),
        grid=(grid,),
        out_shape=tuple(jax.ShapeDtypeStruct(s, t) for s, t, _ in shapes),
        in_specs=[
            pl.BlockSpec(memory_space=pltpu.SMEM),
            whole((LEN, D)),
            whole((D, LEN)),
            whole((LEN, D)),
            pl.BlockSpec((D, block), lambda g: (0, g)),
            pl.BlockSpec((1, block), lambda g: (0, g)),
            pl.BlockSpec((block, D), lambda g: (g, 0)),
        ],
        out_specs=tuple(spec for _, _, spec in shapes),
        scratch_shapes=[pltpu.VMEM((block, LEN), bf16), pltpu.VMEM((LEN, block), bf16)],
        compiler_params=pltpu.CompilerParams(vmem_limit_bytes=48 << 20),
        cost_estimate=pl.CostEstimate(
            flops=6 * 2 * LEN * D * units, transcendentals=0, bytes_accessed=30 << 20
        ),
        name="mlp",
    )(core, hid, hid_t, dy, w1, b1, w2)


def rest_rows(value, rows, core):
    blocks = value.reshape(-1, 2, rows, value.shape[-1])
    return jnp.concatenate(
        [pick(blocks, 1, core).reshape(-1, value.shape[-1]), pick(blocks, 1, 1 - core).reshape(-1, value.shape[-1])]
    )


def pick(value, axis, index):
    return lax.dynamic_index_in_dim(value, index, axis, keepdims=False)


def alternate(keep, send, rows):
    both = jnp.stack([keep.reshape(-1, rows, keep.shape[-1]), send.reshape(-1, rows, keep.shape[-1])], axis=1)
    return both.reshape(-1, keep.shape[-1])


def shards(
    grid,
    tokens,
    ln_gain,
    ln_bias,
    qkv_weight,
    qkv_bias,
    out_weight,
    out_bias,
    fc1_weight,
    fc1_bias,
    fc2_weight,
    fc2_bias,
    cotangent,
    doc_lengths,
    node_seeds,
    node_weights,
):
    n = grid.n
    rows = qkv_weight.shape[0]
    staged = rows % 32 == 0
    parts = PARTS if staged else 1
    vectors = (ln_gain, ln_bias, qkv_bias, out_bias, fc1_bias, fc2_bias)
    small = jnp.concatenate(vectors)
    per_row = small.shape[0] // rows
    small = jnp.pad(small.reshape(rows, per_row), ((0, 0), (0, 128 - per_row)))
    units = FF // parts
    wide = units // n if staged else 64
    folds = wide // 32
    if staged:
        first = jnp.concatenate(
            [qkv_weight[:, : 2 * D], small, qkv_weight[:, 2 * D :], out_weight], axis=1
        )
        qk_weight, small_all, v_weight, attn_weight = gather(
            grid,
            first,
            2 * D + 128,
            ((0, 2 * D, 1), (2 * D, 128, 1), (2 * D + 128, D, 1), (3 * D + 128, D, 1)),
        )
        up_weights, down_weights = [], []
        split = fc1_weight.reshape(rows, n, parts, wide)
        for m in range(parts):
            folded = fc2_weight[m * wide : (m + 1) * wide].reshape(folds, rows, D)
            packed = jnp.concatenate(
                [split[:, :, m].reshape(rows, units)] + [folded[i] for i in range(folds)], axis=1
            )
            if m == 0:
                packed, qk_weight = lax.optimization_barrier((packed, qk_weight))
            up, down = gather(grid, packed, units, ((0, units, 1), (units, folds * D, folds)))
            up_weights.append(up)
            down_weights.append(down)
    else:
        joint_weight, small_all, attn_weight, up, down = [
            lax.all_gather(w, AXES, axis=0, tiled=True)
            for w in (qkv_weight, small, out_weight, fc1_weight, fc2_weight)
        ]
        qk_weight, v_weight = joint_weight[:, : 2 * D], joint_weight[:, 2 * D :]
        up_weights, down_weights = [up], [down]
    small_all = small_all[:, :per_row].reshape(n, rows * per_row)
    whole = []
    at = 0
    for v in vectors:
        whole.append(small_all[:, at : at + v.shape[0]].reshape(n * v.shape[0]).astype(f32))
        at += v.shape[0]
    norm_gain, norm_shift, joint_bias, attn_bias, up_bias, down_bias = whole

    core = grid.digits()["c"] if staged else jnp.zeros((), jnp.int32)
    core_arg = core.reshape(1).astype(jnp.int32)
    block_rows = rows if staged else 32
    rows_x = tokens.astype(f32)
    center = rows_x - jnp.mean(rows_x, axis=-1, keepdims=True)
    inv_std = lax.rsqrt(jnp.mean(center * center, axis=-1, keepdims=True) + epsilon)
    normed = center * inv_std
    hidden_low = (normed * norm_gain + norm_shift).astype(bf16)
    hidden_t = rest_rows(hidden_low.T, block_rows, core)
    dy_low = cotangent.astype(bf16)
    dy_sums = jnp.sum(dy_low.astype(f32), axis=0)

    projection, quad = tables(node_seeds, node_weights)
    doc_ids, positions = layout(doc_lengths[0])
    cos, sin = rotary(positions)
    flat = jnp.ones((LEN, HD - ROT), f32)
    none = jnp.zeros((LEN, ROT // 2), f32)
    cos_t = feature_scale * jnp.tile(jnp.concatenate([cos, cos, flat], axis=1), (1, PER))
    left_t = feature_scale * jnp.tile(jnp.concatenate([-sin, none, 0 * flat], axis=1), (1, PER))
    right_t = feature_scale * jnp.tile(jnp.concatenate([none, sin, 0 * flat], axis=1), (1, PER))
    eye = jnp.eye(PER, dtype=f32)
    wide_proj = jnp.einsum("ab,jd->ajbd", eye, projection, precision=precise).reshape(WIDE, WIDE)
    near = lax.reduce_precision(wide_proj, 8, 7)
    ones = jnp.kron(eye, jnp.ones((HD, HD), f32)).astype(bf16)

    branch, d_hidden, keep_qk, send_qk, keep_vo, send_vo, joint_sums = attention(
        core_arg,
        block_rows,
        hidden_low,
        hidden_t,
        dy_low,
        qk_weight,
        v_weight,
        joint_bias[None],
        attn_weight,
        cos_t,
        left_t,
        right_t,
        near.astype(bf16),
        (wide_proj - near).astype(bf16),
        ones,
        jnp.tile(quad, PER)[None],
        doc_ids[:, None],
        doc_ids[None],
    )
    split_bias = up_bias.reshape(-1, parts, wide)
    branches, backs, up_sums, mlp_grads = [branch], [d_hidden], [], []
    for m in range(parts):
        more, back, keep_1, send_1, keep_2, send_2, sums = mlp(
            core_arg,
            block_rows,
            wide,
            BLOCK,
            hidden_low,
            hidden_t,
            dy_low,
            up_weights[m],
            split_bias[:, m].reshape(1, units),
            down_weights[m],
        )
        branches.append(more)
        backs.append(back)
        up_sums.append(sums.reshape(-1, 1, wide))
        mlp_grads.append((keep_1, send_1, keep_2, send_2))
    output = rows_x + (attn_bias + down_bias)
    for more in branches:
        output = output + more
    d_hidden = backs[0]
    for back in backs[1:]:
        d_hidden = d_hidden + back

    g_up_bias = jnp.concatenate(up_sums, axis=1).reshape(FF)
    g_joint_bias = joint_sums[:3].reshape(3 * D)
    g_norm_gain = jnp.sum(d_hidden * normed, axis=0)
    g_norm_shift = jnp.sum(d_hidden, axis=0)
    d_normed = d_hidden * norm_gain
    mean_grad = jnp.mean(d_normed, axis=-1, keepdims=True)
    mean_cross = jnp.mean(d_normed * normed, axis=-1, keepdims=True)
    input_grad = cotangent + inv_std * (d_normed - mean_grad - normed * mean_cross)

    grads = (g_norm_gain, g_norm_shift, g_joint_bias, dy_sums, g_up_bias)
    packed = jnp.concatenate([g.reshape(n, -1) for g in grads], axis=1)
    if staged:
        s_qk, s_vo = reduce_to_owner(grid, keep_qk, send_qk, keep_vo, send_vo)
        s_joint = jnp.concatenate([s_qk[0], s_qk[1], s_vo[0]], axis=1)
        s_attn = s_vo[1]
        ups, downs = [], []
        for mine in mlp_grads:
            s_1, s_2 = reduce_to_owner(grid, *mine)
            ups.append(s_1.transpose(1, 0, 2).reshape(rows, n, 1, wide))
            downs.append(s_2.reshape(wide, D))
        s_up = jnp.concatenate(ups, axis=2).reshape(rows, FF)
        s_down = jnp.concatenate(downs, axis=0)
        s_small = reduce_small(grid, packed)
    else:
        flat_of = lambda v: v.transpose(1, 0, 2).reshape(v.shape[1], -1)
        keep_1, send_1, keep_2, send_2 = mlp_grads[0]
        both = (
            alternate(
                jnp.concatenate([flat_of(keep_qk), keep_vo[0]], axis=1),
                jnp.concatenate([flat_of(send_qk), send_vo[0]], axis=1),
                block_rows,
            ),
            alternate(keep_vo[1], send_vo[1], block_rows),
            alternate(flat_of(keep_1), flat_of(send_1), block_rows),
            alternate(*(v.reshape(folds, -1, 32, D).transpose(1, 0, 2, 3).reshape(-1, D) for v in (keep_2, send_2)), wide),
        )
        s_joint, s_attn, s_up, s_down = [
            lax.psum_scatter(g.astype(f32), AXES, scatter_dimension=0, tiled=True) for g in both
        ]
        s_small = lax.psum_scatter(packed, AXES, scatter_dimension=0, tiled=True)[0]
    small_outs = []
    at = 0
    for g in grads:
        small_outs.append(s_small[at : at + g.shape[0] // n])
        at += g.shape[0] // n
    s_gain, s_shift, s_joint_bias, s_dy, s_up_bias = small_outs
    return (
        output,
        input_grad,
        s_gain,
        s_shift,
        s_joint,
        s_joint_bias,
        s_attn,
        s_dy,
        s_up,
        s_up_bias,
        s_down,
        s_dy,
    )


def solution(mesh):
    grid = Grid(mesh.shape["dp"], mesh.shape["fsdp"])
    rows2, rows1 = P(AXES, None), P(AXES)
    in_specs = (
        rows2,
        rows1,
        rows1,
        rows2,
        rows1,
        rows2,
        rows1,
        rows2,
        rows1,
        rows2,
        rows1,
        rows2,
        rows2,
        P(),
        P(),
    )
    out_specs = (
        rows2,
        rows2,
        rows1,
        rows1,
        rows2,
        rows1,
        rows2,
        rows1,
        rows2,
        rows1,
        rows2,
        rows1,
    )
    return jax.shard_map(
        functools.partial(shards, grid),
        mesh=mesh,
        in_specs=in_specs,
        out_specs=out_specs,
        check_vma=False,
    )
```

time: 1780 us -> 614 us (0.34)
  Pallas kernels: 1070 us -> 257 us
  matrix products: 333 us -> 0.41 us
  waiting for transfers between devices: 129 us -> 109 us
    pallas_call x8 -> x12, Pallas kernels: 1070 us -> 17.4 us  [place(): pl.pallas_call(body, out_shape=tuple(outs), in_specs=[pl.BlockSpec(memory...]
    dot_general x28 -> x0, matrix products: 333 us -> none  [the longest x4 76.6 us: plain_dot(): return jnp.dot(left, right, preferred_element_type=jnp.float32)]
    pallas_call x0 -> x12, Pallas kernels: none -> 239 us  [the longest x1 124 us: attention(): pl.pallas_call(functools.partial(attention_body, rows), grid=(groups,), o...]
    unnamed x188 -> x129, local copies, waits for them, and re-layouts: 11.9 us -> 50.9 us
    dynamic_slice x12 -> x4, local copies, waits for them, and re-layouts: 34.8 us -> 1.88 us  [pick(): return lax.dynamic_index_in_dim(value, index, axis, keepdims=False)]
    slice x19 -> x6, local copies, waits for them, and re-layouts: 37.7 us -> 7.08 us  [the longest x1 3.65 us: shards(): split[:, :, m].reshape(rows, units)]
    ppermute x52 -> x75, waiting for transfers between devices: 129 us -> 109 us  [swap(): return lax.ppermute(value, AXES, pairs)]
    ppermute x52 -> x75, starting transfers between devices: 99 us -> 92.2 us  [swap(): return lax.ppermute(value, AXES, pairs)]
  transfers between devices with their start and end apart: 52 -> 75, of which waited for: 17 -> 21; matrix products, arithmetic and copies ran while one was open for 11% -> 15% of each run, Pallas kernels for 28% -> 42%
where the time goes in v2:
time: 614 us; the launch traced here: 608 us
  Pallas kernels  257 us (42%)
  waiting for transfers between devices  109 us (18%)
  local copies, waits for them, and re-layouts  99.2 us (16%)
  starting transfers between devices  92.2 us (15%)
  other arithmetic  48.3 us (8%)
    pallas_call x1, Pallas kernels, attention(): pl.pallas_call(functools.partial(attention_body, rows), grid=(groups,), o...  124 us
    ppermute x75, waiting for transfers between devices, swap(): return lax.ppermute(value, AXES, pairs)  109 us
    ppermute x75, starting transfers between devices, swap(): return lax.ppermute(value, AXES, pairs)  92.2 us
    pallas_call x2, Pallas kernels, mlp(): pl.pallas_call(functools.partial(mlp_body, rows, wide), grid=(grid,), out...  80.9 us
    unnamed x129, local copies, waits for them, and re-layouts  50.9 us
    pallas_call x9, Pallas kernels, fold(): pl.pallas_call(body, grid_spec=pltpu.PrefetchScalarGridSpec(num_scalar_pr...  34 us
    pallas_call x12, Pallas kernels, place(): pl.pallas_call(body, out_shape=tuple(outs), in_specs=[pl.BlockSpec(memory...  17.4 us
  transfers between devices with their start and end apart: 75, of which 21 were waited for; matrix products, arithmetic and copies ran while one was open for 15% of the time, Pallas kernels for 42%

profile of v2, /device:TPU:0, one launch (start us, length us, event | category | flops | bytes accessed | tf_op | source)
XLA Modules:
  0.0 607.8 jit_solution(3242028513312016175)
XLA Ops:
  2.4 4.1 concatenate.50
  37.7 6.8 %collective-permute-done.7.refs_1_ = bf16[4,32,2048]{2,1,0:T(8,128)(2,1)S(1)} collective-permute-done((bf16[4,32,2048]{2,1,0:T(8,128)(2,1)S(1)}, bf16[4,32,2048]{2,1,0:T(8,128)(2,1)S(1)}, u32[]{:S(2)}, u32[]{:S(2)}) %collective-permute-start.7) | collective-permute-done | bytes 524320 | tf_op jit(solution)/shard_map/ppermute | solution.py:52
  60.4 11.3 %collective-permute-done.9.refs_6_ = bf16[2,4,32,2048]{3,2,1,0:T(8,128)(2,1)} collective-permute-done((bf16[2,4,32,2048]{3,2,1,0:T(8,128)(2,1)S(1)}, bf16[2,4,32,2048]{3,2,1,0:T(8,128)(2,1)}, u32[]{:S(2)}, u32[]{:S(2)}) %collective-permute-start.9) | collective-permute-done | bytes 1048608 | tf_op jit(solution)/shard_map/ppermute | solution.py:52
  89.2 4.0 convert_reduce_fusion.1
  99.0 8.4 %collective-permute-done.29.refs_1_ = bf16[4,32,2048]{2,1,0:T(8,128)(2,1)} collective-permute-done((bf16[4,32,2048]{2,1,0:T(8,128)(2,1)}, bf16[4,32,2048]{2,1,0:T(8,128)(2,1)}, u32[]{:S(2)}, u32[]{:S(2)}) %collective-permute-start.29) | collective-permute-done | bytes 524320 | tf_op jit(solution)/shard_map/ppermute | solution.py:52
  120.8 11.5 %collective-permute-start.11 = (bf16[32,4096]{1,0:T(8,128)(2,1)S(1)}, bf16[32,4096]{1,0:T(8,128)(2,1)S(1)}, u32[]{:S(2)}, u32[]{:S(2)}) collective-permute-start(bf16[32,4096]{1,0:T(8,128)(2,1)S(1)} %pad_maximum_fusion.4.refs_0_), channel_id=1, source_target_pairs={{0,4},{1,5},{2,6},{3,7},{4,0},{5,1},{6,2},{7,3},{8,12},{9,13},{10,... | collective-permute-start | bytes 786440 | tf_op jit(solution)/shard_map/ppermute | solution.py:52
  143.5 3.9 copy.72
  151.4 124.4 %attention.1 = (f32[1024,1024]{1,0:T(8,128)}, f32[1024,1024]{1,0:T(8,128)}, bf16[2,512,1024]{2,1,0:T(8,128)(2,1)}, bf16[2,512,1024]{2,1,0:T(8,128)(2,1)}, bf16[2...) custom-call(s32[1]{0:T(128)} %bitcast.1.core_ref, bf16[1024,1024]{1,0:T(8,128)(2,1)} %fusion.7.hid_ref, ...), custom_call_target="tpu_custom_call" | custom-call | flops 85899345920 | bytes 31457280 | tf_op jit(solution)/shard_map/attention/pallas_call | solution.py:603
  283.5 12.8 %collective-permute-done.18.refs_1_ = bf16[4,32,2048]{2,1,0:T(8,128)(2,1)S(1)} collective-permute-done((bf16[4,32,2048]{2,1,0:T(8,128)(2,1)S(1)}, bf16[4,32,2048]{2,1,0:T(8,128)(2,1)S(1)}, u32[]{:S(2)}, u32[]{:S(2)}) %collective-permute-start.18) | collective-permute-done | bytes 524320 | tf_op jit(solution)/shard_map/ppermute | solution.py:52
  313.3 12.7 %collective-permute-done.20.refs_6_ = bf16[2,4,32,2048]{3,2,1,0:T(8,128)(2,1)} collective-permute-done((bf16[2,4,32,2048]{3,2,1,0:T(8,128)(2,1)}, bf16[2,4,32,2048]{3,2,1,0:T(8,128)(2,1)}, u32[]{:S(2)}, u32[]{:S(2)}) %collective-permute-start.20) | collective-permute-done | bytes 1048608 | tf_op jit(solution)/shard_map/ppermute | solution.py:52
  329.1 40.3 %mlp.3 = (f32[1024,1024]{1,0:T(8,128)}, f32[1024,1024]{1,0:T(8,128)}, bf16[2,512,1024]{2,1,0:T(8,128)(2,1)S(1)}, bf16[2,512,1024]{2,1,0:T(8,128)(2,1)S(1)}, bf16...) custom-call(s32[1]{0:T(128)} %bitcast.1.core_ref, ...), custom_call_target="tpu_custom_call" | custom-call | flops 25769803776 | bytes 31457280 | tf_op jit(solution)/shard_map/mlp/pallas_call | solution.py:701
  376.9 5.1 fold.9
  394.8 40.6 %mlp.2 = (f32[1024,1024]{1,0:T(8,128)}, f32[1024,1024]{1,0:T(8,128)}, bf16[2,512,1024]{2,1,0:T(8,128)(2,1)S(1)}, bf16[2,512,1024]{2,1,0:T(8,128)(2,1)S(1)}, bf16...) custom-call(s32[1]{0:T(128)} %bitcast.1.core_ref, ...), custom_call_target="tpu_custom_call" | custom-call | flops 25769803776 | bytes 31457280 | tf_op jit(solution)/shard_map/mlp/pallas_call | solution.py:701
  437.6 7.9 %fusion.12 = (f32[1024]{0:T(1024)S(1)}, f32[1024]{0:T(1024)S(1)}, f32[1024]{0:T(1024)S(1)}, f32[1024]{0:T(1024)S(1)}, f32[1024,1024]{1,0:T(8,128)}) fusion(bf16[1024,1024]{1,0:T(8,128)(2,1)} %param.15, f32[1024]{0:T(1024)S(1)} %copy-done.55, f32[1024]{0:T(1024)S(1)} %copy-done.53, f32[1024]{0:T(1024)S(1)} %copy-done.57, f32[1024,1024]{1,0:T(8,128)} %get-tuple-element.118, ...), kind=kLoop, calls=%fused_computation.15 | loop fusion | flops 12578816 | bytes 18903040 | tf_op jit(solution)/shard_map/reduce_sum | solution.py:879
  451.1 5.4 fold.15
  462.0 22.9 %collective-permute-done.35 = f32[4,320]{1,0:T(4,128)S(1)} collective-permute-done((f32[4,320]{1,0:T(4,128)S(1)}, f32[4,320]{1,0:T(4,128)S(1)}, u32[]{:S(2)}, u32[]{:S(2)}) %collective-permute-start.35) | collective-permute-done | bytes 5152 | tf_op jit(solution)/shard_map/ppermute | solution.py:52
  490.7 4.5 fold.10
  503.6 4.1 fold.16
  511.6 9.7 %fusion.11 = (f32[1024,1024]{1,0:T(8,128)}, f32[1024,1024]{1,0:T(8,128)}) fusion(f32[1024,1024]{1,0:T(8,128)S(1)} %copy-done.50, bf16[1024,1024]{1,0:T(8,128)(2,1)S(1)} %copy-done.49, f32[1024,1024]{1,0:T(8,128)} %get-tuple-element.196, f32[1024]{0:T(1024)S(1)} %broadcast_multiply_fusion, f32[1024]{0:T(1024)S(1)} %broadcast_multiply_fusion.1, ...), kind=kLoop, calls=%fused_computation.14 | loop fusion | flops 13631488 | bytes 31481856 | tf_op jit(solution)/shard_map/add | solution.py:884
  521.3 11.1 %collective-permute-done.44 = bf16[2,4,1,32,1024]{4,3,1,0,2:T(8,128)(2,1)S(1)} collective-permute-done((bf16[2,4,1,32,1024]{4,3,1,0,2:T(8,128)(2,1)S(1)}, bf16[2,4,1,32,1024]{4,3,1,0,2:T(8,128)(2,1)S(1)}, u32[]{:S(2)}, u32[]{:S(2)}) %collective-permute-start.44) | collective-permute-done | bytes 524320 | tf_op jit(solution)/shard_map/ppermute | solution.py:52
  540.1 4.4 fold.12
  554.7 4.6 collective-permute-done.48
  559.4 3.9 collective-permute-done.49
  588.5 9.0 %collective-permute-start.69 = (bf16[2,1,1,32,1024]{4,3,2,1,0:T(8,128)(2,1)S(1)}, bf16[2,1,1,32,1024]{4,3,2,1,0:T(8,128)(2,1)S(1)}, u32[]{:S(2)}, u32[]{:S(2)}) collective-permute-start(bf16[2,1,1,32,1024]{4,3,2,1,0:T(8,128)(2,1)S(1)} %get-tuple-element.175), channel_id=1, source_target_pairs={{0,4},{1,5},{2,6},{3,7},{4,0},{5,1},{6,2},{7,3},{8,12},{9,13},{10,... | collective-permute-start | bytes 393224 | tf_op jit(solution)/shard_map/ppermute | solution.py:52
  (396 shorter events, 232.3 us)
Async XLA Ops:
  59.9 50.6 %collective-permute-start.8 = (bf16[2,4,32,2048]{3,2,1,0:T(8,128)(2,1)S(1)}, bf16[2,4,32,2048]{3,2,1,0:T(8,128)(2,1)}, u32[]{:S(2)}, u32[]{:S(2)}) collective-permute-start(bf16[2,4,32,2048]{3,2,1,0:T(8,128)(2,1)S(1)} %place.14.refs_4_), channel_id=1, source_target_pairs={{0,1},{1,0},{2,3},{3,2},{4,5},{5,4},{6,7},{7,6},{8,9},{9,8},{10,11... | collective-permute-start | bytes 3145736 | tf_op jit(solution)/shard_map/ppermute | solution.py:52
  59.9 52.2 %collective-permute-start.4 = (bf16[4,2,32,2176]{3,2,1,0:T(8,128)(2,1)S(1)}, bf16[4,2,32,2176]{3,2,1,0:T(8,128)(2,1)}, u32[]{:S(2)}, u32[]{:S(2)}) collective-permute-start(bf16[4,2,32,2176]{3,2,1,0:T(8,128)(2,1)S(1)} %place.13.refs_0_), channel_id=1, source_target_pairs={{0,1},{1,0},{2,3},{3,2},{4,5},{5,4},{6,7},{7,6},{8,9},{9,8},{10,11... | collective-permute-start | bytes 3342344 | tf_op jit(solution)/shard_map/ppermute | solution.py:52
  71.7 40.4 %collective-permute-start.10 = (bf16[2,4,32,2048]{3,2,1,0:T(8,128)(2,1)}, bf16[2,4,32,2048]{3,2,1,0:T(8,128)(2,1)}, u32[]{:S(2)}, u32[]{:S(2)}) collective-permute-start(bf16[2,4,32,2048]{3,2,1,0:T(8,128)(2,1)} %collective-permute-done.9.refs_6_), channel_id=1, source_target_pairs={{0,1},{1,0},{2,3},{3,2},{4,5},{5,4},{6,7},{7,6},{8,9},{9,8},{10,11... | collective-permute-start | bytes 3145736 | tf_op jit(solution)/shard_map/ppermute | solution.py:52
  71.7 40.4 %collective-permute-start.6 = (bf16[4,2,32,2176]{3,2,1,0:T(8,128)(2,1)}, bf16[4,2,32,2176]{3,2,1,0:T(8,128)(2,1)}, u32[]{:S(2)}, u32[]{:S(2)}) collective-permute-start(bf16[4,2,32,2176]{3,2,1,0:T(8,128)(2,1)} %collective-permute-done.5.refs_2_), channel_id=1, source_target_pairs={{0,1},{1,0},{2,3},{3,2},{4,5},{5,4},{6,7},{7,6},{8,9},{9,8},{10,11... | collective-permute-start | bytes 3342344 | tf_op jit(solution)/shard_map/ppermute | solution.py:52
  107.3 174.5 %collective-permute-start.27 = (bf16[4,2,32,2048]{3,2,1,0:T(8,128)(2,1)S(1)}, bf16[4,2,32,2048]{3,2,1,0:T(8,128)(2,1)}, u32[]{:S(2)}, u32[]{:S(2)}) collective-permute-start(bf16[4,2,32,2048]{3,2,1,0:T(8,128)(2,1)S(1)} %place.21.refs_0_), channel_id=1, source_target_pairs={{0,16},{1,17},{2,18},{3,19},{4,20},{5,21},{6,22},{7,23},{8,24},{9,... | collective-permute-start | bytes 3145736 | tf_op jit(solution)/shard_map/ppermute | solution.py:52
  110.5 172.5 %collective-permute-start.31 = (bf16[2,4,32,2048]{3,2,1,0:T(8,128)(2,1)}, bf16[2,4,32,2048]{3,2,1,0:T(8,128)(2,1)}, u32[]{:S(2)}, u32[]{:S(2)}) collective-permute-start(bf16[2,4,32,2048]{3,2,1,0:T(8,128)(2,1)} %place.22.refs_4_), channel_id=1, source_target_pairs={{0,2},{1,3},{2,0},{3,1},{4,6},{5,7},{6,4},{7,5},{8,10},{9,11},{10,... | collective-permute-start | bytes 3145736 | tf_op jit(solution)/shard_map/ppermute | solution.py:52
  120.8 155.0 %collective-permute-start.11 = (bf16[32,4096]{1,0:T(8,128)(2,1)S(1)}, bf16[32,4096]{1,0:T(8,128)(2,1)S(1)}, u32[]{:S(2)}, u32[]{:S(2)}) collective-permute-start(bf16[32,4096]{1,0:T(8,128)(2,1)S(1)} %pad_maximum_fusion.4.refs_0_), channel_id=1, source_target_pairs={{0,4},{1,5},{2,6},{3,7},{4,0},{5,1},{6,2},{7,3},{8,12},{9,13},{10,... | collective-permute-start | bytes 786440 | tf_op jit(solution)/shard_map/ppermute | solution.py:52
  132.4 144.2 %collective-permute-start.12 = (bf16[32,4096]{1,0:T(8,128)(2,1)S(1)}, bf16[32,4096]{1,0:T(8,128)(2,1)S(1)}, u32[]{:S(2)}, u32[]{:S(2)}) collective-permute-start(bf16[32,4096]{1,0:T(8,128)(2,1)S(1)} %pad_maximum_fusion.4.refs_0_), channel_id=1, source_target_pairs={{0,8},{1,9},{2,10},{3,11},{4,12},{5,13},{6,14},{7,15},{8,0},{9,1},... | collective-permute-start | bytes 786440 | tf_op jit(solution)/shard_map/ppermute | solution.py:52
  134.3 143.5 %collective-permute-start.13 = (bf16[32,4096]{1,0:T(8,128)(2,1)S(1)}, bf16[32,4096]{1,0:T(8,128)(2,1)S(1)}, u32[]{:S(2)}, u32[]{:S(2)}) collective-permute-start(bf16[32,4096]{1,0:T(8,128)(2,1)S(1)} %pad_maximum_fusion.4.refs_0_), channel_id=1, source_target_pairs={{0,12},{1,13},{2,14},{3,15},{4,8},{5,9},{6,10},{7,11},{8,4},{9,5},... | collective-permute-start | bytes 786440 | tf_op jit(solution)/shard_map/ppermute | solution.py:52
  278.5 48.8 %collective-permute-start.39 = (bf16[2,512,1024]{2,1,0:T(8,128)(2,1)}, bf16[2,512,1024]{2,1,0:T(8,128)(2,1)S(1)}, u32[]{:S(2)}, u32[]{:S(2)}) collective-permute-start(bf16[2,512,1024]{2,1,0:T(8,128)(2,1)} %get-tuple-element.123), channel_id=1, source_target_pairs={{0,1},{1,0},{2,3},{3,2},{4,5},{5,4},{6,7},{7,6},{8,9},{9,8},{10,11... | collective-permute-start | bytes 6291464 | tf_op jit(solution)/shard_map/ppermute | solution.py:52
  312.8 60.8 %collective-permute-start.40 = (bf16[2,512,1024]{2,1,0:T(8,128)(2,1)}, bf16[2,512,1024]{2,1,0:T(8,128)(2,1)}, u32[]{:S(2)}, u32[]{:S(2)}) collective-permute-start(bf16[2,512,1024]{2,1,0:T(8,128)(2,1)} %get-tuple-element.125), channel_id=1, source_target_pairs={{0,1},{1,0},{2,3},{3,2},{4,5},{5,4},{6,7},{7,6},{8,9},{9,8},{10,11... | collective-permute-start | bytes 6291464 | tf_op jit(solution)/shard_map/ppermute | solution.py:52
  312.8 69.2 %collective-permute-start.19 = (bf16[2,4,32,2048]{3,2,1,0:T(8,128)(2,1)}, bf16[2,4,32,2048]{3,2,1,0:T(8,128)(2,1)S(1)}, u32[]{:S(2)}, u32[]{:S(2)}) collective-permute-start(bf16[2,4,32,2048]{3,2,1,0:T(8,128)(2,1)} %place.18.refs_4_), channel_id=1, source_target_pairs={{0,1},{1,0},{2,3},{3,2},{4,5},{5,4},{6,7},{7,6},{8,9},{9,8},{10,11... | collective-permute-start | bytes 3145736 | tf_op jit(solution)/shard_map/ppermute | solution.py:52
  326.1 57.4 %collective-permute-start.15 = (bf16[4,2,32,2048]{3,2,1,0:T(8,128)(2,1)}, bf16[4,2,32,2048]{3,2,1,0:T(8,128)(2,1)}, u32[]{:S(2)}, u32[]{:S(2)}) collective-permute-start(bf16[4,2,32,2048]{3,2,1,0:T(8,128)(2,1)} %place.17.refs_0_), channel_id=1, source_target_pairs={{0,1},{1,0},{2,3},{3,2},{4,5},{5,4},{6,7},{7,6},{8,9},{9,8},{10,11... | collective-permute-start | bytes 3145736 | tf_op jit(solution)/shard_map/ppermute | solution.py:52
  327.3 57.7 %collective-permute-start.21 = (bf16[2,4,32,2048]{3,2,1,0:T(8,128)(2,1)}, bf16[2,4,32,2048]{3,2,1,0:T(8,128)(2,1)}, u32[]{:S(2)}, u32[]{:S(2)}) collective-permute-start(bf16[2,4,32,2048]{3,2,1,0:T(8,128)(2,1)} %collective-permute-done.20.refs_6_), channel_id=1, source_target_pairs={{0,1},{1,0},{2,3},{3,2},{4,5},{5,4},{6,7},{7,6},{8,9},{9,8},{10,11... | collective-permute-start | bytes 3145736 | tf_op jit(solution)/shard_map/ppermute | solution.py:52
  328.6 57.4 %collective-permute-start.17 = (bf16[4,2,32,2048]{3,2,1,0:T(8,128)(2,1)}, bf16[4,2,32,2048]{3,2,1,0:T(8,128)(2,1)}, u32[]{:S(2)}, u32[]{:S(2)}) collective-permute-start(bf16[4,2,32,2048]{3,2,1,0:T(8,128)(2,1)} %collective-permute-done.16.refs_2_), channel_id=1, source_target_pairs={{0,1},{1,0},{2,3},{3,2},{4,5},{5,4},{6,7},{7,6},{8,9},{9,8},{10,11... | collective-permute-start | bytes 3145736 | tf_op jit(solution)/shard_map/ppermute | solution.py:52
  373.6 74.3 %collective-permute-start.60 = (bf16[2,512,1024]{2,1,0:T(8,128)(2,1)}, bf16[2,512,1024]{2,1,0:T(8,128)(2,1)}, u32[]{:S(2)}, u32[]{:S(2)}) collective-permute-start(bf16[2,512,1024]{2,1,0:T(8,128)(2,1)} %copy-done.43), channel_id=1, source_target_pairs={{0,1},{1,0},{2,3},{3,2},{4,5},{5,4},{6,7},{7,6},{8,9},{9,8},{10,11... | collective-permute-start | bytes 6291464 | tf_op jit(solution)/shard_map/ppermute | solution.py:52
  383.0 64.9 %collective-permute-start.61 = (bf16[2,512,1024]{2,1,0:T(8,128)(2,1)}, bf16[2,512,1024]{2,1,0:T(8,128)(2,1)}, u32[]{:S(2)}, u32[]{:S(2)}) collective-permute-start(bf16[2,512,1024]{2,1,0:T(8,128)(2,1)} %get-tuple-element.161), channel_id=1, source_target_pairs={{0,1},{1,0},{2,3},{3,2},{4,5},{5,4},{6,7},{7,6},{8,9},{9,8},{10,11... | collective-permute-start | bytes 6291464 | tf_op jit(solution)/shard_map/ppermute | solution.py:52
  383.5 101.4 %collective-permute-start.41 = (bf16[2,8,1,32,1024]{4,3,2,1,0:T(8,128)(2,1)}, bf16[2,8,1,32,1024]{4,3,2,1,0:T(8,128)(2,1)S(1)}, u32[]{:S(2)}, u32[]{:S(2)}) collective-permute-start(bf16[2,8,1,32,1024]{4,3,2,1,0:T(8,128)(2,1)} %get-tuple-element.127), channel_id=1, source_target_pairs={{0,2},{1,3},{2,0},{3,1},{4,6},{5,7},{6,4},{7,5},{8,10},{9,11},{10,... | collective-permute-start | bytes 3145736 | tf_op jit(solution)/shard_map/ppermute | solution.py:52
  385.0 101.4 %collective-permute-start.42 = (bf16[2,1,8,32,1024]{4,3,2,1,0:T(8,128)(2,1)}, bf16[2,1,8,32,1024]{4,3,2,1,0:T(8,128)(2,1)}, u32[]{:S(2)}, u32[]{:S(2)}) collective-permute-start(bf16[2,1,8,32,1024]{4,3,2,1,0:T(8,128)(2,1)} %get-tuple-element.129), channel_id=1, source_target_pairs={{0,16},{1,17},{2,18},{3,19},{4,20},{5,21},{6,22},{7,23},{8,24},{9,... | collective-permute-start | bytes 3145736 | tf_op jit(solution)/shard_map/ppermute | solution.py:52
  458.4 38.9 %collective-permute-start.62 = (bf16[2,8,1,32,1024]{4,3,2,1,0:T(8,128)(2,1)}, bf16[2,8,1,32,1024]{4,3,2,1,0:T(8,128)(2,1)}, u32[]{:S(2)}, u32[]{:S(2)}) collective-permute-start(bf16[2,8,1,32,1024]{4,3,2,1,0:T(8,128)(2,1)} %get-tuple-element.163), channel_id=1, source_target_pairs={{0,2},{1,3},{2,0},{3,1},{4,6},{5,7},{6,4},{7,5},{8,10},{9,11},{10,... | collective-permute-start | bytes 3145736 | tf_op jit(solution)/shard_map/ppermute | solution.py:52
  459.8 39.7 %collective-permute-start.63 = (bf16[2,1,8,32,1024]{4,3,2,1,0:T(8,128)(2,1)}, bf16[2,1,8,32,1024]{4,3,2,1,0:T(8,128)(2,1)}, u32[]{:S(2)}, u32[]{:S(2)}) collective-permute-start(bf16[2,1,8,32,1024]{4,3,2,1,0:T(8,128)(2,1)} %get-tuple-element.165), channel_id=1, source_target_pairs={{0,16},{1,17},{2,18},{3,19},{4,20},{5,21},{6,22},{7,23},{8,24},{9,... | collective-permute-start | bytes 3145736 | tf_op jit(solution)/shard_map/ppermute | solution.py:52
  484.9 50.8 %collective-permute-start.51 = (bf16[2,512,1024]{2,1,0:T(8,128)(2,1)}, bf16[2,512,1024]{2,1,0:T(8,128)(2,1)}, u32[]{:S(2)}, u32[]{:S(2)}) collective-permute-start(bf16[2,512,1024]{2,1,0:T(8,128)(2,1)} %copy-done.42), channel_id=1, source_target_pairs={{0,1},{1,0},{2,3},{3,2},{4,5},{5,4},{6,7},{7,6},{8,9},{9,8},{10,11... | collective-permute-start | bytes 6291464 | tf_op jit(solution)/shard_map/ppermute | solution.py:52
  485.9 52.7 %collective-permute-start.52 = (bf16[2,512,1024]{2,1,0:T(8,128)(2,1)}, bf16[2,512,1024]{2,1,0:T(8,128)(2,1)}, u32[]{:S(2)}, u32[]{:S(2)}) collective-permute-start(bf16[2,512,1024]{2,1,0:T(8,128)(2,1)} %get-tuple-element.145), channel_id=1, source_target_pairs={{0,1},{1,0},{2,3},{3,2},{4,5},{5,4},{6,7},{7,6},{8,9},{9,8},{10,11... | collective-permute-start | bytes 6291464 | tf_op jit(solution)/shard_map/ppermute | solution.py:52
  507.7 36.7 %collective-permute-start.64 = (bf16[2,1,4,32,1024]{4,3,2,0,1:T(8,128)(2,1)S(1)}, bf16[2,1,4,32,1024]{4,3,2,0,1:T(8,128)(2,1)S(1)}, u32[]{:S(2)}, u32[]{:S(2)}) collective-permute-start(bf16[2,1,4,32,1024]{4,3,2,0,1:T(8,128)(2,1)S(1)} %bitcast.195), channel_id=1, source_target_pairs={{0,16},{1,17},{2,18},{3,19},{4,20},{5,21},{6,22},{7,23},{8,24},{9,... | collective-permute-start | bytes 1572872 | tf_op jit(solution)/shard_map/ppermute | solution.py:52
  (114 other events, 1624.9 us)

commit v3 on v1

v3 whole, which is shorter than its diff:
```python
import functools
import math

import jax
import jax.numpy as jnp
from jax import lax
from jax.experimental import pallas as pl
from jax.experimental.pallas import tpu as pltpu
from jax.sharding import PartitionSpec as P

D = 1024
HEADS = 16
HD = 64
ROT = 16
LEN = 1024
DOCS = 4
FF = 4096
AXES = ("dp", "fsdp")
BLOCK = 512

feature_scale = 0.2
epsilon = 1e-05
precise = lax.Precision.HIGHEST
bf16 = jnp.bfloat16
f32 = jnp.float32
VMEM_LIMIT = 60 << 20


def cost(flops, transcendentals, bytes_accessed):
    return pl.CostEstimate(
        flops=flops * 4, transcendentals=transcendentals, bytes_accessed=bytes_accessed * 4
    )


class Grid:
    def __init__(self, dp, fsdp):
        self.dp, self.fsdp = dp, fsdp
        rest = fsdp // 2
        self.nx = 4 if rest % 16 == 0 else 2
        self.nz = rest // self.nx
        self.ny = dp
        self.n = dp * fsdp
        self.sizes = {"y": self.ny, "z": self.nz, "x": self.nx, "c": 2}
        self.stride = {"y": fsdp, "z": self.nx * 2, "x": 2, "c": 1}

    def digits(self):
        y = lax.axis_index("dp")
        f = lax.axis_index("fsdp")
        return {"y": y, "z": f // (self.nx * 2), "x": (f // 2) % self.nx, "c": f % 2}

    def swap(self, value, digit, k):
        stride = self.stride[digit]
        size = self.sizes[digit]
        pairs = []
        for i in range(self.n):
            d = (i // stride) % size
            pairs.append((i, i + ((d ^ k) - d) * stride))
        return lax.ppermute(value, AXES, pairs)

    def swap_by_core(self, value, digit_0, digit_1):
        flips = (self.stride[digit_0], self.stride[digit_1])
        return lax.ppermute(value, AXES, [(i, i ^ flips[i % 2]) for i in range(self.n)])


def place(pieces, outs, moves, after=()):
    n_in = len(pieces)
    n_out = len(outs)

    def body(*refs):
        ins, rest = refs[:n_in], refs[n_in + len(after) :]
        res, held, sem, done = rest[:n_out], rest[n_out : 2 * n_out], rest[-2], rest[-1]
        copies = []
        for i, (src, src_at, dst, dst_at) in enumerate(moves):
            copies.append(
                pltpu.make_async_copy(ins[src].at[src_at()], held[dst].at[dst_at()], sem.at[i])
            )
        for copy in copies:
            copy.start()
        back = []
        for o in range(n_out):
            for copy, move in zip(copies, moves):
                if move[2] == o:
                    copy.wait()
            back.append(pltpu.make_async_copy(held[o], res[o], done.at[o]))
            back[-1].start()
        for copy in back:
            copy.wait()

    total = sum(math.prod(o.shape) * o.dtype.itemsize for o in outs)
    return pl.pallas_call(
        body,
        out_shape=tuple(outs),
        in_specs=[pl.BlockSpec(memory_space=pl.ANY)] * (n_in + len(after)),
        out_specs=tuple([pl.BlockSpec(memory_space=pl.ANY)] * n_out),
        scratch_shapes=[pltpu.VMEM(o.shape, o.dtype) for o in outs]
        + [pltpu.SemaphoreType.DMA((len(moves),)), pltpu.SemaphoreType.DMA((n_out,))],
        compiler_params=pltpu.CompilerParams(vmem_limit_bytes=VMEM_LIMIT),
        cost_estimate=cost(flops=0, transcendentals=0, bytes_accessed=2 * total),
        name="place",
    )(*pieces, *after)


class Gather:
    def __init__(self, grid, both, fields, after=()):
        if after:
            both, *_ = lax.optimization_barrier((both, *after))
        self.grid, self.fields = grid, fields
        self.shape, self.dt = both.shape, both.dtype
        self.pieces = [both] + [grid.swap(both, "z", k) for k in range(1, grid.nz)]

    def first(self):
        g = self.grid
        outs = [jax.ShapeDtypeStruct((g.nz,) + self.shape, self.dt)]
        moves = [
            (k, lambda: (slice(None),), 0, lambda k=k: (g.digits()["z"] ^ k,)) for k in range(g.nz)
        ]
        return self.pieces, outs, moves, self.after_first

    def after_first(self, placed):
        self.pieces = [placed[0], self.grid.swap_by_core(placed[0], "x", "y")]

    def second(self):
        g = self.grid
        outs = [jax.ShapeDtypeStruct((2, g.nz) + self.shape, self.dt)]

        def dst_at(k):
            d = g.digits()
            return (jnp.where(d["c"] == 0, d["x"], d["y"]) ^ k,)

        moves = [(k, lambda: (slice(None),), 0, lambda k=k: dst_at(k)) for k in range(2)]
        return self.pieces, outs, moves, self.after_second

    def after_second(self, placed):
        self.pieces = [placed[0], self.grid.swap_by_core(placed[0], "y", "x")]

    def cores(self, after=()):
        pieces = tuple(self.pieces)
        if after:
            pieces = lax.optimization_barrier((*pieces, *after))[:2]
        self.pieces = list(pieces) + [self.grid.swap(piece, "c", 1) for piece in pieces]

    def third(self):
        g, rows = self.grid, self.shape[1]
        outs, moves = [], []
        first = 0
        for o, (cols, blocks) in enumerate(self.fields):
            wide = cols // blocks
            split = blocks == 1
            outs.append(
                jax.ShapeDtypeStruct(
                    (2, g.nz, 2, 2, 1 if split else 2 * blocks, rows, 2 * wide if split else wide), self.dt
                )
            )
            for p in range(4):
                for d1 in range(2):
                    for b in range(blocks):
                        start = first + b * wide

                        def src_at(d1=d1, start=start, wide=wide):
                            return (d1, slice(None), slice(None), slice(None), pl.ds(start, wide))

                        def dst_at(p=p, d1=d1, b=b, wide=wide, split=split, blocks=blocks):
                            d = g.digits()
                            half = d["c"] ^ (p // 2)
                            d2 = jnp.where(half == 0, d["y"], d["x"]) ^ (p % 2)
                            y = jnp.where(half == 0, d2, d1)
                            x = jnp.where(half == 0, d1, d2)
                            block = 0 if split else half * blocks + b
                            at = pl.ds(pl.multiple_of(half * wide, wide), wide) if split else slice(None)
                            return (y, slice(None), x, slice(None), block, slice(None), at)

                        moves.append((p, src_at, o, dst_at))
            first += cols
        return self.pieces, outs, moves, self.after_third

    def after_third(self, placed):
        self.full = [w.reshape(-1, w.shape[-1]) for w in placed]


def pack(grid, groups):
    core = grid.digits()["c"]
    halves = [[], []]
    for group in groups:
        for shard, _ in group:
            middle = shard.shape[1] // 2
            halves[0].append(shard[:, :middle])
            halves[1].append(shard[:, middle:])
    low, high = [jnp.concatenate(h, axis=1) for h in halves]
    mine, other = jnp.where(core == 0, low, high), jnp.where(core == 0, high, low)
    got = grid.swap(other, "c", 1)
    both = jnp.stack([jnp.where(core == 0, mine, got), jnp.where(core == 0, got, mine)])
    result = []
    at = 0
    for group in groups:
        cols = sum(shard.shape[1] // 2 for shard, _ in group)
        result.append((both[:, :, at : at + cols], [(s.shape[1] // 2, max(1, b // 2)) for s, b in group]))
        at += cols
    return result


def place_all(plans, after=()):
    pieces, outs, moves = [], [], []
    for p, o, m, _ in plans:
        moves += [(len(pieces) + src, src_at, len(outs) + dst, dst_at) for src, src_at, dst, dst_at in m]
        pieces += p
        outs += o
    placed = place(pieces, outs, moves, after)
    at = 0
    for _, o, _, done in plans:
        done(placed[at : at + len(o)])
        at += len(o)
    return list(placed[:1])


TILE = 256
WIDE = 256
PER = WIDE // HD
STEPS = LEN // TILE
GROUPS = HEADS // PER
PAIRS = [(q, k) for q in range(STEPS) for k in range(max(0, q - 2), q + 1)]


def nn(a, b):
    return lax.dot_general(a, b, (((1,), (0,)), ((), ())), preferred_element_type=f32)


def nt(a, b):
    return lax.dot_general(a, b, (((1,), (1,)), ((), ())), preferred_element_type=f32)


def halves(v):
    high = v.astype(bf16)
    return high, (v - high.astype(f32)).astype(bf16)


ANYWHERE = pl.BlockSpec(memory_space=pl.ANY)


def once(shape):
    return pl.BlockSpec(shape, lambda *g: (0,) * len(shape), pipeline_mode=pl.Buffered(1))


def norm_body(x_ref, gain_ref, shift_ref, hid_ref, hid_t_ref):
    x = x_ref[...].astype(f32)
    center = x - jnp.mean(x, axis=-1, keepdims=True)
    inv = lax.rsqrt(jnp.mean(center * center, axis=-1, keepdims=True) + epsilon)
    hid = center * inv * gain_ref[...] + shift_ref[...]
    hid_ref[...] = hid.astype(bf16)
    hid_t_ref[...] = hid.T.astype(bf16)


def norm(tokens, gain, shift):
    return pl.pallas_call(
        norm_body,
        grid=(STEPS,),
        out_shape=(jax.ShapeDtypeStruct((LEN, D), bf16), jax.ShapeDtypeStruct((D, LEN), bf16)),
        in_specs=[pl.BlockSpec((TILE, D), lambda g: (g, 0)), once((1, D)), once((1, D))],
        out_specs=(
            pl.BlockSpec((TILE, D), lambda g: (g, 0)),
            pl.BlockSpec((D, TILE), lambda g: (0, g)),
        ),
        compiler_params=pltpu.CompilerParams(vmem_limit_bytes=VMEM_LIMIT),
        cost_estimate=cost(flops=1 << 25, transcendentals=0, bytes_accessed=6 << 20),
        name="norm",
    )(tokens, gain, shift)


def attention_body(
    n_carried,
    core_ref,
    hid_ref,
    hid_t_ref,
    dy_ref,
    wq_ref,
    wk_ref,
    wv_ref,
    bq_ref,
    bk_ref,
    bv_ref,
    wo_ref,
    cos_ref,
    left_ref,
    right_ref,
    proj_ref,
    proj_low_ref,
    ones_ref,
    quad_ref,
    doc_col_ref,
    doc_row_ref,
    *rest,
):
    (
        att_ref,
        dm_ref,
        keep_ref,
        send_ref,
        keep_o_ref,
        send_o_ref,
        sums_ref,
        mask,
        scores,
        yq,
        yk,
        fq,
        fk,
        val,
        val_h,
        fq_t,
        dnum,
        dnum_t,
        cross,
        cross_low,
        att_t,
        num,
        den,
        dfq,
        dfk_t,
        dv_t,
        eq,
        ek,
    ) = rest[n_carried:]
    span = [pl.ds(r * TILE, TILE) for r in range(STEPS)]
    lane = lax.broadcasted_iota(jnp.int32, (TILE, WIDE), 1) // HD
    ones = ones_ref[...]
    proj, proj_low = proj_ref[...], proj_low_ref[...]

    for i, (q, k) in enumerate(PAIRS):
        here = doc_col_ref[span[q], :] == doc_row_ref[:, span[k]]
        if q == k:
            row = lax.broadcasted_iota(jnp.int32, (TILE, TILE), 0)
            col = lax.broadcasted_iota(jnp.int32, (TILE, TILE), 1)
            here = here & (row >= col)
        mask[i] = jnp.where(here, 1.0, 0.0).astype(bf16)

    hid = hid_ref[...]
    val[...] = (nn(hid, wv_ref[...]) + bv_ref[...]).astype(bf16)
    eq[...] = nn(hid, wq_ref[...]) + bq_ref[...]
    ek[...] = nn(hid, wk_ref[...]) + bk_ref[...]
    for r in range(STEPS):
        for y_out, f_out, e_out, scale in ((yq, fq, eq, True), (yk, fk, ek, False)):
            raw = e_out[span[r], :]
            y = (
                raw * cos_ref[span[r], :]
                + pltpu.roll(raw, WIDE - 8, 1) * left_ref[span[r], :]
                + pltpu.roll(raw, 8, 1) * right_ref[span[r], :]
            )
            y_high, y_low = halves(y)
            s_high, s_low = halves(y * y)
            power = nt(y_high, proj) + nt(y_low, proj) + nt(y_high, proj_low)
            power = power - 0.5 * (nn(s_high, ones) + nn(s_low, ones))
            feat = jnp.exp(power)
            if scale:
                feat = feat * quad_ref[...]
            y_out[span[r], :] = y
            e_out[span[r], :] = feat
            f_out[span[r], :] = feat.astype(bf16)
            if scale:
                fq_t[:, span[r]] = feat.T.astype(bf16)

    def forward(h, carry):
        own = lane == h
        for r in range(STEPS):
            val_h[h, span[r], :] = jnp.where(own, val[span[r], :], jnp.ones((), bf16))
        total = None
        for i, (q, k) in enumerate(PAIRS):
            query = jnp.where(own, fq[span[q], :], jnp.zeros((), bf16))
            tile = nt(query, fk[span[k], :]).astype(bf16) * mask[i]
            scores[h * len(PAIRS) + i] = tile
            part = nn(tile, val_h[h, span[k], :])
            total = part if total is None else total + part
            if k == q:
                num[span[q], :] = jnp.where(own, total, num[span[q], :])
                den[span[q], :] = jnp.where(own, pltpu.roll(total, HD, 1), den[span[q], :])
                total = None
        return carry

    lax.fori_loop(0, PER, forward, 0, unroll=True)

    dfq[...] = nt(dy_ref[...], wo_ref[...])
    for r in range(STEPS):
        grad = dfq[span[r], :]
        inv = 1.0 / den[span[r], :]
        att = num[span[r], :] * inv
        att_ref[span[r], :] = att.astype(bf16)
        d_num = grad * inv
        dnum[span[r], :] = d_num.astype(bf16)
        dnum_t[:, span[r]] = d_num.T.astype(bf16)
        att_t[:, span[r]] = att.T.astype(bf16)
        high, low = halves(pltpu.roll(-d_num * att, HD, 1))
        cross[span[r], :] = high
        cross_low[span[r], :] = pltpu.roll(low.astype(f32), HD, 1).astype(bf16)

    def backward(h, carry):
        own = lane == h
        after = lane == lax.rem(h + 1, PER)
        later = lane == lax.rem(h + 2, PER)
        mine = pl.ds(pl.multiple_of(h * HD, HD), HD)
        dfk_t[mine, :] = jnp.zeros((HD, LEN), f32)
        dv_t[mine, :] = jnp.zeros((HD, LEN), f32)
        total = None
        for i, (q, k) in enumerate(PAIRS):
            left = jnp.where(
                own,
                dnum[span[q], :],
                jnp.where(
                    after,
                    cross[span[q], :],
                    jnp.where(later, cross_low[span[q], :], jnp.zeros((), bf16)),
                ),
            )
            tile = nt(left, val_h[h, span[k], :]).astype(bf16) * mask[i]
            part = nn(tile, fk[span[k], :])
            total = part if total is None else total + part
            dfk_t[mine, span[k]] += nn(fq_t[mine, span[q]], tile)
            dv_t[mine, span[k]] += nn(dnum_t[mine, span[q]], scores[h * len(PAIRS) + i])
            if k == q:
                dfq[span[q], :] = jnp.where(own, total, dfq[span[q], :])
                total = None
        return carry

    lax.fori_loop(0, PER, backward, 0, unroll=True)

    sums = [jnp.zeros((1, WIDE), f32)] * 3
    for r in range(STEPS):
        grads = []
        for d_feat, feat, y in (
            (dfq[span[r], :], eq, yq),
            (dfk_t[:, span[r]].T, ek, yk),
        ):
            e_high, e_low = halves(d_feat * feat[span[r], :])
            d_y = nn(e_high, proj) + nn(e_low, proj) + nn(e_high, proj_low)
            d_y = d_y - (nn(e_high, ones) + nn(e_low, ones)) * y[span[r], :]
            grads.append(
                d_y * cos_ref[span[r], :]
                - pltpu.roll(d_y, WIDE - 8, 1) * left_ref[span[r], :]
                - pltpu.roll(d_y, 8, 1) * right_ref[span[r], :]
            )
        grads.append(dv_t[:, span[r]].T)
        for i in range(3):
            low = grads[i].astype(bf16)
            dm_ref[i, span[r], :] = low
            sums[i] = sums[i] + jnp.sum(low.astype(f32), axis=0, keepdims=True)
    for i in range(3):
        sums_ref[pl.ds(i, 1), :] = sums[i]

    first = core_ref[0] == 0
    half = WIDE // 2
    for i in range(3):
        full = nn(hid_t_ref[...], dm_ref[i]).astype(bf16)
        low, high = full[:, :half], full[:, half:]
        keep_ref[i] = jnp.where(first, low, high)
        send_ref[i] = jnp.where(first, high, low)
    full = nn(att_t[...], dy_ref[...]).astype(bf16)
    low, high = full[:, : D // 2], full[:, D // 2 :]
    keep_o_ref[...] = jnp.where(first, low, high)
    send_o_ref[...] = jnp.where(first, high, low)


def attention(core, group, operands, w_qkv, w_out, carried, after):
    hid, hid_t, dy, b_qkv, cos_t, left_t, right_t, proj, proj_low, ones, quad, doc_col, doc_row = operands
    half = D // 2
    at = lambda shape, index: pl.BlockSpec(shape, lambda s: index, pipeline_mode=pl.Buffered(1))
    col = lambda part: at((D, WIDE), (0, part * 2 + group % 2))
    bias = lambda part: at((1, WIDE), (0, part * GROUPS + group))
    shapes = [
        ((LEN, D), bf16, at((LEN, WIDE), (0, group))),
        ((3, LEN, D), bf16, at((3, LEN, WIDE), (0, 0, group))),
        ((3, D, half), bf16, at((3, D, WIDE // 2), (0, 0, group))),
        ((3, D, half), bf16, at((3, D, WIDE // 2), (0, 0, group))),
        ((D, half), bf16, at((WIDE, half), (group, 0))),
        ((D, half), bf16, at((WIDE, half), (group, 0))),
        ((8, D), f32, at((8, WIDE), (0, group))),
    ]
    in_specs = [
        pl.BlockSpec(memory_space=pltpu.SMEM),
        once((LEN, D)),
        once((D, LEN)),
        once((LEN, D)),
        col(0),
        col(1),
        col(2),
        bias(0),
        bias(1),
        bias(2),
        at((WIDE, D), (group, 0)),
        once((LEN, WIDE)),
        once((LEN, WIDE)),
        once((LEN, WIDE)),
        once((WIDE, WIDE)),
        once((WIDE, WIDE)),
        once((WIDE, WIDE)),
        once((1, WIDE)),
        once((LEN, 1)),
        once((1, LEN)),
    ]
    extra = list(carried) + list(after)
    vm = pltpu.VMEM
    tall, flat = (LEN, WIDE), (WIDE, LEN)
    scratch = [
        vm((len(PAIRS), TILE, TILE), bf16),
        vm((PER * len(PAIRS), TILE, TILE), bf16),
        vm(tall, f32),
        vm(tall, f32),
        vm(tall, bf16),
        vm(tall, bf16),
        vm(tall, bf16),
        vm((PER,) + tall, bf16),
        vm(flat, bf16),
        vm(tall, bf16),
        vm(flat, bf16),
        vm(tall, bf16),
        vm(tall, bf16),
        vm(flat, bf16),
        vm(tall, f32),
        vm(tall, f32),
        vm(tall, f32),
        vm(flat, f32),
        vm(flat, f32),
        vm(tall, f32),
        vm(tall, f32),
    ]
    return pl.pallas_call(
        functools.partial(attention_body, len(extra)),
        grid=(1,),
        out_shape=tuple(jax.ShapeDtypeStruct(s, t) for s, t, _ in shapes),
        in_specs=in_specs + [ANYWHERE] * len(extra),
        out_specs=tuple(spec for _, _, spec in shapes),
        scratch_shapes=scratch,
        input_output_aliases={len(in_specs) + i: i for i in range(len(carried))},
        compiler_params=pltpu.CompilerParams(vmem_limit_bytes=VMEM_LIMIT),
        cost_estimate=cost(flops=30 << 30, transcendentals=0, bytes_accessed=20 << 20),
        name="attention",
    )(
        core, hid, hid_t, dy, w_qkv, w_qkv, w_qkv, b_qkv, b_qkv, b_qkv, w_out,
        cos_t, left_t, right_t, proj, proj_low, ones, quad, doc_col, doc_row, *extra,
    )


CALLS = 2


def up_body(rows, wide, n_extra, core_ref, hid_ref, dy_ref, w1_ref, b1_ref, *rest):
    act_ref, slope_ref, keep_ref, send_ref, act_t = rest[n_extra:]
    block = w1_ref.shape[1]
    for r in range(STEPS):
        at = pl.ds(r * TILE, TILE)
        upper = nn(hid_ref[at, :], w1_ref[...]) + b1_ref[...]
        bell = jnp.exp(-0.5 * upper * upper)
        phi = 0.5 + 0.5 * lax.erf(upper * (1.0 / math.sqrt(2.0)))
        act = (upper * phi).astype(bf16)
        act_ref[at, :] = act
        act_t[:, at] = act.T
        slope_ref[at, :] = (phi + upper * bell * (1.0 / math.sqrt(2.0 * math.pi))).astype(bf16)
    first = core_ref[0] == 0
    full = nn(act_t[...], dy_ref[...]).astype(bf16)
    top = wide // rows // 2
    for p in range(block // wide):
        for b in range(top):
            low = full[p * wide + b * rows : p * wide + (b + 1) * rows]
            start = p * wide + (top + b) * rows
            high = full[start : start + rows]
            keep_ref[b, pl.ds(p * rows, rows), :] = jnp.where(first, low, high)
            send_ref[b, pl.ds(p * rows, rows), :] = jnp.where(first, high, low)


def up_part(core, rows, wide, call, hid, dy, w1, b1, carried=(), after=()):
    grid = FF // BLOCK // CALLS
    base = call * grid
    top = wide // rows // 2
    per = BLOCK // wide * rows
    total = FF // wide * rows
    grad = ((top, total, D), bf16, pl.BlockSpec((top, per, D), lambda g: (0, base + g, 0)))
    units = ((LEN, FF), bf16, pl.BlockSpec((LEN, BLOCK), lambda g: (0, base + g)))
    shapes = [units, units, grad, grad]
    extra = list(carried) + list(after)
    return pl.pallas_call(
        functools.partial(up_body, rows, wide, len(extra)),
        grid=(grid,),
        out_shape=tuple(jax.ShapeDtypeStruct(s, t) for s, t, _ in shapes),
        in_specs=[
            pl.BlockSpec(memory_space=pltpu.SMEM),
            once((LEN, D)),
            once((LEN, D)),
            pl.BlockSpec((D, BLOCK), lambda g: (0, base + g)),
            pl.BlockSpec((1, BLOCK), lambda g: (0, base + g)),
        ]
        + [ANYWHERE] * len(extra),
        out_specs=tuple(spec for _, _, spec in shapes),
        scratch_shapes=[pltpu.VMEM((BLOCK, LEN), bf16)],
        input_output_aliases={5 + i: i for i in range(len(carried))},
        compiler_params=pltpu.CompilerParams(vmem_limit_bytes=VMEM_LIMIT),
        cost_estimate=cost(
            flops=4 * LEN * D * FF // CALLS, transcendentals=0, bytes_accessed=18 << 20
        ),
        name="up",
    )(core, hid, dy, w1, b1, *extra)


def down_body(n_extra, core_ref, hid_t_ref, dy_ref, w2_ref, slope_ref, *rest):
    dup_ref, sums_ref, grad_ref = rest[n_extra:]
    block = w2_ref.shape[0]
    total = jnp.zeros((1, block), f32)
    for r in range(STEPS):
        at = pl.ds(r * TILE, TILE)
        d_up = (nt(dy_ref[at, :], w2_ref[...]) * slope_ref[at, :].astype(f32)).astype(bf16)
        dup_ref[at, :] = d_up
        total = total + jnp.sum(d_up.astype(f32), axis=0, keepdims=True)
    sums_ref[...] = total
    grad_ref[0] = nn(hid_t_ref[...], dup_ref[...]).astype(bf16)


def down_part(core, call, hid_t, dy, w2, slope, carried=(), after=()):
    grid = FF // BLOCK // CALLS
    per = D // BLOCK
    unit = lambda g, ref: (ref[0] ^ 1 ^ call) * grid + g
    shapes = [
        ((LEN, FF), bf16, pl.BlockSpec((LEN, BLOCK), lambda g, ref: (0, unit(g, ref)))),
        ((1, FF), f32, pl.BlockSpec((1, BLOCK), lambda g, ref: (0, unit(g, ref)))),
        (
            (FF // D // CALLS, D, D),
            bf16,
            pl.BlockSpec((1, D, BLOCK), lambda g, ref: (g // per, 0, g % per)),
        ),
    ]
    extra = list(carried) + list(after)
    return pl.pallas_call(
        functools.partial(down_body, len(extra)),
        grid_spec=pltpu.PrefetchScalarGridSpec(
            num_scalar_prefetch=1,
            grid=(grid,),
            in_specs=[
                once((D, LEN)),
                once((LEN, D)),
                pl.BlockSpec((BLOCK, D), lambda g, ref: (unit(g, ref), 0)),
                pl.BlockSpec((LEN, BLOCK), lambda g, ref: (0, unit(g, ref))),
            ]
            + [ANYWHERE] * len(extra),
            out_specs=tuple(spec for _, _, spec in shapes),
        ),
        out_shape=tuple(jax.ShapeDtypeStruct(s, t) for s, t, _ in shapes),
        input_output_aliases={5 + i: i for i in range(len(carried))},
        compiler_params=pltpu.CompilerParams(vmem_limit_bytes=VMEM_LIMIT),
        cost_estimate=cost(
            flops=4 * LEN * D * FF // CALLS, transcendentals=0, bytes_accessed=18 << 20
        ),
        name="down",
    )(core, hid_t, dy, w2, slope, *extra)


CHUNK = 512


def output_first_body(n_after, act_ref, w2_ref, x_ref, bias_ref, *rest):
    out_ref = rest[n_after]

    @pl.when(pl.program_id(0) == 0)
    def _():
        out_ref[...] = x_ref[...].astype(f32) + bias_ref[...]

    out_ref[...] += nn(act_ref[...], w2_ref[...])


def output_first(act, w2, tokens, bias, after=()):
    return pl.pallas_call(
        functools.partial(output_first_body, len(after)),
        grid=(FF // CHUNK // 2,),
        out_shape=jax.ShapeDtypeStruct((LEN, D), f32),
        in_specs=[
            pl.BlockSpec((LEN, CHUNK), lambda g: (0, g)),
            pl.BlockSpec((CHUNK, D), lambda g: (g, 0)),
            once((LEN, D)),
            once((1, D)),
        ]
        + [ANYWHERE] * len(after),
        out_specs=once((LEN, D)),
        compiler_params=pltpu.CompilerParams(vmem_limit_bytes=VMEM_LIMIT),
        cost_estimate=cost(
            flops=LEN * D * FF, transcendentals=0, bytes_accessed=14 << 20
        ),
        name="output_first",
    )(act, w2, tokens, bias, *after)


def output_rest_body(n_after, act_ref, att_ref, w2_ref, wo_ref, acc_ref, *rest):
    out_ref = rest[n_after]
    step = pl.program_id(0)

    @pl.when(step == 0)
    def _():
        out_ref[...] = acc_ref[...] + nn(act_ref[...], w2_ref[...])

    @pl.when((step > 0) & (step < FF // CHUNK // 2))
    def _():
        out_ref[...] += nn(act_ref[...], w2_ref[...])

    @pl.when(step >= FF // CHUNK // 2)
    def _():
        out_ref[...] += nn(att_ref[...], wo_ref[...])


def output_rest(act, att, w2, wo, acc, after=()):
    lead, tail = FF // CHUNK // 2, D // CHUNK
    low = lambda g: lead + jnp.minimum(g, lead - 1)
    high = lambda g: jnp.maximum(g - lead, 0)
    return pl.pallas_call(
        functools.partial(output_rest_body, len(after)),
        grid=(lead + tail,),
        out_shape=jax.ShapeDtypeStruct((LEN, D), f32),
        in_specs=[
            pl.BlockSpec((LEN, CHUNK), lambda g: (0, low(g))),
            pl.BlockSpec((LEN, CHUNK), lambda g: (0, high(g))),
            pl.BlockSpec((CHUNK, D), lambda g: (low(g), 0)),
            pl.BlockSpec((CHUNK, D), lambda g: (high(g), 0)),
            once((LEN, D)),
        ]
        + [ANYWHERE] * len(after),
        out_specs=once((LEN, D)),
        compiler_params=pltpu.CompilerParams(vmem_limit_bytes=VMEM_LIMIT),
        cost_estimate=cost(
            flops=LEN * D * (FF + 2 * D), transcendentals=0, bytes_accessed=18 << 20
        ),
        name="output_rest",
    )(act, att, w2, wo, acc, *after)


def back_body(n_after, dup_ref, w1_ref, *rest):
    acc_ref = rest[n_after]
    step = pl.program_id(0)

    @pl.when(step == 0)
    def _():
        acc_ref[...] = nt(dup_ref[...], w1_ref[...])

    @pl.when(step > 0)
    def _():
        acc_ref[...] += nt(dup_ref[...], w1_ref[...])


def back_part(d_up, w1, after=()):
    return pl.pallas_call(
        functools.partial(back_body, len(after)),
        grid=(FF // CHUNK,),
        out_shape=jax.ShapeDtypeStruct((LEN, D), f32),
        in_specs=[
            pl.BlockSpec((LEN, CHUNK), lambda g: (0, g)),
            pl.BlockSpec((D, CHUNK), lambda g: (0, g)),
        ]
        + [ANYWHERE] * len(after),
        out_specs=once((LEN, D)),
        compiler_params=pltpu.CompilerParams(vmem_limit_bytes=VMEM_LIMIT),
        cost_estimate=cost(
            flops=2 * LEN * D * FF, transcendentals=0, bytes_accessed=20 << 20
        ),
        name="back",
    )(d_up, w1, *after)


def input_body(n_after, dm_ref, wa_ref, wb_ref, acc_ref, x_ref, cot_ref, gain_ref, *rest):
    out_ref, sums_ref, acc = rest[n_after:]
    step = pl.program_id(0)
    last = 3 * D // CHUNK - 1

    @pl.when(step == 0)
    def _():
        acc[...] = acc_ref[...] + nt(dm_ref[0], wa_ref[...])

    @pl.when((step > 0) & (step < 3))
    def _():
        acc[...] += nt(dm_ref[0], wa_ref[...])

    @pl.when(step >= 3)
    def _():
        acc[...] += nt(dm_ref[0], wb_ref[...])

    @pl.when(step == last)
    def _():
        g_gain, g_shift = jnp.zeros((1, D), f32), jnp.zeros((1, D), f32)
        for r in range(STEPS):
            at = pl.ds(r * TILE, TILE)
            x = x_ref[at, :].astype(f32)
            center = x - jnp.mean(x, axis=-1, keepdims=True)
            inv = lax.rsqrt(jnp.mean(center * center, axis=-1, keepdims=True) + epsilon)
            normed = center * inv
            d_hidden = acc[at, :]
            g_gain = g_gain + jnp.sum(d_hidden * normed, axis=0, keepdims=True)
            g_shift = g_shift + jnp.sum(d_hidden, axis=0, keepdims=True)
            d_normed = d_hidden * gain_ref[...]
            mean_grad = jnp.mean(d_normed, axis=-1, keepdims=True)
            mean_cross = jnp.mean(d_normed * normed, axis=-1, keepdims=True)
            out_ref[at, :] = cot_ref[at, :] + inv * (d_normed - mean_grad - normed * mean_cross)
        sums_ref[0:1, :] = g_gain
        sums_ref[1:2, :] = g_shift


def input_part(d_mixed, wa, wb, acc, tokens, cotangent, gain, after=()):
    per = D // CHUNK
    return pl.pallas_call(
        functools.partial(input_body, len(after)),
        grid=(3 * per,),
        out_shape=(jax.ShapeDtypeStruct((LEN, D), f32), jax.ShapeDtypeStruct((8, D), f32)),
        in_specs=[
            pl.BlockSpec((1, LEN, CHUNK), lambda g: (g % 3, 0, g // 3)),
            pl.BlockSpec((D, CHUNK), lambda g: (0, jnp.minimum(g, 2))),
            pl.BlockSpec((D, CHUNK), lambda g: (0, jnp.maximum(g - 3, 0))),
            once((LEN, D)),
            once((LEN, D)),
            once((LEN, D)),
            once((1, D)),
        ]
        + [ANYWHERE] * len(after),
        out_specs=(once((LEN, D)), once((8, D))),
        scratch_shapes=[pltpu.VMEM((LEN, D), f32)],
        compiler_params=pltpu.CompilerParams(vmem_limit_bytes=VMEM_LIMIT),
        cost_estimate=cost(
            flops=6 * LEN * D * D, transcendentals=0, bytes_accessed=32 << 20
        ),
        name="input",
    )(d_mixed, wa, wb, acc, tokens, cotangent, gain, *after)


def fold(terms, view, block, in_at, out_view, out_block, out_at, n, steps, scalars, after=()):
    args, in_specs, out_specs, shapes, plan = [], [], [], [], []
    count = sum(part.shape[0] for part in terms[0])
    for j in range(n):
        sources = []
        for term in terms:
            spans = []
            at = 0
            for part in term:
                k = part.shape[0]
                spans.append((len(args), at, k))
                args.append(part.reshape((k,) + view))
                in_specs.append(
                    pl.BlockSpec((k,) + block, lambda s, ref, j=j: (0,) + in_at(s, j, ref))
                )
                at += k
            sources.append(spans)
        plan.append(sources)
        out_specs.append(pl.BlockSpec((count,) + out_block, lambda s, ref: (0,) + out_at(s)))
        shapes.append(jax.ShapeDtypeStruct((count,) + out_view, bf16))
    n_args = len(args)
    n_after = len(after)
    moved = n * (len(terms) + 1) * 2 * count * math.prod(out_view)

    def body(ref, *refs):
        for o, sources in enumerate(plan):
            out = refs[n_args + n_after + o]
            cuts = sorted({cut for spans in sources for _, at, k in spans for cut in (at, at + k)})
            for lo, hi in zip(cuts, cuts[1:]):
                total = None
                for spans in sources:
                    for arg, at, k in spans:
                        if at <= lo and hi <= at + k:
                            value = refs[arg][lo - at : hi - at].astype(f32)
                            total = value if total is None else total + value
                out[lo:hi] = total.astype(bf16).reshape((hi - lo,) + out_block)

    return list(
        pl.pallas_call(
            body,
            grid_spec=pltpu.PrefetchScalarGridSpec(
                num_scalar_prefetch=1,
                grid=(steps,),
                in_specs=in_specs + [ANYWHERE] * n_after,
                out_specs=out_specs,
            ),
            out_shape=tuple(shapes),
            compiler_params=pltpu.CompilerParams(vmem_limit_bytes=VMEM_LIMIT),
            cost_estimate=cost(flops=moved, transcendentals=0, bytes_accessed=moved),
            name="fold",
        )(scalars, *args, *after)
    )


class Reduction:
    def __init__(self, grid, keep, send):
        self.grid = grid
        self.d = d = grid.digits()
        first = d["c"] == 0
        self.own = jnp.where(first, d["x"], d["y"]).astype(jnp.int32)
        self.next = jnp.where(first, d["y"], d["x"]).astype(jnp.int32)
        self.cols = keep[0].shape[-1]
        self.rows = keep[0].shape[1] // grid.n
        self.terms = [keep, [grid.swap(v, "c", 1) for v in send]]

    def token(self):
        return self.terms[0]

    def first(self, after=()):
        g, cols, two = self.grid, self.cols, 2 * self.rows
        half = cols // 2

        def in_at(s, j, ref):
            mine, other = ref[1] ^ j, s // 2
            y = jnp.where(ref[0] == 0, other, mine)
            x = jnp.where(ref[0] == 0, mine, other)
            return (y, 0, x, 0, s % 2)

        parts = fold(
            self.terms,
            (2, g.nz, 2, two, cols),
            (1, g.nz, 1, two, half),
            in_at,
            (2, g.nz, two, cols),
            (1, g.nz, two, half),
            lambda s: (s // 2, 0, 0, s % 2),
            2,
            4,
            jnp.stack([self.d["c"].astype(jnp.int32), self.own]),
            after,
        )
        self.terms = [parts[:1], [g.swap_by_core(parts[1], "x", "y")]]

    def second(self, after=()):
        g, cols, two = self.grid, self.cols, 2 * self.rows
        part = cols // 4
        parts = fold(
            self.terms,
            (2, g.nz, two, cols),
            (1, g.nz, two, part),
            lambda s, j, ref: (ref[0] ^ j, 0, 0, s),
            (g.nz, two, cols),
            (g.nz, two, part),
            lambda s: (0, 0, s),
            2,
            4,
            self.next[None],
            after,
        )
        self.terms = [parts[:1], [g.swap_by_core(parts[1], "y", "x")]]

    def third(self, after=()):
        g, cols, two = self.grid, self.cols, 2 * self.rows
        part = cols // 2
        parts = fold(
            self.terms,
            (g.nz, two, cols),
            (1, two, part),
            lambda s, j, ref: (ref[0] ^ j, 0, s),
            (two, cols),
            (two, part),
            lambda s: (0, s),
            g.nz,
            2,
            self.d["z"].astype(jnp.int32)[None],
            after,
        )
        self.parts = [parts[0]] + [g.swap(parts[j], "z", j) for j in range(1, g.nz)]

    def result(self, after=()):
        if after:
            self.parts = lax.optimization_barrier((*self.parts, *after))[: len(self.parts)]
        total = self.parts[0].astype(f32)
        for part in self.parts[1:]:
            total = total + part.astype(f32)
        total = total.reshape(-1, 2, self.rows, self.cols)
        core = self.d["c"]
        mine = pick(total, 1, core)
        got = self.grid.swap(pick(total, 1, 1 - core), "c", 1)
        return jnp.where(core == 0, mine, got), jnp.where(core == 0, got, mine)


class SmallReduction:
    def __init__(self, grid, grad):
        self.grid = grid
        self.d = grid.digits()
        self.now = grad.reshape(grid.ny, grid.nz, grid.nx, 2, grad.shape[1])

    def step(self, digit, axis, after=None):
        if after is not None:
            self.now, _ = lax.optimization_barrier((self.now, after))
        mine = pick(self.now, axis, self.d[digit])
        for k in range(1, self.grid.sizes[digit]):
            mine = mine + self.grid.swap(pick(self.now, axis, self.d[digit] ^ k), digit, k)
        self.now = mine

    def last(self):
        self.step("z", 0)
        return self.now


def tables(node_seeds, node_weights):
    width = node_seeds.shape[1]
    uniform_pts = (node_seeds.astype(jnp.float32) + 0.5) / 1024.0
    nodes = math.sqrt(2.0) * lax.erf_inv(2.0 * uniform_pts - 1.0)
    order = jnp.arange(width).astype(jnp.float32)
    scales = jnp.where(order[:, None] == 0.0, math.sqrt(1.0 / width), math.sqrt(2.0 / width))
    basis = scales * jnp.cos(
        math.pi * (2.0 * order[None, :] + 1.0) * order[:, None] / (2.0 * width)
    )
    projection = jnp.dot(nodes, basis, precision=precise)
    weights_float = node_weights.astype(jnp.float32)
    return (projection, weights_float / jnp.sum(weights_float))


def layout(lengths):
    ends = jnp.cumsum(lengths)
    starts = ends - lengths
    places = jnp.arange(LEN, dtype=jnp.int32)
    doc_ids = jnp.sum((places[:, None] >= ends[None, :]).astype(jnp.int32), axis=1)
    owners = doc_ids[:, None] == jnp.arange(DOCS, dtype=jnp.int32)[None, :]
    begins = jnp.sum(jnp.where(owners, starts[None, :], 0), axis=1)
    return (doc_ids, (places - begins).astype(jnp.float32))


def rotary(positions):
    half_rot = ROT // 2
    freqs = 10000.0 ** (-2.0 * jnp.arange(half_rot).astype(jnp.float32) / ROT)
    angles = positions[:, None] * freqs[None, :]
    return (jnp.cos(angles), jnp.sin(angles))


def pick(value, axis, index):
    return lax.dynamic_index_in_dim(value, index, axis, keepdims=False)


def shards(
    grid,
    tokens,
    ln_gain,
    ln_bias,
    qkv_weight,
    qkv_bias,
    out_weight,
    out_bias,
    fc1_weight,
    fc1_bias,
    fc2_weight,
    fc2_bias,
    cotangent,
    doc_lengths,
    node_seeds,
    node_weights,
):
    n = grid.n
    rows = qkv_weight.shape[0]
    staged = rows % 32 == 0 and grid.nx == 2 and grid.ny == 2
    block_rows = rows if staged else 32
    wide = FF // n if staged else 64
    folds = wide // block_rows
    vectors = (ln_gain, ln_bias, qkv_bias, out_bias, fc1_bias, fc2_bias)
    small = jnp.concatenate(vectors)
    per_row = small.shape[0] // rows
    small = jnp.pad(small.reshape(rows, per_row), ((0, 0), (0, 128 - per_row)))
    if staged:
        pairs = [
            jnp.concatenate([qkv_weight[:, p * D + h : p * D + h + D // 2] for p in range(3)], axis=1)
            for h in (0, D // 2)
        ]
        folded = fc2_weight.reshape(folds, rows, D)
        folded = jnp.concatenate([folded[i] for i in range(folds)], axis=1)
        packed = pack(
            grid,
            [
                [(pairs[0], 1), (out_weight, 1), (jnp.pad(small, ((0, 0), (0, 128))), 1)],
                [(pairs[1], 1)],
                [(fc1_weight, 1)],
                [(folded, folds)],
            ],
        )
        head = Gather(grid, *packed[0])
        token = place_all([head.first()])
        rest = Gather(grid, *packed[1], token)
        token = place_all([head.second(), rest.first()])
        head.cores()
        ups = Gather(grid, *packed[2], token)
        place_all([head.third()])
        pair_weights, attn_weight, small_all = [head.full[0], None], head.full[1], head.full[2]
    else:
        joint_weight, small_all, attn_weight, up_weight, down_weight = [
            lax.all_gather(w, AXES, axis=0, tiled=True)
            for w in (qkv_weight, small, out_weight, fc1_weight, fc2_weight)
        ]
        pair_weights = [
            jnp.concatenate([joint_weight[:, p * D + h : p * D + h + D // 2] for p in range(3)], axis=1)
            for h in (0, D // 2)
        ]
    small_all = small_all[:, :per_row].reshape(n, rows * per_row)
    whole = []
    at = 0
    for v in vectors:
        whole.append(small_all[:, at : at + v.shape[0]].reshape(n * v.shape[0]).astype(f32))
        at += v.shape[0]
    norm_gain, norm_shift, joint_bias, attn_bias, up_bias, down_bias = whole

    core = grid.digits()["c"] if staged else jnp.zeros((), jnp.int32)
    core_arg = core.reshape(1).astype(jnp.int32)
    dy_low = cotangent.astype(bf16)
    dy_sums = jnp.sum(dy_low.astype(f32), axis=0)
    hidden_low, hidden_t = norm(tokens, norm_gain[None], norm_shift[None])

    projection, quad = tables(node_seeds, node_weights)
    doc_ids, positions = layout(doc_lengths[0])
    cos, sin = rotary(positions)
    flat = jnp.ones((LEN, HD - ROT), f32)
    none = jnp.zeros((LEN, ROT // 2), f32)
    cos_t = feature_scale * jnp.tile(jnp.concatenate([cos, cos, flat], axis=1), (1, PER))
    left_t = feature_scale * jnp.tile(jnp.concatenate([-sin, none, 0 * flat], axis=1), (1, PER))
    right_t = feature_scale * jnp.tile(jnp.concatenate([none, sin, 0 * flat], axis=1), (1, PER))
    eye = jnp.eye(PER, dtype=f32)
    wide_proj = jnp.einsum("ab,jd->ajbd", eye, projection, precision=precise).reshape(WIDE, WIDE)
    near = lax.reduce_precision(wide_proj, 8, 7)
    ones = jnp.kron(eye, jnp.ones((HD, HD), f32)).astype(bf16)

    operands = (
        hidden_low,
        hidden_t,
        dy_low,
        joint_bias[None],
        cos_t,
        left_t,
        right_t,
        near.astype(bf16),
        (wide_proj - near).astype(bf16),
        ones,
        jnp.tile(quad, PER)[None],
        doc_ids[:, None],
        doc_ids[None],
    )
    carried = ()
    for group in range(GROUPS):
        after = ()
        if staged and group == 1:
            token = place_all([rest.second(), ups.first()], carried[:1])
            after = token
        if staged and group == 2:
            rest.cores(carried[:1])
            place_all([rest.third(), ups.second()])
            pair_weights[1] = rest.full[0]
            downs = Gather(grid, *packed[3], (rest.full[0],))
        if staged and group == 3:
            ups.cores(carried[:1])
            token = place_all([ups.third(), downs.first()], carried[:1])
            up_weight = ups.full[0]
            after = token
        carried = attention(
            core_arg, group, operands, pair_weights[group // 2], attn_weight, carried, after
        )
    att, d_mixed, keep_qkv, send_qkv, keep_o, send_o, joint_sums = carried
    after = carried[:1]
    if staged:
        joint_sum = Reduction(grid, [keep_qkv, keep_o[None]], [send_qkv, send_o[None]])
        after = place_all([downs.second()], carried[:1])
    hidden = ()
    for call in range(CALLS):
        if staged and call == 1:
            joint_sum.first(hidden[:1])
            after = joint_sum.token()
        hidden = up_part(
            core_arg, block_rows, wide, call, hidden_low, dy_low, up_weight, up_bias[None], hidden, after
        )
    act, slope, keep_2, send_2 = hidden
    after = hidden[:1]
    if staged:
        downs.cores(hidden[:1])
        joint_sum.second(hidden[:1])
        place_all([downs.third()], joint_sum.token())
        (down_weight,) = downs.full
        down_sum = Reduction(grid, [keep_2], [send_2])
    back = ()
    grads_1 = []
    for call in range(CALLS):
        if staged and call == 1:
            joint_sum.third(back[:1])
            down_sum.first(joint_sum.parts[:1])
            after = down_sum.token()
        d_up, up_sums, grad = down_part(
            core_arg, call, hidden_t, dy_low, down_weight, slope, back, after
        )
        back = (d_up, up_sums)
        grads_1.append(grad)
    after = ()
    if staged:
        up_sum = Reduction(grid, grads_1[1:], grads_1[:1])
        down_sum.second(back[:1])
        after = down_sum.token()
    d_hidden = back_part(d_up, up_weight, after)
    bias = (attn_bias + down_bias)[None]
    g_up_bias = up_sums.reshape(FF)
    g_joint_bias = joint_sums[:3].reshape(3 * D)
    after = ()
    if staged:
        up_sum.first([d_hidden])
        total = joint_sum.result([d_hidden])
        down_sum.third(up_sum.token())
        after = down_sum.parts[:1]
    input_grad, norm_sums = input_part(
        d_mixed, *pair_weights, d_hidden, tokens, cotangent, norm_gain[None], after
    )
    grads = (norm_sums[0], norm_sums[1], g_joint_bias, dy_sums, g_up_bias)
    packed = jnp.concatenate([g.reshape(n, -1) for g in grads], axis=1)
    after = ()
    if staged:
        up_sum.second([input_grad])
        small_sum = SmallReduction(grid, packed)
        small_sum.step("c", 3)
        after = up_sum.token()
    output = output_first(act, down_weight, tokens, bias, after)
    if staged:
        down_total = down_sum.result([output])
        small_sum.step("x", 2, output)
        up_sum.third([output])
        after = up_sum.parts[:1]
    output = output_rest(act, att, down_weight, attn_weight, output, after)
    if staged:
        small_sum.step("y", 0, output)
        s_small = small_sum.last()
        up_total = up_sum.result([output])
        both = jnp.stack([h[:3].reshape(3, rows, GROUPS, WIDE // 2) for h in total], axis=3)
        both = both.reshape(3, rows, D)
        s_joint = jnp.concatenate([both[0], both[1], both[2]], axis=1)
        s_attn = jnp.concatenate([h[3] for h in total], axis=1)
        s_up = jnp.concatenate([h[i] for h in up_total for i in range(2)], axis=1)
        s_down = jnp.concatenate([h.reshape(-1, D) for h in down_total])
    else:
        both = jnp.stack([h.reshape(3, D, GROUPS, WIDE // 2) for h in (keep_qkv, send_qkv)], axis=3)
        both = both.reshape(3, D, D)
        fold_rows = jnp.concatenate([keep_2, send_2]).reshape(folds, FF // wide, block_rows, D)
        both = (
            jnp.concatenate([both[0], both[1], both[2]], axis=1),
            jnp.concatenate([keep_o, send_o], axis=1),
            jnp.concatenate([h[i] for h in grads_1[::-1] for i in range(2)], axis=1),
            fold_rows.transpose(1, 0, 2, 3).reshape(FF, D),
        )
        s_joint, s_attn, s_up, s_down = [
            lax.psum_scatter(g.astype(f32), AXES, scatter_dimension=0, tiled=True) for g in both
        ]
        s_small = lax.psum_scatter(packed, AXES, scatter_dimension=0, tiled=True)[0]
    small_outs = []
    at = 0
    for g in grads:
        small_outs.append(s_small[at : at + g.shape[0] // n])
        at += g.shape[0] // n
    s_gain, s_shift, s_joint_bias, s_dy, s_up_bias = small_outs
    return (
        output,
        input_grad,
        s_gain,
        s_shift,
        s_joint,
        s_joint_bias,
        s_attn,
        s_dy,
        s_up,
        s_up_bias,
        s_down,
        s_dy,
    )


def solution(mesh):
    grid = Grid(mesh.shape["dp"], mesh.shape["fsdp"])
    rows2, rows1 = P(AXES, None), P(AXES)
    in_specs = (
        rows2,
        rows1,
        rows1,
        rows2,
        rows1,
        rows2,
        rows1,
        rows2,
        rows1,
        rows2,
        rows1,
        rows2,
        rows2,
        P(),
        P(),
    )
    out_specs = (
        rows2,
        rows2,
        rows1,
        rows1,
        rows2,
        rows1,
        rows2,
        rows1,
        rows2,
        rows1,
        rows2,
        rows1,
    )
    return jax.shard_map(
        functools.partial(shards, grid),
        mesh=mesh,
        in_specs=in_specs,
        out_specs=out_specs,
        check_vma=False,
    )
```

time: 1780 us -> 547 us (0.31)
  Pallas kernels: 1070 us -> 299 us
  matrix products: 333 us -> 1.17 us
  local copies, waits for them, and re-layouts: 97.9 us -> 51.5 us
  starting transfers between devices: 99 us -> 63.8 us
  other arithmetic: 45.7 us -> 18.4 us
  waiting for transfers between devices: 129 us -> 104 us
    pallas_call x8, Pallas kernels: 1070 us -> 33.1 us  [place(): pl.pallas_call(body, out_shape=tuple(outs), in_specs=[pl.BlockSpec(memory...]
    dot_general x28 -> x0, matrix products: 333 us -> none  [the longest x4 76.6 us: plain_dot(): return jnp.dot(left, right, preferred_element_type=jnp.float32)]
    pallas_call x0 -> x22, Pallas kernels: none -> 266 us  [the longest x4 103 us: attention(): pl.pallas_call(functools.partial(attention_body, len(extra)), grid=(1,),...]
    ppermute x52 -> x43, waiting for transfers between devices: 129 us -> 60 us  [swap(): return lax.ppermute(value, AXES, pairs)]
    ppermute x52 -> x43, starting transfers between devices: 99 us -> 49.8 us  [swap(): return lax.ppermute(value, AXES, pairs)]
    ppermute x0 -> x14, waiting for transfers between devices: none -> 43.7 us  [swap_by_core(): lax.ppermute(value, AXES, [(i, i ^ flips[i % 2]) for i in range(self.n)])]
    dynamic_slice x12 -> x3, local copies, waits for them, and re-layouts: 34.8 us -> 0.12 us  [pick(): return lax.dynamic_index_in_dim(value, index, axis, keepdims=False)]
    slice x19 -> x10, local copies, waits for them, and re-layouts: 37.7 us -> 7.83 us  [the longest x4 2.84 us: shards(): s_joint = jnp.concatenate([both[0], both[1], both[2]], axis=1)]
  transfers between devices with their start and end apart: 52 -> 57, of which waited for: 17 -> 19; matrix products, arithmetic and copies ran while one was open for 11% -> 9% of each run, Pallas kernels for 28% -> 49%
where the time goes in v3:
time: 547 us; the launch traced here: 540 us
  Pallas kernels  299 us (55%)
  waiting for transfers between devices  104 us (19%)
  starting transfers between devices  63.8 us (12%)
  local copies, waits for them, and re-layouts  51.5 us (9%)
  other arithmetic  18.4 us (3%)
    pallas_call x4, Pallas kernels, attention(): pl.pallas_call(functools.partial(attention_body, len(extra)), grid=(1,),...  103 us
    ppermute x43, waiting for transfers between devices, swap(): return lax.ppermute(value, AXES, pairs)  60 us
    ppermute x43, starting transfers between devices, swap(): return lax.ppermute(value, AXES, pairs)  49.8 us
    ppermute x14, waiting for transfers between devices, swap_by_core(): lax.ppermute(value, AXES, [(i, i ^ flips[i % 2]) for i in range(self.n)])  43.7 us
    pallas_call x9, Pallas kernels, fold(): pl.pallas_call(body, grid_spec=pltpu.PrefetchScalarGridSpec(num_scalar_pr...  41.8 us
    pallas_call x8, Pallas kernels, place(): pl.pallas_call(body, out_shape=tuple(outs), in_specs=[pl.BlockSpec(memory...  33.1 us
    pallas_call x2, Pallas kernels, up_part(): pl.pallas_call(functools.partial(up_body, rows, wide, len(extra)), grid=(...  30.4 us
    pallas_call x2, Pallas kernels, down_part(): pl.pallas_call(functools.partial(down_body, len(extra)), grid_spec=pltpu....  28 us
  transfers between devices with their start and end apart: 57, of which 19 were waited for; matrix products, arithmetic and copies ran while one was open for 9% of the time, Pallas kernels for 49%

profile of v3, /device:TPU:0, one launch (start us, length us, event | category | flops | bytes accessed | tf_op | source)
XLA Modules:
  0.0 539.8 jit_solution(7269859930360918429)
XLA Ops:
  22.6 7.9 %collective-permute-done.2.refs_2_ = bf16[2,32,1408]{2,1,0:T(8,128)(2,1)S(1)} collective-permute-done((bf16[2,32,1408]{2,1,0:T(8,128)(2,1)S(1)}, bf16[2,32,1408]{2,1,0:T(8,128)(2,1)S(1)}, u32[]{:S(2)}, u32[]{:S(2)}) %collective-permute-start.2) | collective-permute-done | bytes 180256 | tf_op jit(solution)/shard_map/ppermute | solution.py:58
  58.8 12.7 %collective-permute-done.8.refs_1_ = bf16[2,4,2,32,1408]{4,3,2,1,0:T(8,128)(2,1)} collective-permute-done((bf16[2,4,2,32,1408]{4,3,2,1,0:T(8,128)(2,1)}, bf16[2,4,2,32,1408]{4,3,2,1,0:T(8,128)(2,1)}, u32[]{:S(2)}, u32[]{:S(2)}) %collective-permute-start.8) | collective-permute-done | bytes 1441824 | tf_op jit(solution)/shard_map/ppermute | solution.py:62
  103.4 25.8 %attention.4 = (bf16[1024,1024]{1,0:T(8,128)(2,1)}, bf16[3,1024,1024]{2,1,0:T(8,128)(2,1)}, bf16[3,1024,512]{2,1,0:T(8,128)(2,1)}, bf16[3,1024,512]{2,1,0:T(8,12...) custom-call(s32[1]{0:T(128)} %bitcast.core_ref, ...), custom_call_target="tpu_custom_call" | custom-call | flops 128849018880 | bytes 83886080 | tf_op jit(solution)/shard_map/attention/pallas_call | solution.py:522
  133.7 25.5 %attention.5 = (bf16[1024,1024]{1,0:T(8,128)(2,1)}, bf16[3,1024,1024]{2,1,0:T(8,128)(2,1)}, bf16[3,1024,512]{2,1,0:T(8,128)(2,1)}, bf16[3,1024,512]{2,1,0:T(8,12...) custom-call(s32[1]{0:T(128)} %bitcast.core_ref, ...), custom_call_target="tpu_custom_call", output_to_operand_aliasing={{0}: (20, {}), {1}: (21, {}), {2}: (22, {}), {3}: (23, {}),... | custom-call | flops 128849018880 | bytes 83886080 | tf_op jit(solution)/shard_map/attention/pallas_call | solution.py:522
  168.8 26.1 %attention.6 = (bf16[1024,1024]{1,0:T(8,128)(2,1)}, bf16[3,1024,1024]{2,1,0:T(8,128)(2,1)}, bf16[3,1024,512]{2,1,0:T(8,128)(2,1)}, bf16[3,1024,512]{2,1,0:T(8,12...) custom-call(s32[1]{0:T(128)} %bitcast.core_ref, ...), custom_call_target="tpu_custom_call", output_to_operand_aliasing={{0}: (20, {}), {1}: (21, {}), {2}: (22, {}), {3}: (23, {}),... | custom-call | flops 128849018880 | bytes 83886080 | tf_op jit(solution)/shard_map/attention/pallas_call | solution.py:522
  201.9 6.8 %collective-permute-done.22.refs_5_ = bf16[2,32,2048]{2,1,0:T(8,128)(2,1)S(1)} collective-permute-done((bf16[2,32,2048]{2,1,0:T(8,128)(2,1)S(1)}, bf16[2,32,2048]{2,1,0:T(8,128)(2,1)S(1)}, u32[]{:S(2)}, u32[]{:S(2)}) %collective-permute-start.22) | collective-permute-done | bytes 262176 | tf_op jit(solution)/shard_map/ppermute | solution.py:58
  208.7 8.9 %collective-permute-done.23.refs_6_ = bf16[2,32,2048]{2,1,0:T(8,128)(2,1)S(1)} collective-permute-done((bf16[2,32,2048]{2,1,0:T(8,128)(2,1)S(1)}, bf16[2,32,2048]{2,1,0:T(8,128)(2,1)S(1)}, u32[]{:S(2)}, u32[]{:S(2)}) %collective-permute-start.23) | collective-permute-done | bytes 262176 | tf_op jit(solution)/shard_map/ppermute | solution.py:58
  218.3 7.2 %place.13 = (bf16[2,4,2,2,1,32,4096]{6,5,4,3,2,1,0:T(8,128)(2,1)}, bf16[4,2,32,2048]{3,2,1,0:T(8,128)(2,1)}) custom-call(bf16[2,4,2,32,2048]{4,3,2,1,0:T(8,128)(2,1)} %get-tuple-element.146.refs_0_, bf16[2,4,2,32,2048]{4,3,2,1,0:T(8,128)(2,1)} %collective-permute-done.19.refs_1_, bf16[2,4,2,32,2048]{4,3,2,1,0:T(8,128)(2,1)} %collective-permute-done.20.refs_2_, ...), custom_call_target="tpu_custom_call" | custom-call | bytes 75497472 | tf_op jit(solution)/shard_map/place/pallas_call | solution.py:90
  227.1 25.5 %attention.7 = (bf16[1024,1024]{1,0:T(8,128)(2,1)}, bf16[3,1024,1024]{2,1,0:T(8,128)(2,1)}, bf16[3,1024,512]{2,1,0:T(8,128)(2,1)}, bf16[3,1024,512]{2,1,0:T(8,12...) custom-call(s32[1]{0:T(128)} %bitcast.core_ref, ...), custom_call_target="tpu_custom_call", output_to_operand_aliasing={{0}: (20, {}), {1}: (21, {}), {2}: (22, {}), {3}: (23, {}),... | custom-call | flops 128849018880 | bytes 83886080 | tf_op jit(solution)/shard_map/attention/pallas_call | solution.py:522
  256.6 15.1 %up.2 = (bf16[1024,4096]{1,0:T(8,128)(2,1)}, bf16[1024,4096]{1,0:T(8,128)(2,1)}, bf16[2,1024,1024]{2,1,0:T(8,128)(2,1)}, bf16[2,1024,1024]{2,1,0:T(8,128)(2,1)}) custom-call(s32[1]{0:T(128)} %bitcast.core_ref, bf16[1024,1024]{1,0:T(8,128)(2,1)} %get-tuple-element.119.hid_ref, bf16[1024,1024]{1,0:T(8,128)(2,1)} %get-tuple-element.227.dy_ref, ...), custom_call_target="tpu_custom_call" | custom-call | flops 34359738368 | bytes 75497472 | tf_op jit(solution)/shard_map/up/pallas_call | solution.py:576
  273.4 7.1 %fold.9 = (bf16[4,2,4,64,512]{4,3,2,1,0:T(8,128)(2,1)}, bf16[4,2,4,64,512]{4,3,2,1,0:T(8,128)(2,1)}) custom-call(s32[2]{0:T(128)} %pad_add_fusion.ref, bf16[3,2,4,2,64,512]{5,4,3,2,1,0:T(8,128)(2,1)} %bitcast.90, bf16[1,2,4,2,64,512]{5,4,3,2,1,0:T(8,128)(2,1)} %bitcast.98, bf16[3,2,4,2,64,512]{5,4,3,2,1,0:T(8,128)(2,1)} %bitcast.92, ...), custom_call_target="tpu_custom_call" | custom-call | flops 50331648 | bytes 50331648 | tf_op jit(solution)/shard_map/fold/pallas_call | solution.py:859
  281.4 15.3 %up.3 = (bf16[1024,4096]{1,0:T(8,128)(2,1)}, bf16[1024,4096]{1,0:T(8,128)(2,1)}, bf16[2,1024,1024]{2,1,0:T(8,128)(2,1)}, bf16[2,1024,1024]{2,1,0:T(8,128)(2,1)}) custom-call(s32[1]{0:T(128)} %bitcast.core_ref, bf16[1024,1024]{1,0:T(8,128)(2,1)} %get-tuple-element.119.hid_ref, ...), custom_call_target="tpu_custom_call", output_to_operand_aliasing={{0}: (5, {}), {1}: (6, {}), {2}: (7, {}), {3}: (8, {})} | custom-call | flops 34359738368 | bytes 75497472 | tf_op jit(solution)/shard_map/up/pallas_call | solution.py:576
  297.4 9.5 %collective-permute-done.31.refs_1_.refs_3_ = bf16[4,2,4,64,512]{4,3,2,1,0:T(8,128)(2,1)} collective-permute-done((bf16[4,2,4,64,512]{4,3,2,1,0:T(8,128)(2,1)}, bf16[4,2,4,64,512]{4,3,2,1,0:T(8,128)(2,1)}, u32[]{:S(2)}, u32[]{:S(2)}) %collective-permute-start.31) | collective-permute-done | bytes 2097184 | tf_op jit(solution)/shard_map/ppermute | solution.py:62
  312.7 6.9 %place.15 = bf16[2,4,2,2,4,32,1024]{6,5,4,3,2,1,0:T(8,128)(2,1)} custom-call(bf16[2,4,2,32,2048]{4,3,2,1,0:T(8,128)(2,1)} %place.14.rest_0_.refs_0_, bf16[2,4,2,32,2048]{4,3,2,1,0:T(8,128)(2,1)} %collective-permute-done.28.refs_1_, bf16[2,4,2,32,2048]{4,3,2,1,0:T(8,128)(2,1)} %collective-permute-done.29.refs_2_, ...), custom_call_target="tpu_custom_call" | custom-call | bytes 67108864 | tf_op jit(solution)/shard_map/place/pallas_call | solution.py:90
  319.7 14.1 %down.2 = (bf16[1024,4096]{1,0:T(8,128)(2,1)}, f32[1,4096]{1,0:T(1,128)}, bf16[2,1024,1024]{2,1,0:T(8,128)(2,1)}) custom-call(s32[1]{0:T(128)} %bitcast.core_ref, bf16[1024,1024]{1,0:T(8,128)(2,1)} %get-tuple-element.122.hid_t_ref, bf16[1024,1024]{1,0:T(8,128)(2,1)} %get-tuple-element.227.dy_ref, bf16[4096,1024]{1,0:T(8,128)(2,1)} %bitcast.94, ...), custom_call_target="tpu_custom_call" | custom-call | flops 34359738368 | bytes 75497472 | tf_op jit(solution)/shard_map/down/pallas_call | solution.py:626
  352.1 13.9 %down.3 = (bf16[1024,4096]{1,0:T(8,128)(2,1)}, f32[1,4096]{1,0:T(1,128)}, bf16[2,1024,1024]{2,1,0:T(8,128)(2,1)}) custom-call(s32[1]{0:T(128)} %bitcast.core_ref, bf16[1024,1024]{1,0:T(8,128)(2,1)} %get-tuple-element.122.hid_t_ref, bf16[1024,1024]{1,0:T(8,128)(2,1)} %get-tuple-element.227.dy_ref, ...), custom_call_target="tpu_custom_call", output_to_operand_aliasing={{0}: (5, {}), {1}: (6, {})} | custom-call | flops 34359738368 | bytes 75497472 | tf_op jit(solution)/shard_map/down/pallas_call | solution.py:626
  366.0 11.8 %collective-permute-done.35.refs_1_.refs_3_ = bf16[2,2,4,64,1024]{4,3,2,1,0:T(8,128)(2,1)S(1)} collective-permute-done((bf16[2,2,4,64,1024]{4,3,2,1,0:T(8,128)(2,1)}, bf16[2,2,4,64,1024]{4,3,2,1,0:T(8,128)(2,1)S(1)}, u32[]{:S(2)}, u32[]{:S(2)}) %collective-permute-start.35) | collective-permute-done | bytes 2097184 | tf_op jit(solution)/shard_map/ppermute | solution.py:62
  383.5 14.9 %back.1.refs_4_.acc_ref = f32[1024,1024]{1,0:T(8,128)} custom-call(bf16[1024,4096]{1,0:T(8,128)(2,1)} %get-tuple-element.182.refs_4_.dup_ref, bf16[1024,4096]{1,0:T(8,128)(2,1)} %bitcast.125, bf16[2,4,64,1024]{3,2,1,0:T(8,128)(2,1)} %get-tuple-element.184.rest_0_.refs_0_.refs_2_.refs_4_.refs_6_), custom_call_target="tpu_custom_call" | custom-call | flops 34359738368 | bytes 83886080 | tf_op jit(solution)/shard_map/back/pallas_call | solution.py:740
  401.7 7.3 %fold.14 = (bf16[2,2,4,64,1024]{4,3,2,1,0:T(8,128)(2,1)}, bf16[2,2,4,64,1024]{4,3,2,1,0:T(8,128)(2,1)}) custom-call(s32[2]{0:T(128)} %pad_add_fusion.ref, bf16[2,2,4,2,64,1024]{5,4,3,2,1,0:T(8,128)(2,1)} %bitcast.88, bf16[2,2,4,2,64,1024]{5,4,3,2,1,0:T(8,128)(2,1)} %bitcast.31.refs_1_.refs_3_, bf16[2,2,4,2,64,1024]{5,4,3,2,1,0:T(8,128)(2,1)} %bitcast.89, ...), custom_call_target="tpu_custom_call" | custom-call | flops 50331648 | bytes 50331648 | tf_op jit(solution)/shard_map/fold/pallas_call | solution.py:859
  430.9 18.9 %input.1 = (f32[1024,1024]{1,0:T(8,128)}, f32[8,1024]{1,0:T(8,128)}) custom-call(bf16[3,1024,1024]{2,1,0:T(8,128)(2,1)} %get-tuple-element.187.dm_ref, bf16[1024,1536]{1,0:T(8,128)(2,1)} %bitcast.132, bf16[1024,1536]{1,0:T(8,128)(2,1)} %bitcast.139, f32[1024,1024]{1,0:T(8,128)} %back.1.refs_4_.acc_ref, bf16[1024,1024]{1,0:T(8,128)(2,1)} %x_ref.5, ...), custom_call_target="tpu_custom_call" | custom-call | flops 25769803776 | bytes 134217728 | tf_op jit(solution)/shard_map/input/pallas_call | solution.py:797
  461.3 10.1 %output_first.1.refs_8_.acc_ref = f32[1024,1024]{1,0:T(8,128)} custom-call(bf16[1024,4096]{1,0:T(8,128)(2,1)} %get-tuple-element.167.refs_4_.rest_0_.act_ref, bf16[4096,1024]{1,0:T(8,128)(2,1)} %bitcast.96, bf16[1024,1024]{1,0:T(8,128)(2,1)} %x_ref.5, f32[1,1024]{1,0:T(1,128)} %add.149.bias_ref, ...), custom_call_target="tpu_custom_call" | custom-call | flops 17179869184 | bytes 58720256 | tf_op jit(solution)/shard_map/output_first/pallas_call | solution.py:664
  479.0 9.7 %collective-permute-done.38.refs_1_.refs_3_.refs_5_.refs_7_ = bf16[2,4,64,1024]{3,2,1,0:T(8,128)(2,1)S(1)} collective-permute-done((bf16[2,4,64,1024]{3,2,1,0:T(8,128)(2,1)S(1)}, bf16[2,4,64,1024]{3,2,1,0:T(8,128)(2,1)S(1)}, u32[]{:S(2)}, u32[]{:S(2)}) %collective-permute-start.38) | collective-permute-done | bytes 1048608 | tf_op jit(solution)/shard_map/ppermute | solution.py:62
  492.3 14.1 %output_rest.1 = f32[1024,1024]{1,0:T(8,128)} custom-call(bf16[1024,4096]{1,0:T(8,128)(2,1)} %get-tuple-element.167.refs_4_.rest_0_.act_ref, bf16[1024,1024]{1,0:T(8,128)(2,1)} %get-tuple-element.157.refs_2_.att_ref, bf16[4096,1024]{1,0:T(8,128)(2,1)} %bitcast.97, bf16[1024,1024]{1,0:T(8,128)(2,1)} %bitcast.144, f32[1024,1024]{1,0:T(8,128)} %output_first.1.refs_8_.acc_ref, ...), custom_call_target="tpu_custom_call" | custom-call | flops 25769803776 | bytes 75497472 | tf_op jit(solution)/shard_map/output_rest/pallas_call | solution.py:705
  523.2 10.0 %collective-permute-done.50 = bf16[2,64,1024]{2,1,0:T(8,128)(2,1)S(1)} collective-permute-done((bf16[2,64,1024]{2,1,0:T(8,128)(2,1)S(1)}, bf16[2,64,1024]{2,1,0:T(8,128)(2,1)S(1)}, u32[]{:S(2)}, u32[]{:S(2)}) %collective-permute-start.50) | collective-permute-done | bytes 262176 | tf_op jit(solution)/shard_map/ppermute | solution.py:58
  (330 shorter events, 212.9 us)
Async XLA Ops:
  58.7 29.8 %collective-permute-start.9 = (bf16[2,4,2,32,1408]{4,3,2,1,0:T(8,128)(2,1)S(1)}, bf16[2,4,2,32,1408]{4,3,2,1,0:T(8,128)(2,1)}, u32[]{:S(2)}, u32[]{:S(2)}) collective-permute-start(bf16[2,4,2,32,1408]{4,3,2,1,0:T(8,128)(2,1)S(1)} %copy-done.10), channel_id=1, source_target_pairs={{0,1},{1,0},{2,3},{3,2},{4,5},{5,4},{6,7},{7,6},{8,9},{9,8},{10,11... | collective-permute-start | bytes 4325384 | tf_op jit(solution)/shard_map/ppermute | solution.py:58
  84.1 45.1 %collective-permute-start.12 = (bf16[2,32,2048]{2,1,0:T(8,128)(2,1)S(1)}, bf16[2,32,2048]{2,1,0:T(8,128)(2,1)S(1)}, u32[]{:S(2)}, u32[]{:S(2)}) collective-permute-start(bf16[2,32,2048]{2,1,0:T(8,128)(2,1)S(1)} %get-tuple-element.121.refs_2_), channel_id=1, source_target_pairs={{0,4},{1,5},{2,6},{3,7},{4,0},{5,1},{6,2},{7,3},{8,12},{9,13},{10,... | collective-permute-start | bytes 786440 | tf_op jit(solution)/shard_map/ppermute | solution.py:58
  85.7 43.5 %collective-permute-start.13 = (bf16[2,32,2048]{2,1,0:T(8,128)(2,1)S(1)}, bf16[2,32,2048]{2,1,0:T(8,128)(2,1)S(1)}, u32[]{:S(2)}, u32[]{:S(2)}) collective-permute-start(bf16[2,32,2048]{2,1,0:T(8,128)(2,1)S(1)} %get-tuple-element.121.refs_2_), channel_id=1, source_target_pairs={{0,8},{1,9},{2,10},{3,11},{4,12},{5,13},{6,14},{7,15},{8,0},{9,1},... | collective-permute-start | bytes 786440 | tf_op jit(solution)/shard_map/ppermute | solution.py:58
  86.8 42.5 %collective-permute-start.14 = (bf16[2,32,2048]{2,1,0:T(8,128)(2,1)S(1)}, bf16[2,32,2048]{2,1,0:T(8,128)(2,1)}, u32[]{:S(2)}, u32[]{:S(2)}) collective-permute-start(bf16[2,32,2048]{2,1,0:T(8,128)(2,1)S(1)} %get-tuple-element.121.refs_2_), channel_id=1, source_target_pairs={{0,12},{1,13},{2,14},{3,15},{4,8},{5,9},{6,10},{7,11},{8,4},{9,5},... | collective-permute-start | bytes 786440 | tf_op jit(solution)/shard_map/ppermute | solution.py:58
  88.5 40.7 %collective-permute-start.11 = (bf16[4,2,32,768]{3,2,1,0:T(8,128)(2,1)S(1)}, bf16[4,2,32,768]{3,2,1,0:T(8,128)(2,1)S(1)}, u32[]{:S(2)}, u32[]{:S(2)}) collective-permute-start(bf16[4,2,32,768]{3,2,1,0:T(8,128)(2,1)S(1)} %copy-done.21), channel_id=1, source_target_pairs={{0,2},{1,17},{2,0},{3,19},{4,6},{5,21},{6,4},{7,23},{8,10},{9,25},... | collective-permute-start | bytes 1179656 | tf_op jit(solution)/shard_map/ppermute | solution.py:62
  132.6 26.6 %collective-permute-start.15 = (bf16[2,4,2,32,768]{4,3,2,1,0:T(8,128)(2,1)}, bf16[2,4,2,32,768]{4,3,2,1,0:T(8,128)(2,1)S(1)}, u32[]{:S(2)}, u32[]{:S(2)}) collective-permute-start(bf16[2,4,2,32,768]{4,3,2,1,0:T(8,128)(2,1)} %get-tuple-element.134.rest_7_.refs_0_), channel_id=1, source_target_pairs={{0,16},{1,3},{2,18},{3,1},{4,20},{5,7},{6,22},{7,5},{8,24},{9,11},... | collective-permute-start | bytes 2359304 | tf_op jit(solution)/shard_map/ppermute | solution.py:62
  133.2 26.7 %collective-permute-start.18 = (bf16[4,2,32,2048]{3,2,1,0:T(8,128)(2,1)}, bf16[4,2,32,2048]{3,2,1,0:T(8,128)(2,1)S(1)}, u32[]{:S(2)}, u32[]{:S(2)}) collective-permute-start(bf16[4,2,32,2048]{3,2,1,0:T(8,128)(2,1)} %get-tuple-element.136.refs_4_), channel_id=1, source_target_pairs={{0,2},{1,17},{2,0},{3,19},{4,6},{5,21},{6,4},{7,23},{8,10},{9,25},... | collective-permute-start | bytes 3145736 | tf_op jit(solution)/shard_map/ppermute | solution.py:62
  167.3 27.7 %collective-permute-start.19 = (bf16[2,4,2,32,2048]{4,3,2,1,0:T(8,128)(2,1)}, bf16[2,4,2,32,2048]{4,3,2,1,0:T(8,128)(2,1)}, u32[]{:S(2)}, u32[]{:S(2)}) collective-permute-start(bf16[2,4,2,32,2048]{4,3,2,1,0:T(8,128)(2,1)} %get-tuple-element.146.refs_0_), channel_id=1, source_target_pairs={{0,16},{1,3},{2,18},{3,1},{4,20},{5,7},{6,22},{7,5},{8,24},{9,11},... | collective-permute-start | bytes 6291464 | tf_op jit(solution)/shard_map/ppermute | solution.py:62
  194.9 22.6 %collective-permute-start.20 = (bf16[2,4,2,32,2048]{4,3,2,1,0:T(8,128)(2,1)S(1)}, bf16[2,4,2,32,2048]{4,3,2,1,0:T(8,128)(2,1)}, u32[]{:S(2)}, u32[]{:S(2)}) collective-permute-start(bf16[2,4,2,32,2048]{4,3,2,1,0:T(8,128)(2,1)S(1)} %copy-done.9), channel_id=1, source_target_pairs={{0,1},{1,0},{2,3},{3,2},{4,5},{5,4},{6,7},{7,6},{8,9},{9,8},{10,11... | collective-permute-start | bytes 6291464 | tf_op jit(solution)/shard_map/ppermute | solution.py:58
  195.0 22.5 %collective-permute-start.21 = (bf16[2,4,2,32,2048]{4,3,2,1,0:T(8,128)(2,1)}, bf16[2,4,2,32,2048]{4,3,2,1,0:T(8,128)(2,1)}, u32[]{:S(2)}, u32[]{:S(2)}) collective-permute-start(bf16[2,4,2,32,2048]{4,3,2,1,0:T(8,128)(2,1)} %collective-permute-done.19.refs_1_), channel_id=1, source_target_pairs={{0,1},{1,0},{2,3},{3,2},{4,5},{5,4},{6,7},{7,6},{8,9},{9,8},{10,11... | collective-permute-start | bytes 6291464 | tf_op jit(solution)/shard_map/ppermute | solution.py:58
  225.5 27.6 %collective-permute-start.25 = (bf16[4,2,32,2048]{3,2,1,0:T(8,128)(2,1)}, bf16[4,2,32,2048]{3,2,1,0:T(8,128)(2,1)}, u32[]{:S(2)}, u32[]{:S(2)}) collective-permute-start(bf16[4,2,32,2048]{3,2,1,0:T(8,128)(2,1)} %get-tuple-element.150.refs_0_), channel_id=1, source_target_pairs={{0,2},{1,17},{2,0},{3,19},{4,6},{5,21},{6,4},{7,23},{8,10},{9,25},... | collective-permute-start | bytes 3145736 | tf_op jit(solution)/shard_map/ppermute | solution.py:62
  256.1 40.6 %collective-permute-start.28 = (bf16[2,4,2,32,2048]{4,3,2,1,0:T(8,128)(2,1)}, bf16[2,4,2,32,2048]{4,3,2,1,0:T(8,128)(2,1)}, u32[]{:S(2)}, u32[]{:S(2)}) collective-permute-start(bf16[2,4,2,32,2048]{4,3,2,1,0:T(8,128)(2,1)} %place.14.rest_0_.refs_0_), channel_id=1, source_target_pairs={{0,16},{1,3},{2,18},{3,1},{4,20},{5,7},{6,22},{7,5},{8,24},{9,11},... | collective-permute-start | bytes 6291464 | tf_op jit(solution)/shard_map/ppermute | solution.py:62
  280.5 26.4 %collective-permute-start.31 = (bf16[4,2,4,64,512]{4,3,2,1,0:T(8,128)(2,1)}, bf16[4,2,4,64,512]{4,3,2,1,0:T(8,128)(2,1)}, u32[]{:S(2)}, u32[]{:S(2)}) collective-permute-start(bf16[4,2,4,64,512]{4,3,2,1,0:T(8,128)(2,1)} %get-tuple-element.170), channel_id=1, source_target_pairs={{0,2},{1,17},{2,0},{3,19},{4,6},{5,21},{6,4},{7,23},{8,10},{9,25},... | collective-permute-start | bytes 6291464 | tf_op jit(solution)/shard_map/ppermute | solution.py:62
  297.3 47.5 %collective-permute-start.32 = (bf16[2,1024,1024]{2,1,0:T(8,128)(2,1)}, bf16[2,1024,1024]{2,1,0:T(8,128)(2,1)}, u32[]{:S(2)}, u32[]{:S(2)}) collective-permute-start(bf16[2,1024,1024]{2,1,0:T(8,128)(2,1)} %get-tuple-element.176), channel_id=1, source_target_pairs={{0,1},{1,0},{2,3},{3,2},{4,5},{5,4},{6,7},{7,6},{8,9},{9,8},{10,11... | collective-permute-start | bytes 12582920 | tf_op jit(solution)/shard_map/ppermute | solution.py:58
  311.2 22.5 %collective-permute-start.33 = (bf16[4,4,64,512]{3,2,1,0:T(8,128)(2,1)}, bf16[4,4,64,512]{3,2,1,0:T(8,128)(2,1)S(1)}, u32[]{:S(2)}, u32[]{:S(2)}) collective-permute-start(bf16[4,4,64,512]{3,2,1,0:T(8,128)(2,1)} %get-tuple-element.177), channel_id=1, source_target_pairs={{0,16},{1,3},{2,18},{3,1},{4,20},{5,7},{6,22},{7,5},{8,24},{9,11},... | collective-permute-start | bytes 3145736 | tf_op jit(solution)/shard_map/ppermute | solution.py:62
  333.7 67.9 %collective-permute-start.34 = (bf16[2,1024,1024]{2,1,0:T(8,128)(2,1)}, bf16[2,1024,1024]{2,1,0:T(8,128)(2,1)}, u32[]{:S(2)}, u32[]{:S(2)}) collective-permute-start(bf16[2,1024,1024]{2,1,0:T(8,128)(2,1)} %get-tuple-element.181), channel_id=1, source_target_pairs={{0,1},{1,0},{2,3},{3,2},{4,5},{5,4},{6,7},{7,6},{8,9},{9,8},{10,11... | collective-permute-start | bytes 12582920 | tf_op jit(solution)/shard_map/ppermute | solution.py:58
  337.4 61.1 %collective-permute-start.45 = (bf16[4,64,512]{2,1,0:T(8,128)(2,1)}, bf16[4,64,512]{2,1,0:T(8,128)(2,1)S(1)}, u32[]{:S(2)}, u32[]{:S(2)}) collective-permute-start(bf16[4,64,512]{2,1,0:T(8,128)(2,1)} %get-tuple-element.199), channel_id=1, source_target_pairs={{0,4},{1,5},{2,6},{3,7},{4,0},{5,1},{6,2},{7,3},{8,12},{9,13},{10,... | collective-permute-start | bytes 786440 | tf_op jit(solution)/shard_map/ppermute | solution.py:58
  342.4 56.1 %collective-permute-start.46 = (bf16[4,64,512]{2,1,0:T(8,128)(2,1)}, bf16[4,64,512]{2,1,0:T(8,128)(2,1)S(1)}, u32[]{:S(2)}, u32[]{:S(2)}) collective-permute-start(bf16[4,64,512]{2,1,0:T(8,128)(2,1)} %get-tuple-element.200), channel_id=1, source_target_pairs={{0,8},{1,9},{2,10},{3,11},{4,12},{5,13},{6,14},{7,15},{8,0},{9,1},... | collective-permute-start | bytes 786440 | tf_op jit(solution)/shard_map/ppermute | solution.py:58
  343.3 55.2 %collective-permute-start.47 = (bf16[4,64,512]{2,1,0:T(8,128)(2,1)}, bf16[4,64,512]{2,1,0:T(8,128)(2,1)S(1)}, u32[]{:S(2)}, u32[]{:S(2)}) collective-permute-start(bf16[4,64,512]{2,1,0:T(8,128)(2,1)} %get-tuple-element.201), channel_id=1, source_target_pairs={{0,12},{1,13},{2,14},{3,15},{4,8},{5,9},{6,10},{7,11},{8,4},{9,5},... | collective-permute-start | bytes 786440 | tf_op jit(solution)/shard_map/ppermute | solution.py:58
  351.6 26.2 %collective-permute-start.35 = (bf16[2,2,4,64,1024]{4,3,2,1,0:T(8,128)(2,1)}, bf16[2,2,4,64,1024]{4,3,2,1,0:T(8,128)(2,1)S(1)}, u32[]{:S(2)}, u32[]{:S(2)}) collective-permute-start(bf16[2,2,4,64,1024]{4,3,2,1,0:T(8,128)(2,1)} %get-tuple-element.183), channel_id=1, source_target_pairs={{0,2},{1,17},{2,0},{3,19},{4,6},{5,21},{6,4},{7,23},{8,10},{9,25},... | collective-permute-start | bytes 6291464 | tf_op jit(solution)/shard_map/ppermute | solution.py:62
  401.2 26.2 %collective-permute-start.37 = (bf16[2,4,64,1024]{3,2,1,0:T(8,128)(2,1)}, bf16[2,4,64,1024]{3,2,1,0:T(8,128)(2,1)S(1)}, u32[]{:S(2)}, u32[]{:S(2)}) collective-permute-start(bf16[2,4,64,1024]{3,2,1,0:T(8,128)(2,1)} %get-tuple-element.188), channel_id=1, source_target_pairs={{0,16},{1,3},{2,18},{3,1},{4,20},{5,7},{6,22},{7,5},{8,24},{9,11},... | collective-permute-start | bytes 3145736 | tf_op jit(solution)/shard_map/ppermute | solution.py:62
  409.0 46.7 %collective-permute-start.36 = (bf16[2,2,4,64,1024]{4,3,2,1,0:T(8,128)(2,1)}, bf16[2,2,4,64,1024]{4,3,2,1,0:T(8,128)(2,1)S(1)}, u32[]{:S(2)}, u32[]{:S(2)}) collective-permute-start(bf16[2,2,4,64,1024]{4,3,2,1,0:T(8,128)(2,1)} %get-tuple-element.186), channel_id=1, source_target_pairs={{0,2},{1,17},{2,0},{3,19},{4,6},{5,21},{6,4},{7,23},{8,10},{9,25},... | collective-permute-start | bytes 6291464 | tf_op jit(solution)/shard_map/ppermute | solution.py:62
  452.3 21.5 %collective-permute-start.54 = (bf16[2,64,1024]{2,1,0:T(8,128)(2,1)}, bf16[2,64,1024]{2,1,0:T(8,128)(2,1)S(1)}, u32[]{:S(2)}, u32[]{:S(2)}) collective-permute-start(bf16[2,64,1024]{2,1,0:T(8,128)(2,1)} %get-tuple-element.214), channel_id=1, source_target_pairs={{0,8},{1,9},{2,10},{3,11},{4,12},{5,13},{6,14},{7,15},{8,0},{9,1},... | collective-permute-start | bytes 786440 | tf_op jit(solution)/shard_map/ppermute | solution.py:58
  511.7 21.5 %collective-permute-start.50 = (bf16[2,64,1024]{2,1,0:T(8,128)(2,1)S(1)}, bf16[2,64,1024]{2,1,0:T(8,128)(2,1)S(1)}, u32[]{:S(2)}, u32[]{:S(2)}) collective-permute-start(bf16[2,64,1024]{2,1,0:T(8,128)(2,1)S(1)} %copy-done.46), channel_id=1, source_target_pairs={{0,8},{1,9},{2,10},{3,11},{4,12},{5,13},{6,14},{7,15},{8,0},{9,1},... | collective-permute-start | bytes 786440 | tf_op jit(solution)/shard_map/ppermute | solution.py:58
  (82 other events, 923.5 us)

commit v4 on v3

--- a/solution.py
+++ b/solution.py
@@ -851,9 +851,9 @@
                 for spans in sources:
                     for arg, at, k in spans:
                         if at <= lo and hi <= at + k:
-                            value = refs[arg][lo - at : hi - at].astype(f32)
+                            value = refs[arg][lo - at : hi - at]
                             total = value if total is None else total + value
-                out[lo:hi] = total.astype(bf16).reshape((hi - lo,) + out_block)
+                out[lo:hi] = total.reshape((hi - lo,) + out_block)
 
     return list(
         pl.pallas_call(
@@ -947,13 +947,18 @@
         )
         self.parts = [parts[0]] + [g.swap(parts[j], "z", j) for j in range(1, g.nz)]
 
-    def result(self, after=()):
+    def settle(self, after=()):
         if after:
             self.parts = lax.optimization_barrier((*self.parts, *after))[: len(self.parts)]
         total = self.parts[0].astype(f32)
         for part in self.parts[1:]:
             total = total + part.astype(f32)
-        total = total.reshape(-1, 2, self.rows, self.cols)
+        self.total = total.reshape(-1, 2, self.rows, self.cols)
+
+    def result(self, after=()):
+        total = self.total
+        if after:
+            total = lax.optimization_barrier((total, *after))[0]
         core = self.d["c"]
         mine = pick(total, 1, core)
         got = self.grid.swap(pick(total, 1, 1 - core), "c", 1)
@@ -973,10 +978,6 @@
         for k in range(1, self.grid.sizes[digit]):
             mine = mine + self.grid.swap(pick(self.now, axis, self.d[digit] ^ k), digit, k)
         self.now = mine
-
-    def last(self):
-        self.step("z", 0)
-        return self.now
 
 
 def tables(node_seeds, node_weights):
@@ -1042,6 +1043,21 @@
     small = jnp.concatenate(vectors)
     per_row = small.shape[0] // rows
     small = jnp.pad(small.reshape(rows, per_row), ((0, 0), (0, 128 - per_row)))
+    dy_low = cotangent.astype(bf16)
+    dy_sums = jnp.sum(dy_low.astype(f32), axis=0)
+    projection, quad = tables(node_seeds, node_weights)
+    doc_ids, positions = layout(doc_lengths[0])
+    cos, sin = rotary(positions)
+    flat = jnp.ones((LEN, HD - ROT), f32)
+    none = jnp.zeros((LEN, ROT // 2), f32)
+    cos_t = feature_scale * jnp.tile(jnp.concatenate([cos, cos, flat], axis=1), (1, PER))
+    left_t = feature_scale * jnp.tile(jnp.concatenate([-sin, none, 0 * flat], axis=1), (1, PER))
+    right_t = feature_scale * jnp.tile(jnp.concatenate([none, sin, 0 * flat], axis=1), (1, PER))
+    eye = jnp.eye(PER, dtype=f32)
+    wide_proj = jnp.einsum("ab,jd->ajbd", eye, projection, precision=precise).reshape(WIDE, WIDE)
+    near = lax.reduce_precision(wide_proj, 8, 7)
+    ones = jnp.kron(eye, jnp.ones((HD, HD), f32)).astype(bf16)
+
     if staged:
         pairs = [
             jnp.concatenate([qkv_weight[:, p * D + h : p * D + h + D // 2] for p in range(3)], axis=1)
@@ -1062,9 +1078,11 @@
         token = place_all([head.first()])
         rest = Gather(grid, *packed[1], token)
         token = place_all([head.second(), rest.first()])
-        head.cores()
+        fill = lax.optimization_barrier((dy_low, dy_sums, cos_t, left_t, right_t, near))
+        dy_low, dy_sums, cos_t, left_t, right_t, near = fill
+        head.cores(fill)
+        token = place_all([head.third()])
         ups = Gather(grid, *packed[2], token)
-        place_all([head.third()])
         pair_weights, attn_weight, small_all = [head.full[0], None], head.full[1], head.full[2]
     else:
         joint_weight, small_all, attn_weight, up_weight, down_weight = [
@@ -1085,22 +1103,7 @@
 
     core = grid.digits()["c"] if staged else jnp.zeros((), jnp.int32)
     core_arg = core.reshape(1).astype(jnp.int32)
-    dy_low = cotangent.astype(bf16)
-    dy_sums = jnp.sum(dy_low.astype(f32), axis=0)
     hidden_low, hidden_t = norm(tokens, norm_gain[None], norm_shift[None])
-
-    projection, quad = tables(node_seeds, node_weights)
-    doc_ids, positions = layout(doc_lengths[0])
-    cos, sin = rotary(positions)
-    flat = jnp.ones((LEN, HD - ROT), f32)
-    none = jnp.zeros((LEN, ROT // 2), f32)
-    cos_t = feature_scale * jnp.tile(jnp.concatenate([cos, cos, flat], axis=1), (1, PER))
-    left_t = feature_scale * jnp.tile(jnp.concatenate([-sin, none, 0 * flat], axis=1), (1, PER))
-    right_t = feature_scale * jnp.tile(jnp.concatenate([none, sin, 0 * flat], axis=1), (1, PER))
-    eye = jnp.eye(PER, dtype=f32)
-    wide_proj = jnp.einsum("ab,jd->ajbd", eye, projection, precision=precise).reshape(WIDE, WIDE)
-    near = lax.reduce_precision(wide_proj, 8, 7)
-    ones = jnp.kron(eye, jnp.ones((HD, HD), f32)).astype(bf16)
 
     operands = (
         hidden_low,
@@ -1121,18 +1124,16 @@
     for group in range(GROUPS):
         after = ()
         if staged and group == 1:
-            token = place_all([rest.second(), ups.first()], carried[:1])
-            after = token
+            after = place_all([rest.second(), ups.first()], carried[:1])
+            downs = Gather(grid, *packed[3], after)
         if staged and group == 2:
-            rest.cores(carried[:1])
-            place_all([rest.third(), ups.second()])
+            token = place_all([ups.second(), downs.first()], carried[:1])
+            rest.cores(token)
+            place_all([rest.third()], token)
             pair_weights[1] = rest.full[0]
-            downs = Gather(grid, *packed[3], (rest.full[0],))
         if staged and group == 3:
+            after = place_all([downs.second()], carried[:1])
             ups.cores(carried[:1])
-            token = place_all([ups.third(), downs.first()], carried[:1])
-            up_weight = ups.full[0]
-            after = token
         carried = attention(
             core_arg, group, operands, pair_weights[group // 2], attn_weight, carried, after
         )
@@ -1140,23 +1141,24 @@
     after = carried[:1]
     if staged:
         joint_sum = Reduction(grid, [keep_qkv, keep_o[None]], [send_qkv, send_o[None]])
-        after = place_all([downs.second()], carried[:1])
+        after = place_all([ups.third()], carried[:1])
+        up_weight = ups.full[0]
+        downs.cores(carried[:1])
     hidden = ()
     for call in range(CALLS):
         if staged and call == 1:
             joint_sum.first(hidden[:1])
-            after = joint_sum.token()
+            after = place_all([downs.third()], joint_sum.token())
+            (down_weight,) = downs.full
         hidden = up_part(
             core_arg, block_rows, wide, call, hidden_low, dy_low, up_weight, up_bias[None], hidden, after
         )
     act, slope, keep_2, send_2 = hidden
     after = hidden[:1]
     if staged:
-        downs.cores(hidden[:1])
+        down_sum = Reduction(grid, [keep_2], [send_2])
         joint_sum.second(hidden[:1])
-        place_all([downs.third()], joint_sum.token())
-        (down_weight,) = downs.full
-        down_sum = Reduction(grid, [keep_2], [send_2])
+        after = joint_sum.token()
     back = ()
     grads_1 = []
     for call in range(CALLS):
@@ -1172,8 +1174,9 @@
     after = ()
     if staged:
         up_sum = Reduction(grid, grads_1[1:], grads_1[:1])
+        joint_sum.settle(back[:1])
         down_sum.second(back[:1])
-        after = down_sum.token()
+        after = down_sum.token() + [joint_sum.total]
     d_hidden = back_part(d_up, up_weight, after)
     bias = (attn_bias + down_bias)[None]
     g_up_bias = up_sums.reshape(FF)
@@ -1181,7 +1184,6 @@
     after = ()
     if staged:
         up_sum.first([d_hidden])
-        total = joint_sum.result([d_hidden])
         down_sum.third(up_sum.token())
         after = down_sum.parts[:1]
     input_grad, norm_sums = input_part(
@@ -1191,27 +1193,31 @@
     packed = jnp.concatenate([g.reshape(n, -1) for g in grads], axis=1)
     after = ()
     if staged:
-        up_sum.second([input_grad])
+        down_sum.settle([input_grad])
+        up_sum.second([input_grad, down_sum.total])
+        token = up_sum.token()
+        total, down_total = joint_sum.result(token), down_sum.result(token)
+        packed, _ = lax.optimization_barrier((packed, token[0]))
         small_sum = SmallReduction(grid, packed)
-        small_sum.step("c", 3)
-        after = up_sum.token()
-    output = output_first(act, down_weight, tokens, bias, after)
-    if staged:
-        down_total = down_sum.result([output])
-        small_sum.step("x", 2, output)
-        up_sum.third([output])
-        after = up_sum.parts[:1]
-    output = output_rest(act, att, down_weight, attn_weight, output, after)
-    if staged:
-        small_sum.step("y", 0, output)
-        s_small = small_sum.last()
-        up_total = up_sum.result([output])
+        small_sum.step("z", 1)
+        small_sum.step("x", 1)
+        small_sum.step("y", 0)
+        small_sum.step("c", 0)
+        s_small = small_sum.now
         both = jnp.stack([h[:3].reshape(3, rows, GROUPS, WIDE // 2) for h in total], axis=3)
         both = both.reshape(3, rows, D)
         s_joint = jnp.concatenate([both[0], both[1], both[2]], axis=1)
         s_attn = jnp.concatenate([h[3] for h in total], axis=1)
+        s_down = jnp.concatenate([h.reshape(-1, D) for h in down_total])
+        s_small, s_joint, s_attn, s_down = lax.optimization_barrier((s_small, s_joint, s_attn, s_down))
+        up_sum.third([s_small[None], s_joint, s_attn, s_down])
+        after = up_sum.parts[:1]
+    output = output_first(act, down_weight, tokens, bias, after)
+    output = output_rest(act, att, down_weight, attn_weight, output)
+    if staged:
+        up_sum.settle([output])
+        up_total = up_sum.result()
         s_up = jnp.concatenate([h[i] for h in up_total for i in range(2)], axis=1)
-        s_down = jnp.concatenate([h.reshape(-1, D) for h in down_total])
     else:
         both = jnp.stack([h.reshape(3, D, GROUPS, WIDE // 2) for h in (keep_qkv, send_qkv)], axis=3)
         both = both.reshape(3, D, D)

time: 547 us -> 490 us (0.90)
  waiting for transfers between devices: 104 us -> 61.4 us
  local copies, waits for them, and re-layouts: 51.5 us -> 44.9 us
    ppermute x43, waiting for transfers between devices: 60 us -> 28.7 us  [swap(): return lax.ppermute(value, AXES, pairs)]
    ppermute x14, waiting for transfers between devices: 43.7 us -> 32.7 us  [swap_by_core(): lax.ppermute(value, AXES, [(i, i ^ flips[i % 2]) for i in range(self.n)])]
    ppermute x43, starting transfers between devices: 49.8 us -> 42.5 us  [swap(): return lax.ppermute(value, AXES, pairs)]
    pallas_call x8 -> x9, Pallas kernels: 33.1 us -> 35.2 us  [place(): pl.pallas_call(body, out_shape=tuple(outs), in_specs=[pl.BlockSpec(memory...]
    unnamed x106 -> x102, local copies, waits for them, and re-layouts: 16.8 us -> 18.7 us
  transfers between devices with their start and end apart: 57 -> 57, of which waited for: 19 -> 14; matrix products, arithmetic and copies ran while one was open for 9% -> 7% of each run, Pallas kernels for 49% -> 59%
where the time goes in v4:
time: 490 us; the launch traced here: 483 us
  Pallas kernels  301 us (61%)
  waiting for transfers between devices  61.4 us (13%)
  starting transfers between devices  58.4 us (12%)
  local copies, waits for them, and re-layouts  44.9 us (9%)
  other arithmetic  15.2 us (3%)
    pallas_call x4, Pallas kernels, attention(): pl.pallas_call(functools.partial(attention_body, len(extra)), grid=(1,),...  103 us
    ppermute x43, starting transfers between devices, swap(): return lax.ppermute(value, AXES, pairs)  42.5 us
    pallas_call x9, Pallas kernels, fold(): pl.pallas_call(body, grid_spec=pltpu.PrefetchScalarGridSpec(num_scalar_pr...  40.7 us
    pallas_call x9, Pallas kernels, place(): pl.pallas_call(body, out_shape=tuple(outs), in_specs=[pl.BlockSpec(memory...  35.2 us
    ppermute x14, waiting for transfers between devices, swap_by_core(): lax.ppermute(value, AXES, [(i, i ^ flips[i % 2]) for i in range(self.n)])  32.7 us
    pallas_call x2, Pallas kernels, up_part(): pl.pallas_call(functools.partial(up_body, rows, wide, len(extra)), grid=(...  30.4 us
    ppermute x43, waiting for transfers between devices, swap(): return lax.ppermute(value, AXES, pairs)  28.7 us
    pallas_call x2, Pallas kernels, down_part(): pl.pallas_call(functools.partial(down_body, len(extra)), grid_spec=pltpu....  28 us
  transfers between devices with their start and end apart: 57, of which 14 were waited for; matrix products, arithmetic and copies ran while one was open for 7% of the time, Pallas kernels for 59%

profile of v4, /device:TPU:0, one launch (start us, length us, event | category | flops | bytes accessed | tf_op | source)
XLA Modules:
  0.0 482.9 jit_solution(10002972239575709989)
XLA Ops:
  11.4 5.0 %collective-permute-start.3 = (bf16[2,32,1408]{2,1,0:T(8,128)(2,1)S(1)}, bf16[2,32,1408]{2,1,0:T(8,128)(2,1)S(1)}, u32[]{:S(2)}, u32[]{:S(2)}) collective-permute-start(bf16[2,32,1408]{2,1,0:T(8,128)(2,1)S(1)} %pad_maximum_fusion.5.refs_0_), channel_id=1, source_target_pairs={{0,12},{1,13},{2,14},{3,15},{4,8},{5,9},{6,10},{7,11},{8,4},{9,5},... | collective-permute-start | bytes 540680 | tf_op jit(solution)/shard_map/ppermute | solution.py:58
  17.1 4.8 collective-permute-done.3.refs_3_
  22.0 10.1 %collective-permute-done.2.refs_2_ = bf16[2,32,1408]{2,1,0:T(8,128)(2,1)S(1)} collective-permute-done((bf16[2,32,1408]{2,1,0:T(8,128)(2,1)S(1)}, bf16[2,32,1408]{2,1,0:T(8,128)(2,1)S(1)}, u32[]{:S(2)}, u32[]{:S(2)}) %collective-permute-start.2) | collective-permute-done | bytes 180256 | tf_op jit(solution)/shard_map/ppermute | solution.py:58
  60.4 11.1 %collective-permute-done.8.refs_1_ = bf16[2,4,2,32,1408]{4,3,2,1,0:T(8,128)(2,1)} collective-permute-done((bf16[2,4,2,32,1408]{4,3,2,1,0:T(8,128)(2,1)}, bf16[2,4,2,32,1408]{4,3,2,1,0:T(8,128)(2,1)}, u32[]{:S(2)}, u32[]{:S(2)}) %collective-permute-start.8) | collective-permute-done | bytes 1441824 | tf_op jit(solution)/shard_map/ppermute | solution.py:62
  95.7 5.3 %norm.1 = (bf16[1024,1024]{1,0:T(8,128)(2,1)}, bf16[1024,1024]{1,0:T(8,128)(2,1)}) custom-call(bf16[1024,1024]{1,0:T(8,128)(2,1)} %x_ref.5, f32[1,1024]{1,0:T(1,128)} %reshape.301.gain_ref, f32[1,1024]{1,0:T(1,128)} %reshape.302.shift_ref), custom_call_target="tpu_custom_call" | custom-call | flops 134217728 | bytes 25165824 | tf_op jit(solution)/shard_map/norm/pallas_call | solution.py:253
  101.0 25.9 %attention.4 = (bf16[1024,1024]{1,0:T(8,128)(2,1)}, bf16[3,1024,1024]{2,1,0:T(8,128)(2,1)}, bf16[3,1024,512]{2,1,0:T(8,128)(2,1)}, bf16[3,1024,512]{2,1,0:T(8,12...) custom-call(s32[1]{0:T(128)} %bitcast.core_ref, ...), custom_call_target="tpu_custom_call" | custom-call | flops 128849018880 | bytes 83886080 | tf_op jit(solution)/shard_map/attention/pallas_call | solution.py:522
  136.9 25.5 %attention.5 = (bf16[1024,1024]{1,0:T(8,128)(2,1)}, bf16[3,1024,1024]{2,1,0:T(8,128)(2,1)}, bf16[3,1024,512]{2,1,0:T(8,128)(2,1)}, bf16[3,1024,512]{2,1,0:T(8,12...) custom-call(s32[1]{0:T(128)} %bitcast.core_ref, ...), custom_call_target="tpu_custom_call", output_to_operand_aliasing={{0}: (20, {}), {1}: (21, {}), {2}: (22, {}), {3}: (23, {}),... | custom-call | flops 128849018880 | bytes 83886080 | tf_op jit(solution)/shard_map/attention/pallas_call | solution.py:522
  176.0 26.1 %attention.6 = (bf16[1024,1024]{1,0:T(8,128)(2,1)}, bf16[3,1024,1024]{2,1,0:T(8,128)(2,1)}, bf16[3,1024,512]{2,1,0:T(8,128)(2,1)}, bf16[3,1024,512]{2,1,0:T(8,12...) custom-call(s32[1]{0:T(128)} %bitcast.core_ref, ...), custom_call_target="tpu_custom_call", output_to_operand_aliasing={{0}: (20, {}), {1}: (21, {}), {2}: (22, {}), {3}: (23, {}),... | custom-call | flops 128849018880 | bytes 83886080 | tf_op jit(solution)/shard_map/attention/pallas_call | solution.py:522
  207.3 25.5 %attention.7 = (bf16[1024,1024]{1,0:T(8,128)(2,1)}, bf16[3,1024,1024]{2,1,0:T(8,128)(2,1)}, bf16[3,1024,512]{2,1,0:T(8,128)(2,1)}, bf16[3,1024,512]{2,1,0:T(8,12...) custom-call(s32[1]{0:T(128)} %bitcast.core_ref, ...), custom_call_target="tpu_custom_call", output_to_operand_aliasing={{0}: (20, {}), {1}: (21, {}), {2}: (22, {}), {3}: (23, {}),... | custom-call | flops 128849018880 | bytes 83886080 | tf_op jit(solution)/shard_map/attention/pallas_call | solution.py:522
  233.9 6.8 %place.16.rest_0_ = bf16[2,4,2,2,1,32,4096]{6,5,4,3,2,1,0:T(8,128)(2,1)} custom-call(bf16[2,4,2,32,2048]{4,3,2,1,0:T(8,128)(2,1)} %get-tuple-element.165.refs_4_.refs_0_, bf16[2,4,2,32,2048]{4,3,2,1,0:T(8,128)(2,1)} %collective-permute-done.19.refs_1_, bf16[2,4,2,32,2048]{4,3,2,1,0:T(8,128)(2,1)} %collective-permute-done.23.refs_2_, ...), custom_call_target="tpu_custom_call" | custom-call | bytes 67108864 | tf_op jit(solution)/shard_map/place/pallas_call | solution.py:90
  240.7 15.2 %up.2 = (bf16[1024,4096]{1,0:T(8,128)(2,1)}, bf16[1024,4096]{1,0:T(8,128)(2,1)}, bf16[2,1024,1024]{2,1,0:T(8,128)(2,1)}, bf16[2,1024,1024]{2,1,0:T(8,128)(2,1)}) custom-call(s32[1]{0:T(128)} %bitcast.core_ref, bf16[1024,1024]{1,0:T(8,128)(2,1)} %get-tuple-element.138.hid_ref, bf16[1024,1024]{1,0:T(8,128)(2,1)} %get-tuple-element.129.dy_ref, ...), custom_call_target="tpu_custom_call" | custom-call | flops 34359738368 | bytes 75497472 | tf_op jit(solution)/shard_map/up/pallas_call | solution.py:576
  257.5 6.9 %fold.9 = (bf16[4,2,4,64,512]{4,3,2,1,0:T(8,128)(2,1)}, bf16[4,2,4,64,512]{4,3,2,1,0:T(8,128)(2,1)}) custom-call(s32[2]{0:T(128)} %pad_add_fusion.ref, bf16[3,2,4,2,64,512]{5,4,3,2,1,0:T(8,128)(2,1)} %bitcast.98, bf16[1,2,4,2,64,512]{5,4,3,2,1,0:T(8,128)(2,1)} %bitcast.112, bf16[3,2,4,2,64,512]{5,4,3,2,1,0:T(8,128)(2,1)} %bitcast.100, ...), custom_call_target="tpu_custom_call" | custom-call | flops 50331648 | bytes 50331648 | tf_op jit(solution)/shard_map/fold/pallas_call | solution.py:859
  265.7 6.9 %place.17.rest_4_ = bf16[2,4,2,2,4,32,1024]{6,5,4,3,2,1,0:T(8,128)(2,1)} custom-call(bf16[2,4,2,32,2048]{4,3,2,1,0:T(8,128)(2,1)} %place.15.rest_7_.refs_0_, bf16[2,4,2,32,2048]{4,3,2,1,0:T(8,128)(2,1)} %collective-permute-done.26.refs_1_, bf16[2,4,2,32,2048]{4,3,2,1,0:T(8,128)(2,1)} %collective-permute-done.27.refs_2_, ...), custom_call_target="tpu_custom_call" | custom-call | bytes 67108864 | tf_op jit(solution)/shard_map/place/pallas_call | solution.py:90
  272.7 15.2 %up.3 = (bf16[1024,4096]{1,0:T(8,128)(2,1)}, bf16[1024,4096]{1,0:T(8,128)(2,1)}, bf16[2,1024,1024]{2,1,0:T(8,128)(2,1)}, bf16[2,1024,1024]{2,1,0:T(8,128)(2,1)}) custom-call(s32[1]{0:T(128)} %bitcast.core_ref, bf16[1024,1024]{1,0:T(8,128)(2,1)} %get-tuple-element.138.hid_ref, ...), custom_call_target="tpu_custom_call", output_to_operand_aliasing={{0}: (5, {}), {1}: (6, {}), {2}: (7, {}), {3}: (8, {})} | custom-call | flops 34359738368 | bytes 75497472 | tf_op jit(solution)/shard_map/up/pallas_call | solution.py:576
  297.7 14.0 %down.2 = (bf16[1024,4096]{1,0:T(8,128)(2,1)}, f32[1,4096]{1,0:T(1,128)}, bf16[2,1024,1024]{2,1,0:T(8,128)(2,1)}) custom-call(s32[1]{0:T(128)} %bitcast.core_ref, bf16[1024,1024]{1,0:T(8,128)(2,1)} %get-tuple-element.142.hid_t_ref, bf16[1024,1024]{1,0:T(8,128)(2,1)} %get-tuple-element.129.dy_ref, bf16[4096,1024]{1,0:T(8,128)(2,1)} %bitcast.102, ...), custom_call_target="tpu_custom_call" | custom-call | flops 34359738368 | bytes 75497472 | tf_op jit(solution)/shard_map/down/pallas_call | solution.py:626
  319.7 6.5 %fold.12 = (bf16[2,2,4,64,1024]{4,3,2,1,0:T(8,128)(2,1)}, bf16[2,2,4,64,1024]{4,3,2,1,0:T(8,128)(2,1)}) custom-call(s32[2]{0:T(128)} %pad_add_fusion.ref, bf16[2,2,4,2,64,1024]{5,4,3,2,1,0:T(8,128)(2,1)} %bitcast.94, bf16[2,2,4,2,64,1024]{5,4,3,2,1,0:T(8,128)(2,1)} %bitcast.29.refs_1_.refs_3_, bf16[2,2,4,2,64,1024]{5,4,3,2,1,0:T(8,128)(2,1)} %bitcast.95, ...), custom_call_target="tpu_custom_call" | custom-call | flops 50331648 | bytes 50331648 | tf_op jit(solution)/shard_map/fold/pallas_call | solution.py:859
  327.3 13.9 %down.3 = (bf16[1024,4096]{1,0:T(8,128)(2,1)}, f32[1,4096]{1,0:T(1,128)}, bf16[2,1024,1024]{2,1,0:T(8,128)(2,1)}) custom-call(s32[1]{0:T(128)} %bitcast.core_ref, bf16[1024,1024]{1,0:T(8,128)(2,1)} %get-tuple-element.142.hid_t_ref, bf16[1024,1024]{1,0:T(8,128)(2,1)} %get-tuple-element.129.dy_ref, ...), custom_call_target="tpu_custom_call", output_to_operand_aliasing={{0}: (5, {}), {1}: (6, {})} | custom-call | flops 34359738368 | bytes 75497472 | tf_op jit(solution)/shard_map/down/pallas_call | solution.py:626
  342.2 10.3 %collective-permute-done.35.refs_1_.refs_3_ = bf16[2,2,4,64,1024]{4,3,2,1,0:T(8,128)(2,1)S(1)} collective-permute-done((bf16[2,2,4,64,1024]{4,3,2,1,0:T(8,128)(2,1)}, bf16[2,2,4,64,1024]{4,3,2,1,0:T(8,128)(2,1)S(1)}, u32[]{:S(2)}, u32[]{:S(2)}) %collective-permute-start.35) | collective-permute-done | bytes 2097184 | tf_op jit(solution)/shard_map/ppermute | solution.py:62
  359.1 14.9 %back.1.refs_4_.acc_ref = f32[1024,1024]{1,0:T(8,128)} custom-call(bf16[1024,4096]{1,0:T(8,128)(2,1)} %get-tuple-element.199.refs_4_.dup_ref, bf16[1024,4096]{1,0:T(8,128)(2,1)} %bitcast.108, bf16[2,4,64,1024]{3,2,1,0:T(8,128)(2,1)} %get-tuple-element.201.rest_0_.refs_0_.refs_2_.refs_4_.refs_6_, f32[4,2,32,512]{3,2,1,0:T(8,128)} %bitcast.124), custom_call_target="tpu_custom_call" | custom-call | flops 34359738368 | bytes 83886080 | tf_op jit(solution)/shard_map/back/pallas_call | solution.py:740
  374.0 6.5 %fold.14 = (bf16[2,2,4,64,1024]{4,3,2,1,0:T(8,128)(2,1)}, bf16[2,2,4,64,1024]{4,3,2,1,0:T(8,128)(2,1)}) custom-call(s32[2]{0:T(128)} %pad_add_fusion.ref, bf16[2,2,4,2,64,1024]{5,4,3,2,1,0:T(8,128)(2,1)} %bitcast.96, bf16[2,2,4,2,64,1024]{5,4,3,2,1,0:T(8,128)(2,1)} %bitcast.31.refs_1_.refs_3_, bf16[2,2,4,2,64,1024]{5,4,3,2,1,0:T(8,128)(2,1)} %bitcast.97, ...), custom_call_target="tpu_custom_call" | custom-call | flops 50331648 | bytes 50331648 | tf_op jit(solution)/shard_map/fold/pallas_call | solution.py:859
  389.6 19.3 %input.1 = (f32[1024,1024]{1,0:T(8,128)}, f32[8,1024]{1,0:T(8,128)}) custom-call(bf16[3,1024,1024]{2,1,0:T(8,128)(2,1)} %get-tuple-element.211.dm_ref, bf16[1024,1536]{1,0:T(8,128)(2,1)} %bitcast.147, bf16[1024,1536]{1,0:T(8,128)(2,1)} %bitcast.123, f32[1024,1024]{1,0:T(8,128)} %back.1.refs_4_.acc_ref, bf16[1024,1024]{1,0:T(8,128)(2,1)} %x_ref.5, ...), custom_call_target="tpu_custom_call" | custom-call | flops 25769803776 | bytes 134217728 | tf_op jit(solution)/shard_map/input/pallas_call | solution.py:797
  437.4 9.9 %collective-permute-done.44.refs_1_.refs_3_.refs_5_.refs_7_ = bf16[2,4,64,1024]{3,2,1,0:T(8,128)(2,1)S(1)} collective-permute-done((bf16[2,4,64,1024]{3,2,1,0:T(8,128)(2,1)}, bf16[2,4,64,1024]{3,2,1,0:T(8,128)(2,1)S(1)}, u32[]{:S(2)}, u32[]{:S(2)}) %collective-permute-start.44) | collective-permute-done | bytes 1048608 | tf_op jit(solution)/shard_map/ppermute | solution.py:62
  455.2 10.0 %output_first.1.acc_ref = f32[1024,1024]{1,0:T(8,128)} custom-call(bf16[1024,4096]{1,0:T(8,128)(2,1)} %get-tuple-element.186.refs_4_.act_ref, bf16[4096,1024]{1,0:T(8,128)(2,1)} %bitcast.104, bf16[1024,1024]{1,0:T(8,128)(2,1)} %x_ref.5, f32[1,1024]{1,0:T(1,128)} %add.149.bias_ref, bf16[2,64,1024]{2,1,0:T(8,128)(2,1)} %get-tuple-element.238.rest_0_), custom_call_target="tpu_custom_call" | custom-call | flops 17179869184 | bytes 58720256 | tf_op jit(solution)/shard_map/output_first/pallas_call | solution.py:664
  465.3 14.0 %output_rest.1 = f32[1024,1024]{1,0:T(8,128)} custom-call(bf16[1024,4096]{1,0:T(8,128)(2,1)} %get-tuple-element.186.refs_4_.act_ref, bf16[1024,1024]{1,0:T(8,128)(2,1)} %get-tuple-element.174.refs_4_.att_ref, bf16[4096,1024]{1,0:T(8,128)(2,1)} %bitcast.105, bf16[1024,1024]{1,0:T(8,128)(2,1)} %bitcast.152, f32[1024,1024]{1,0:T(8,128)} %output_first.1.acc_ref), custom_call_target="tpu_custom_call" | custom-call | flops 25769803776 | bytes 75497472 | tf_op jit(solution)/shard_map/output_rest/pallas_call | solution.py:705
  (330 shorter events, 171.5 us)
Async XLA Ops:
  82.0 44.9 %collective-permute-start.11 = (bf16[4,2,32,768]{3,2,1,0:T(8,128)(2,1)S(1)}, bf16[4,2,32,768]{3,2,1,0:T(8,128)(2,1)S(1)}, u32[]{:S(2)}, u32[]{:S(2)}) collective-permute-start(bf16[4,2,32,768]{3,2,1,0:T(8,128)(2,1)S(1)} %copy-done.20), channel_id=1, source_target_pairs={{0,2},{1,17},{2,0},{3,19},{4,6},{5,21},{6,4},{7,23},{8,10},{9,25},... | collective-permute-start | bytes 1179656 | tf_op jit(solution)/shard_map/ppermute | solution.py:62
  89.3 37.6 %collective-permute-start.14 = (bf16[2,32,2048]{2,1,0:T(8,128)(2,1)S(1)}, bf16[2,32,2048]{2,1,0:T(8,128)(2,1)S(1)}, u32[]{:S(2)}, u32[]{:S(2)}) collective-permute-start(bf16[2,32,2048]{2,1,0:T(8,128)(2,1)S(1)} %get-tuple-element.141.refs_2_), channel_id=1, source_target_pairs={{0,12},{1,13},{2,14},{3,15},{4,8},{5,9},{6,10},{7,11},{8,4},{9,5},... | collective-permute-start | bytes 786440 | tf_op jit(solution)/shard_map/ppermute | solution.py:58
  91.8 35.1 %collective-permute-start.13 = (bf16[2,32,2048]{2,1,0:T(8,128)(2,1)S(1)}, bf16[2,32,2048]{2,1,0:T(8,128)(2,1)S(1)}, u32[]{:S(2)}, u32[]{:S(2)}) collective-permute-start(bf16[2,32,2048]{2,1,0:T(8,128)(2,1)S(1)} %get-tuple-element.141.refs_2_), channel_id=1, source_target_pairs={{0,8},{1,9},{2,10},{3,11},{4,12},{5,13},{6,14},{7,15},{8,0},{9,1},... | collective-permute-start | bytes 786440 | tf_op jit(solution)/shard_map/ppermute | solution.py:58
  91.8 35.1 %collective-permute-start.12 = (bf16[2,32,2048]{2,1,0:T(8,128)(2,1)S(1)}, bf16[2,32,2048]{2,1,0:T(8,128)(2,1)S(1)}, u32[]{:S(2)}, u32[]{:S(2)}) collective-permute-start(bf16[2,32,2048]{2,1,0:T(8,128)(2,1)S(1)} %get-tuple-element.141.refs_2_), channel_id=1, source_target_pairs={{0,4},{1,5},{2,6},{3,7},{4,0},{5,1},{6,2},{7,3},{8,12},{9,13},{10,... | collective-permute-start | bytes 786440 | tf_op jit(solution)/shard_map/ppermute | solution.py:58
  130.4 32.0 %collective-permute-start.18 = (bf16[2,32,2048]{2,1,0:T(8,128)(2,1)S(1)}, bf16[2,32,2048]{2,1,0:T(8,128)(2,1)S(1)}, u32[]{:S(2)}, u32[]{:S(2)}) collective-permute-start(bf16[2,32,2048]{2,1,0:T(8,128)(2,1)S(1)} %get-tuple-element.147.refs_2_), channel_id=1, source_target_pairs={{0,12},{1,13},{2,14},{3,15},{4,8},{5,9},{6,10},{7,11},{8,4},{9,5},... | collective-permute-start | bytes 786440 | tf_op jit(solution)/shard_map/ppermute | solution.py:58
  132.9 29.5 %collective-permute-start.17 = (bf16[2,32,2048]{2,1,0:T(8,128)(2,1)S(1)}, bf16[2,32,2048]{2,1,0:T(8,128)(2,1)S(1)}, u32[]{:S(2)}, u32[]{:S(2)}) collective-permute-start(bf16[2,32,2048]{2,1,0:T(8,128)(2,1)S(1)} %get-tuple-element.147.refs_2_), channel_id=1, source_target_pairs={{0,8},{1,9},{2,10},{3,11},{4,12},{5,13},{6,14},{7,15},{8,0},{9,1},... | collective-permute-start | bytes 786440 | tf_op jit(solution)/shard_map/ppermute | solution.py:58
  132.9 29.5 %collective-permute-start.16 = (bf16[2,32,2048]{2,1,0:T(8,128)(2,1)S(1)}, bf16[2,32,2048]{2,1,0:T(8,128)(2,1)S(1)}, u32[]{:S(2)}, u32[]{:S(2)}) collective-permute-start(bf16[2,32,2048]{2,1,0:T(8,128)(2,1)S(1)} %get-tuple-element.147.refs_2_), channel_id=1, source_target_pairs={{0,4},{1,5},{2,6},{3,7},{4,0},{5,1},{6,2},{7,3},{8,12},{9,13},{10,... | collective-permute-start | bytes 786440 | tf_op jit(solution)/shard_map/ppermute | solution.py:58
  134.9 32.1 %collective-permute-start.20 = (bf16[2,4,2,32,768]{4,3,2,1,0:T(8,128)(2,1)}, bf16[2,4,2,32,768]{4,3,2,1,0:T(8,128)(2,1)S(1)}, u32[]{:S(2)}, u32[]{:S(2)}) collective-permute-start(bf16[2,4,2,32,768]{4,3,2,1,0:T(8,128)(2,1)} %get-tuple-element.156.rest_7_.refs_0_), channel_id=1, source_target_pairs={{0,16},{1,3},{2,18},{3,1},{4,20},{5,7},{6,22},{7,5},{8,24},{9,11},... | collective-permute-start | bytes 2359304 | tf_op jit(solution)/shard_map/ppermute | solution.py:62
  135.7 26.8 %collective-permute-start.15 = (bf16[4,2,32,2048]{3,2,1,0:T(8,128)(2,1)}, bf16[4,2,32,2048]{3,2,1,0:T(8,128)(2,1)S(1)}, u32[]{:S(2)}, u32[]{:S(2)}) collective-permute-start(bf16[4,2,32,2048]{3,2,1,0:T(8,128)(2,1)} %get-tuple-element.145.refs_0_), channel_id=1, source_target_pairs={{0,2},{1,17},{2,0},{3,19},{4,6},{5,21},{6,4},{7,23},{8,10},{9,25},... | collective-permute-start | bytes 3145736 | tf_op jit(solution)/shard_map/ppermute | solution.py:62
  169.6 37.3 %collective-permute-start.19 = (bf16[2,4,2,32,2048]{4,3,2,1,0:T(8,128)(2,1)}, bf16[2,4,2,32,2048]{4,3,2,1,0:T(8,128)(2,1)}, u32[]{:S(2)}, u32[]{:S(2)}) collective-permute-start(bf16[2,4,2,32,2048]{4,3,2,1,0:T(8,128)(2,1)} %get-tuple-element.165.refs_4_.refs_0_), channel_id=1, source_target_pairs={{0,16},{1,3},{2,18},{3,1},{4,20},{5,7},{6,22},{7,5},{8,24},{9,11},... | collective-permute-start | bytes 6291464 | tf_op jit(solution)/shard_map/ppermute | solution.py:62
  170.3 31.8 %collective-permute-start.25 = (bf16[4,2,32,2048]{3,2,1,0:T(8,128)(2,1)}, bf16[4,2,32,2048]{3,2,1,0:T(8,128)(2,1)S(1)}, u32[]{:S(2)}, u32[]{:S(2)}) collective-permute-start(bf16[4,2,32,2048]{3,2,1,0:T(8,128)(2,1)} %get-tuple-element.173.refs_0_), channel_id=1, source_target_pairs={{0,2},{1,17},{2,0},{3,19},{4,6},{5,21},{6,4},{7,23},{8,10},{9,25},... | collective-permute-start | bytes 3145736 | tf_op jit(solution)/shard_map/ppermute | solution.py:62
  205.9 27.4 %collective-permute-start.26 = (bf16[2,4,2,32,2048]{4,3,2,1,0:T(8,128)(2,1)}, bf16[2,4,2,32,2048]{4,3,2,1,0:T(8,128)(2,1)}, u32[]{:S(2)}, u32[]{:S(2)}) collective-permute-start(bf16[2,4,2,32,2048]{4,3,2,1,0:T(8,128)(2,1)} %place.15.rest_7_.refs_0_), channel_id=1, source_target_pairs={{0,16},{1,3},{2,18},{3,1},{4,20},{5,7},{6,22},{7,5},{8,24},{9,11},... | collective-permute-start | bytes 6291464 | tf_op jit(solution)/shard_map/ppermute | solution.py:62
  206.8 26.6 %collective-permute-start.23 = (bf16[2,4,2,32,2048]{4,3,2,1,0:T(8,128)(2,1)}, bf16[2,4,2,32,2048]{4,3,2,1,0:T(8,128)(2,1)}, u32[]{:S(2)}, u32[]{:S(2)}) collective-permute-start(bf16[2,4,2,32,2048]{4,3,2,1,0:T(8,128)(2,1)} %get-tuple-element.165.refs_4_.refs_0_), channel_id=1, source_target_pairs={{0,1},{1,0},{2,3},{3,2},{4,5},{5,4},{6,7},{7,6},{8,9},{9,8},{10,11... | collective-permute-start | bytes 6291464 | tf_op jit(solution)/shard_map/ppermute | solution.py:58
  206.8 27.1 %collective-permute-start.24 = (bf16[2,4,2,32,2048]{4,3,2,1,0:T(8,128)(2,1)}, bf16[2,4,2,32,2048]{4,3,2,1,0:T(8,128)(2,1)}, u32[]{:S(2)}, u32[]{:S(2)}) collective-permute-start(bf16[2,4,2,32,2048]{4,3,2,1,0:T(8,128)(2,1)} %collective-permute-done.19.refs_1_), channel_id=1, source_target_pairs={{0,1},{1,0},{2,3},{3,2},{4,5},{5,4},{6,7},{7,6},{8,9},{9,8},{10,11... | collective-permute-start | bytes 6291464 | tf_op jit(solution)/shard_map/ppermute | solution.py:58
  233.4 32.3 %collective-permute-start.27 = (bf16[2,4,2,32,2048]{4,3,2,1,0:T(8,128)(2,1)}, bf16[2,4,2,32,2048]{4,3,2,1,0:T(8,128)(2,1)}, u32[]{:S(2)}, u32[]{:S(2)}) collective-permute-start(bf16[2,4,2,32,2048]{4,3,2,1,0:T(8,128)(2,1)} %place.15.rest_7_.refs_0_), channel_id=1, source_target_pairs={{0,1},{1,0},{2,3},{3,2},{4,5},{5,4},{6,7},{7,6},{8,9},{9,8},{10,11... | collective-permute-start | bytes 6291464 | tf_op jit(solution)/shard_map/ppermute | solution.py:58
  233.4 32.3 %collective-permute-start.28 = (bf16[2,4,2,32,2048]{4,3,2,1,0:T(8,128)(2,1)}, bf16[2,4,2,32,2048]{4,3,2,1,0:T(8,128)(2,1)}, u32[]{:S(2)}, u32[]{:S(2)}) collective-permute-start(bf16[2,4,2,32,2048]{4,3,2,1,0:T(8,128)(2,1)} %collective-permute-done.26.refs_1_), channel_id=1, source_target_pairs={{0,1},{1,0},{2,3},{3,2},{4,5},{5,4},{6,7},{7,6},{8,9},{9,8},{10,11... | collective-permute-start | bytes 6291464 | tf_op jit(solution)/shard_map/ppermute | solution.py:58
  264.4 26.2 %collective-permute-start.31 = (bf16[4,2,4,64,512]{4,3,2,1,0:T(8,128)(2,1)}, bf16[4,2,4,64,512]{4,3,2,1,0:T(8,128)(2,1)S(1)}, u32[]{:S(2)}, u32[]{:S(2)}) collective-permute-start(bf16[4,2,4,64,512]{4,3,2,1,0:T(8,128)(2,1)} %get-tuple-element.188), channel_id=1, source_target_pairs={{0,2},{1,17},{2,0},{3,19},{4,6},{5,21},{6,4},{7,23},{8,10},{9,25},... | collective-permute-start | bytes 6291464 | tf_op jit(solution)/shard_map/ppermute | solution.py:62
  287.8 31.9 %collective-permute-start.32 = (bf16[2,1024,1024]{2,1,0:T(8,128)(2,1)}, bf16[2,1024,1024]{2,1,0:T(8,128)(2,1)}, u32[]{:S(2)}, u32[]{:S(2)}) collective-permute-start(bf16[2,1024,1024]{2,1,0:T(8,128)(2,1)} %get-tuple-element.193), channel_id=1, source_target_pairs={{0,1},{1,0},{2,3},{3,2},{4,5},{5,4},{6,7},{7,6},{8,9},{9,8},{10,11... | collective-permute-start | bytes 12582920 | tf_op jit(solution)/shard_map/ppermute | solution.py:58
  311.7 62.3 %collective-permute-start.34 = (bf16[2,1024,1024]{2,1,0:T(8,128)(2,1)}, bf16[2,1024,1024]{2,1,0:T(8,128)(2,1)}, u32[]{:S(2)}, u32[]{:S(2)}) collective-permute-start(bf16[2,1024,1024]{2,1,0:T(8,128)(2,1)} %get-tuple-element.198), channel_id=1, source_target_pairs={{0,1},{1,0},{2,3},{3,2},{4,5},{5,4},{6,7},{7,6},{8,9},{9,8},{10,11... | collective-permute-start | bytes 12582920 | tf_op jit(solution)/shard_map/ppermute | solution.py:58
  315.3 26.0 %collective-permute-start.36 = (bf16[4,64,512]{2,1,0:T(8,128)(2,1)}, bf16[4,64,512]{2,1,0:T(8,128)(2,1)S(1)}, u32[]{:S(2)}, u32[]{:S(2)}) collective-permute-start(bf16[4,64,512]{2,1,0:T(8,128)(2,1)} %get-tuple-element.202), channel_id=1, source_target_pairs={{0,4},{1,5},{2,6},{3,7},{4,0},{5,1},{6,2},{7,3},{8,12},{9,13},{10,... | collective-permute-start | bytes 786440 | tf_op jit(solution)/shard_map/ppermute | solution.py:58
  326.2 26.2 %collective-permute-start.35 = (bf16[2,2,4,64,1024]{4,3,2,1,0:T(8,128)(2,1)}, bf16[2,2,4,64,1024]{4,3,2,1,0:T(8,128)(2,1)S(1)}, u32[]{:S(2)}, u32[]{:S(2)}) collective-permute-start(bf16[2,2,4,64,1024]{4,3,2,1,0:T(8,128)(2,1)} %get-tuple-element.200), channel_id=1, source_target_pairs={{0,2},{1,17},{2,0},{3,19},{4,6},{5,21},{6,4},{7,23},{8,10},{9,25},... | collective-permute-start | bytes 6291464 | tf_op jit(solution)/shard_map/ppermute | solution.py:62
  380.5 30.5 %collective-permute-start.39 = (bf16[2,2,4,64,1024]{4,3,2,1,0:T(8,128)(2,1)}, bf16[2,2,4,64,1024]{4,3,2,1,0:T(8,128)(2,1)S(1)}, u32[]{:S(2)}, u32[]{:S(2)}) collective-permute-start(bf16[2,2,4,64,1024]{4,3,2,1,0:T(8,128)(2,1)} %get-tuple-element.210), channel_id=1, source_target_pairs={{0,2},{1,17},{2,0},{3,19},{4,6},{5,21},{6,4},{7,23},{8,10},{9,25},... | collective-permute-start | bytes 6291464 | tf_op jit(solution)/shard_map/ppermute | solution.py:62
  450.8 28.5 %collective-permute-start.53 = (bf16[2,64,1024]{2,1,0:T(8,128)(2,1)}, bf16[2,64,1024]{2,1,0:T(8,128)(2,1)S(1)}, u32[]{:S(2)}, u32[]{:S(2)}) collective-permute-start(bf16[2,64,1024]{2,1,0:T(8,128)(2,1)} %get-tuple-element.235), channel_id=1, source_target_pairs={{0,4},{1,5},{2,6},{3,7},{4,0},{5,1},{6,2},{7,3},{8,12},{9,13},{10,... | collective-permute-start | bytes 786440 | tf_op jit(solution)/shard_map/ppermute | solution.py:58
  451.9 27.3 %collective-permute-start.54 = (bf16[2,64,1024]{2,1,0:T(8,128)(2,1)}, bf16[2,64,1024]{2,1,0:T(8,128)(2,1)S(1)}, u32[]{:S(2)}, u32[]{:S(2)}) collective-permute-start(bf16[2,64,1024]{2,1,0:T(8,128)(2,1)} %get-tuple-element.236), channel_id=1, source_target_pairs={{0,8},{1,9},{2,10},{3,11},{4,12},{5,13},{6,14},{7,15},{8,0},{9,1},... | collective-permute-start | bytes 786440 | tf_op jit(solution)/shard_map/ppermute | solution.py:58
  (81 other events, 892.2 us)
